TPU v7x, 32 devices: a whole 2x2x4 slice. The times are simulated.
32 devices in a mesh: fsdp: 16 (over z, y, x), tensor: 2 (over core).
Axes of the slice: x: 2, y: 2, z: 4, core: 2. Of those that a mesh axis runs over, the one named last changes fastest.
Arguments:
- tokens: bfloat16 [64, 577, 1024], P(('fsdp', 'tensor')), may hold values from -6 to 6
- cotangent: bfloat16 [64, 577, 1024], P(('fsdp', 'tensor')), may hold values from -6 to 6
- adapter_index: int32 [64], P('fsdp'), may hold values from 0 to 7
- filled: int32 [64], P('fsdp'), may hold values 0 or 1
- ln1_gain: bfloat16 [1024], replicated, may hold values from 0.5 to 1.5
- ln1_shift: bfloat16 [1024], replicated, may hold values from -2 to 2
- qkv_weight: bfloat16 [1024, 3, 1024], P('fsdp', None, 'tensor'), may hold values from -0.1875 to 0.1875
- qv_bias: bfloat16 [2, 1024], replicated, may hold values from -3 to 3
- out_weight: bfloat16 [1024, 1024], P('tensor', 'fsdp'), may hold values from -0.75 to 0.75
- out_bias: bfloat16 [1024], replicated, may hold values from -3 to 3
- ln2_gain: bfloat16 [1024], replicated, may hold values from 0.5 to 1.5
- ln2_shift: bfloat16 [1024], replicated, may hold values from -2 to 2
- fc1_weight: bfloat16 [1024, 4096], P('fsdp', 'tensor'), may hold values from -0.1875 to 0.1875
- fc1_bias: bfloat16 [4096], replicated, may hold values from -3 to 3
- fc2_weight: bfloat16 [4096, 1024], P('tensor', 'fsdp'), may hold values from -0.09375 to 0.09375
- fc2_bias: bfloat16 [1024], replicated, may hold values from -3 to 3
- qkv_down: bfloat16 [8, 16, 1024], P(None, None, ('fsdp', 'tensor')), may hold values from -0.1875 to 0.1875
- qkv_up: bfloat16 [8, 16, 3072], P(None, None, ('fsdp', 'tensor')), may hold values from -0.75 to 0.75
- out_down: bfloat16 [8, 16, 1024], P(None, None, ('fsdp', 'tensor')), may hold values from -0.75 to 0.75
- out_up: bfloat16 [8, 16, 1024], P(None, None, ('fsdp', 'tensor')), may hold values from -0.75 to 0.75
- fc1_down: bfloat16 [8, 16, 1024], P(None, None, ('fsdp', 'tensor')), may hold values from -0.1875 to 0.1875
- fc1_up: bfloat16 [8, 16, 4096], P(None, None, ('fsdp', 'tensor')), may hold values from -0.75 to 0.75
- fc2_down: bfloat16 [8, 16, 4096], P(None, None, ('fsdp', 'tensor')), may hold values from -0.1875 to 0.1875
- fc2_up: bfloat16 [8, 16, 1024], P(None, None, ('fsdp', 'tensor')), may hold values from -0.75 to 0.75
Outputs:
- outputs: bfloat16 [64, 577, 1024], P(('fsdp', 'tensor'))
- input_grad: float32 [64, 577, 1024], P(('fsdp', 'tensor'))
- grad_qkv_down: float32 [8, 16, 1024], P(None, None, ('fsdp', 'tensor'))
- grad_qkv_up: float32 [8, 16, 3072], P(None, None, ('fsdp', 'tensor'))
- grad_out_down: float32 [8, 16, 1024], P(None, None, ('fsdp', 'tensor'))
- grad_out_up: float32 [8, 16, 1024], P(None, None, ('fsdp', 'tensor'))
- grad_fc1_down: float32 [8, 16, 1024], P(None, None, ('fsdp', 'tensor'))
- grad_fc1_up: float32 [8, 16, 4096], P(None, None, ('fsdp', 'tensor'))
- grad_fc2_down: float32 [8, 16, 4096], P(None, None, ('fsdp', 'tensor'))
- grad_fc2_up: float32 [8, 16, 1024], P(None, None, ('fsdp', 'tensor'))
All inputs are finite; a program needn't handle non-finite values. No bound on the sum of `filled` on one device may be relied on, other than what follows from the above.
Results may differ from a plain program's by a relative error of at most 0.014.
Values may be sent and summed in bfloat16 or wider, within the bound.
No kernel may reach another device: no remote copies, remote signals or barrier semaphores. Data moves between devices by JAX's collectives and lax.ppermute only.
A program may use at most 256 MiB of HBM per device.

v0:
```python
from functools import partial

import jax
import jax.numpy as jnp
from jax import lax
from jax.sharding import PartitionSpec as P

D = 1024
HEADS = 16
HEAD_DIM = 64
FF = 4096
SEQ = 577
RANK = 16
ADAPTERS = 8


epsilon = 1e-05
highest = lax.Precision.HIGHEST


def layer_norm(values, gain_row, shift_row):
    center = values - jnp.mean(values, axis=-1, keepdims=True)
    inverse = lax.rsqrt(jnp.mean(center * center, axis=-1, keepdims=True) + epsilon)
    normed = center * inverse
    return (normed * gain_row + shift_row, normed, inverse)


def norm_back(upstream, normed, inverse, gain_row):
    scaled = upstream * gain_row
    return inverse * (
        scaled
        - jnp.mean(scaled, axis=-1, keepdims=True)
        - normed * jnp.mean(scaled * normed, axis=-1, keepdims=True)
    )


def down_map(inputs, chosen):
    return jnp.einsum("isw,irw->isr", inputs, chosen, preferred_element_type=jnp.float32).astype(
        jnp.bfloat16
    )


def up_map(low_rank, chosen):
    return jnp.einsum("isr,irw->isw", low_rank, chosen, preferred_element_type=jnp.float32)


def outer_grad(low_rank, other_side):
    return jnp.einsum("isr,isw->irw", low_rank, other_side, preferred_element_type=jnp.float32)


def attend(blocks):
    queries, key_rows, value_rows = blocks
    score_scale = HEAD_DIM ** (-0.5)
    scores = (
        jnp.einsum("qhd,khd->hqk", queries, key_rows, preferred_element_type=jnp.float32)
        * score_scale
    )
    log_total = jax.nn.logsumexp(scores, axis=-1)
    prob_rows = jnp.exp(scores - log_total[:, :, None]).astype(jnp.bfloat16)
    mixed_rows = jnp.einsum(
        "hqk,khd->qhd", prob_rows, value_rows, preferred_element_type=jnp.float32
    )
    return (mixed_rows.astype(jnp.bfloat16), log_total)


def attend_back(blocks):
    queries, key_rows, value_rows, log_total, mixed_grad = blocks
    score_scale = HEAD_DIM ** (-0.5)
    scores = (
        jnp.einsum("qhd,khd->hqk", queries, key_rows, preferred_element_type=jnp.float32)
        * score_scale
    )
    prob_rows = jnp.exp(scores - log_total[:, :, None])
    prob_grad = jnp.einsum(
        "qhd,khd->hqk", mixed_grad, value_rows, preferred_element_type=jnp.float32
    )
    value_grad = jnp.einsum(
        "hqk,qhd->khd",
        prob_rows.astype(jnp.bfloat16),
        mixed_grad,
        preferred_element_type=jnp.float32,
    )
    score_grad = (
        prob_rows * (prob_grad - jnp.sum(prob_rows * prob_grad, axis=-1, keepdims=True))
    ).astype(jnp.bfloat16)
    query_grad = (
        jnp.einsum("hqk,khd->qhd", score_grad, key_rows, preferred_element_type=jnp.float32)
        * score_scale
    )
    key_grad = (
        jnp.einsum("hqk,qhd->khd", score_grad, queries, preferred_element_type=jnp.float32)
        * score_scale
    )
    return jnp.stack([query_grad, key_grad, value_grad], axis=1).astype(jnp.bfloat16)


def on_device(
    tokens,
    cotangent,
    adapter_index,
    filled,
    ln1_gain,
    ln1_shift,
    qkv_weight,
    qv_bias,
    out_weight,
    out_bias,
    ln2_gain,
    ln2_shift,
    fc1_weight,
    fc1_bias,
    fc2_weight,
    fc2_bias,
    qkv_down,
    qkv_up,
    out_down,
    out_up,
    fc1_down,
    fc1_up,
    fc2_down,
    fc2_up,
):
    own_images = tokens.shape[0]
    own_start = lax.axis_index("tensor") * own_images
    own_mask = lax.dynamic_slice_in_dim(filled, own_start, own_images, 0).astype(jnp.float32)[
        :, None, None
    ]
    stacks = (
        lax.all_gather(qkv_down, ("fsdp", "tensor"), axis=2, tiled=True),
        lax.all_gather(qkv_up, ("fsdp", "tensor"), axis=2, tiled=True),
        lax.all_gather(out_down, ("fsdp", "tensor"), axis=2, tiled=True),
        lax.all_gather(out_up, ("fsdp", "tensor"), axis=2, tiled=True),
        lax.all_gather(fc1_down, ("fsdp", "tensor"), axis=2, tiled=True),
        lax.all_gather(fc1_up, ("fsdp", "tensor"), axis=2, tiled=True),
        lax.all_gather(fc2_down, ("fsdp", "tensor"), axis=2, tiled=True),
        lax.all_gather(fc2_up, ("fsdp", "tensor"), axis=2, tiled=True),
    )
    qkv_local, out_local, first_local, second_local = (
        lax.all_gather(qkv_weight, "fsdp", axis=0, tiled=True),
        lax.all_gather(out_weight, "fsdp", axis=1, tiled=True),
        lax.all_gather(fc1_weight, "fsdp", axis=0, tiled=True),
        lax.all_gather(fc2_weight, "fsdp", axis=1, tiled=True),
    )
    split_count = 1
    member = 0
    work_index = lax.dynamic_slice_in_dim(adapter_index, own_start, own_images, 0)
    qkv_local, out_local, first_local, second_local = (
        lax.all_gather(qkv_local, "tensor", axis=2, tiled=True),
        lax.all_gather(out_local, "tensor", axis=0, tiled=True),
        lax.all_gather(first_local, "tensor", axis=1, tiled=True),
        lax.all_gather(second_local, "tensor", axis=0, tiled=True),
    )
    local_heads = HEADS // split_count
    local_width = D // split_count
    hidden_width = FF // split_count
    hidden_start = member * hidden_width
    choose = (work_index[:, None] == jnp.arange(ADAPTERS, dtype=jnp.int32)[None, :]).astype(
        jnp.bfloat16
    )

    def select(stacked):
        return jnp.einsum(
            "ie,erw->irw", choose, stacked, preferred_element_type=jnp.float32
        ).astype(jnp.bfloat16)

    def gather_back(per_image):
        return jnp.einsum("ie,irw->erw", choose.astype(jnp.float32), per_image, precision=highest)

    qkv_up_local = stacks[1].reshape(ADAPTERS, RANK, 3, D).reshape(ADAPTERS, RANK, 3 * local_width)
    out_down_local = stacks[2]
    fc1_up_local = stacks[5]
    fc2_down_local = stacks[6]
    sel_qkv_down = select(stacks[0])
    sel_qkv_up = select(qkv_up_local)
    sel_out_down = select(out_down_local)
    sel_out_up = select(stacks[3])
    sel_fc1_down = select(stacks[4])
    sel_fc1_up = select(fc1_up_local)
    sel_fc2_down = select(fc2_down_local)
    sel_fc2_up = select(stacks[7])
    gain_one = ln1_gain.astype(jnp.float32)
    gain_two = ln2_gain.astype(jnp.float32)
    inputs = tokens.astype(jnp.float32)
    normed_one, unit_one, inverse_one = layer_norm(inputs, gain_one, ln1_shift.astype(jnp.float32))
    normed_low = normed_one.astype(jnp.bfloat16)
    images = normed_low.shape[0]
    qkv_flat = qkv_local.reshape(D, 3 * local_width)
    projected = jnp.dot(
        normed_low.reshape(images * SEQ, D), qkv_flat, preferred_element_type=jnp.float32
    ).reshape(images, SEQ, 3 * local_width)
    rank_one = down_map(normed_low, sel_qkv_down)
    bias_rows = qv_bias.astype(jnp.float32)
    bias_full = jnp.concatenate([bias_rows[0], jnp.zeros_like(bias_rows[0]), bias_rows[1]])
    projected = (projected + up_map(rank_one, sel_qkv_up) + bias_full).astype(jnp.bfloat16)
    projected = projected.reshape(images, SEQ, 3, local_heads, HEAD_DIM)
    queries = projected[:, :, 0]
    key_rows = projected[:, :, 1]
    value_rows = projected[:, :, 2]
    heads_out, log_total = lax.map(attend, (queries, key_rows, value_rows))
    mixed_low = heads_out.reshape(images, SEQ, local_width)
    attn_part = jnp.dot(
        mixed_low.reshape(images * SEQ, local_width), out_local, preferred_element_type=jnp.float32
    ).reshape(images, SEQ, D)
    rank_out = down_map(mixed_low, sel_out_down)
    attn_part = attn_part + up_map(rank_out, sel_out_up)
    middle = inputs + own_mask * (attn_part + out_bias.astype(jnp.float32))
    normed_two, unit_two, inverse_two = layer_norm(middle, gain_two, ln2_shift.astype(jnp.float32))
    normed_low_two = normed_two.astype(jnp.bfloat16)
    first_shift = fc1_bias.astype(jnp.float32)
    before = jnp.dot(
        normed_low_two.reshape(images * SEQ, D), first_local, preferred_element_type=jnp.float32
    ).reshape(images, SEQ, hidden_width)
    rank_three = down_map(normed_low_two, sel_fc1_down)
    before = before + up_map(rank_three, sel_fc1_up) + first_shift
    exact_gelu = partial(jax.nn.gelu, approximate=False)
    activated, gelu_back = jax.vjp(exact_gelu, before)
    activated = activated.astype(jnp.bfloat16)
    mlp_part = jnp.dot(
        activated.reshape(images * SEQ, hidden_width),
        second_local,
        preferred_element_type=jnp.float32,
    ).reshape(images, SEQ, D)
    rank_four = down_map(activated, sel_fc2_down)
    mlp_part = mlp_part + up_map(rank_four, sel_fc2_up)
    outputs = (middle + own_mask * (mlp_part + fc2_bias.astype(jnp.float32))).astype(jnp.bfloat16)
    upstream = cotangent.astype(jnp.float32)
    branch_grad_two = (own_mask * upstream).astype(jnp.bfloat16)
    grad_fc2_up_sel = outer_grad(rank_four, branch_grad_two)
    rank_four_grad = down_map(branch_grad_two, sel_fc2_up)
    grad_fc2_down_sel = outer_grad(rank_four_grad, activated)
    act_grad = jnp.dot(
        branch_grad_two.reshape(images * SEQ, D), second_local.T, preferred_element_type=jnp.float32
    ).reshape(images, SEQ, hidden_width)
    act_grad = act_grad + up_map(rank_four_grad, sel_fc2_down)
    pre_grad = gelu_back(act_grad)[0].astype(jnp.bfloat16)
    grad_fc1_up_sel = outer_grad(rank_three, pre_grad)
    rank_three_grad = down_map(pre_grad, sel_fc1_up)
    grad_fc1_down_sel = outer_grad(rank_three_grad, normed_low_two)
    norm_part_two = jnp.dot(
        pre_grad.reshape(images * SEQ, hidden_width),
        first_local.T,
        preferred_element_type=jnp.float32,
    ).reshape(images, SEQ, D)
    norm_part_two = norm_part_two + up_map(rank_three_grad, sel_fc1_down)
    middle_grad = upstream + norm_back(norm_part_two, unit_two, inverse_two, gain_two)
    branch_grad_one = (own_mask * middle_grad).astype(jnp.bfloat16)
    grad_out_up_sel = outer_grad(rank_out, branch_grad_one)
    rank_out_grad = down_map(branch_grad_one, sel_out_up)
    grad_out_down_sel = outer_grad(rank_out_grad, mixed_low)
    mixed_grad = jnp.dot(
        branch_grad_one.reshape(images * SEQ, D), out_local.T, preferred_element_type=jnp.float32
    ).reshape(images, SEQ, local_width)
    mixed_grad = (
        (mixed_grad + up_map(rank_out_grad, sel_out_down))
        .astype(jnp.bfloat16)
        .reshape(images, SEQ, local_heads, HEAD_DIM)
    )
    qkv_grad = lax.map(attend_back, (queries, key_rows, value_rows, log_total, mixed_grad)).reshape(
        images, SEQ, 3 * local_width
    )
    grad_qkv_up_sel = outer_grad(rank_one, qkv_grad)
    rank_one_grad = down_map(qkv_grad, sel_qkv_up)
    grad_qkv_down_sel = outer_grad(rank_one_grad, normed_low)
    norm_part_one = jnp.dot(
        qkv_grad.reshape(images * SEQ, 3 * local_width),
        qkv_flat.T,
        preferred_element_type=jnp.float32,
    ).reshape(images, SEQ, D)
    norm_part_one = norm_part_one + up_map(rank_one_grad, sel_qkv_down)
    input_grad = middle_grad + norm_back(norm_part_one, unit_one, inverse_one, gain_one)
    qkv_up_term = gather_back(grad_qkv_up_sel).reshape(ADAPTERS, RANK, 3, local_width)
    qkv_up_term = qkv_up_term.reshape(ADAPTERS, RANK, 3 * D)
    out_down_term = gather_back(grad_out_down_sel)
    fc1_up_term = gather_back(grad_fc1_up_sel)
    fc2_down_term = lax.dynamic_update_slice_in_dim(
        jnp.zeros((ADAPTERS, RANK, FF), jnp.float32),
        gather_back(grad_fc2_down_sel),
        hidden_start,
        2,
    )
    summed = (
        lax.psum_scatter(
            gather_back(grad_qkv_down_sel), ("fsdp", "tensor"), scatter_dimension=2, tiled=True
        ),
        lax.psum_scatter(qkv_up_term, ("fsdp", "tensor"), scatter_dimension=2, tiled=True),
        lax.psum_scatter(out_down_term, ("fsdp", "tensor"), scatter_dimension=2, tiled=True),
        lax.psum_scatter(
            gather_back(grad_out_up_sel), ("fsdp", "tensor"), scatter_dimension=2, tiled=True
        ),
        lax.psum_scatter(
            gather_back(grad_fc1_down_sel), ("fsdp", "tensor"), scatter_dimension=2, tiled=True
        ),
        lax.psum_scatter(fc1_up_term, ("fsdp", "tensor"), scatter_dimension=2, tiled=True),
        lax.psum_scatter(fc2_down_term, ("fsdp", "tensor"), scatter_dimension=2, tiled=True),
        lax.psum_scatter(
            gather_back(grad_fc2_up_sel), ("fsdp", "tensor"), scatter_dimension=2, tiled=True
        ),
    )
    return (
        outputs,
        input_grad,
        summed[0],
        summed[1],
        summed[2],
        summed[3],
        summed[4],
        summed[5],
        summed[6],
        summed[7],
    )


def solution(mesh):
    in_specs = (
        P(("fsdp", "tensor"), None, None),
        P(("fsdp", "tensor"), None, None),
        P("fsdp"),
        P("fsdp"),
        P(),
        P(),
        P("fsdp", None, "tensor"),
        P(),
        P("tensor", "fsdp"),
        P(),
        P(),
        P(),
        P("fsdp", "tensor"),
        P(),
        P("tensor", "fsdp"),
        P(),
        P(None, None, ("fsdp", "tensor")),
        P(None, None, ("fsdp", "tensor")),
        P(None, None, ("fsdp", "tensor")),
        P(None, None, ("fsdp", "tensor")),
        P(None, None, ("fsdp", "tensor")),
        P(None, None, ("fsdp", "tensor")),
        P(None, None, ("fsdp", "tensor")),
        P(None, None, ("fsdp", "tensor")),
    )
    out_specs = (
        P(("fsdp", "tensor"), None, None),
        P(("fsdp", "tensor"), None, None),
        P(None, None, ("fsdp", "tensor")),
        P(None, None, ("fsdp", "tensor")),
        P(None, None, ("fsdp", "tensor")),
        P(None, None, ("fsdp", "tensor")),
        P(None, None, ("fsdp", "tensor")),
        P(None, None, ("fsdp", "tensor")),
        P(None, None, ("fsdp", "tensor")),
        P(None, None, ("fsdp", "tensor")),
    )
    return jax.shard_map(
        on_device, mesh=mesh, in_specs=in_specs, out_specs=out_specs, check_vma=False
    )
```

profile of v0, /device:TPU:0, one launch (start us, length us, event | category | flops | bytes accessed | tf_op | source)
XLA Modules:
  0.0 1887.6 jit_solution(1588785827851483272)
XLA Ops:
  12.9 68.2 %all-gather.11.cloned.1.call-done = bf16[1024,3,512]{2,0,1:T(8,128)(2,1)} async-done(((bf16[64,3,512]{2,0,1:T(8,128)(2,1)}), bf16[1024,3,512]{2,0,1:T(8,128)(2,1)}) %all-gather.11.cloned.1.call-update) | async-done | bytes 3145744 | tf_op jit(solution)/shard_map/all_gather | solution.py:139
  85.9 52.4 %all-gather.15.cloned.1.call-done = bf16[512,1024]{0,1:T(8,128)(2,1)} async-done(((bf16[512,64]{0,1:T(8,128)(2,1)}), bf16[512,1024]{0,1:T(8,128)(2,1)}) %all-gather.15.cloned.1.call-update) | async-done | bytes 1048592 | tf_op jit(solution)/shard_map/all_gather | solution.py:140
  140.6 75.4 %all-gather.19.cloned.1.call-done = bf16[1024,2048]{1,0:T(8,128)(2,1)} async-done(((bf16[64,2048]{1,0:T(8,128)(2,1)}), bf16[1024,2048]{1,0:T(8,128)(2,1)}) %all-gather.19.cloned.1.call-update) | async-done | bytes 4194320 | tf_op jit(solution)/shard_map/all_gather | solution.py:141
  216.2 47.4 %all_gather.50 = bf16[8,16,1024]{1,0,2:T(8,128)(2,1)S(1)} all-gather(bf16[8,16,32]{1,0,2:T(8,128)(2,1)S(1)} %copy.143), channel_id=1, replica_groups=mesh['fsdp'=16,'tensor'=2] {'fsdp','tensor'}, dimensions={2}, use_global_device_ids=true | all-gather | bytes 270336 | tf_op jit(solution)/shard_map/all_gather | solution.py:129
  265.5 78.6 %all_gather.51 = bf16[8,16,3072]{1,0,2:T(8,128)(2,1)} all-gather(bf16[8,16,96]{1,0,2:T(8,128)(2,1)S(1)} %copy.146), channel_id=1, replica_groups=mesh['fsdp'=16,'tensor'=2] {'fsdp','tensor'}, dimensions={2}, use_global_device_ids=true | all-gather | bytes 811008 | tf_op jit(solution)/shard_map/all_gather | solution.py:130
  350.9 58.2 %all_gather.54 = bf16[8,16,1024]{1,0,2:T(8,128)(2,1)S(1)} all-gather(bf16[8,16,32]{1,0,2:T(8,128)(2,1)S(1)} %copy.152), channel_id=1, replica_groups=mesh['fsdp'=16,'tensor'=2] {'fsdp','tensor'}, dimensions={2}, use_global_device_ids=true | all-gather | bytes 270336 | tf_op jit(solution)/shard_map/all_gather | solution.py:131
  411.5 44.4 %all_gather.55 = bf16[8,16,1024]{1,0,2:T(8,128)(2,1)S(1)} all-gather(bf16[8,16,32]{1,0,2:T(8,128)(2,1)S(1)} %copy.156), channel_id=1, replica_groups=mesh['fsdp'=16,'tensor'=2] {'fsdp','tensor'}, dimensions={2}, use_global_device_ids=true | all-gather | bytes 270336 | tf_op jit(solution)/shard_map/all_gather | solution.py:132
  461.4 46.8 %all_gather.58 = bf16[8,16,1024]{1,0,2:T(8,128)(2,1)} all-gather(bf16[8,16,32]{1,0,2:T(8,128)(2,1)} %copy.159), channel_id=1, replica_groups=mesh['fsdp'=16,'tensor'=2] {'fsdp','tensor'}, dimensions={2}, use_global_device_ids=true | all-gather | bytes 270336 | tf_op jit(solution)/shard_map/all_gather | solution.py:133
  513.8 46.7 %all_gather.63 = bf16[8,16,1024]{1,0,2:T(8,128)(2,1)} all-gather(bf16[8,16,32]{1,0,2:T(8,128)(2,1)} %copy.167), channel_id=1, replica_groups=mesh['fsdp'=16,'tensor'=2] {'fsdp','tensor'}, dimensions={2}, use_global_device_ids=true | all-gather | bytes 270336 | tf_op jit(solution)/shard_map/all_gather | solution.py:136
  624.5 75.3 %while.22 = (s32[]{:T(128)}, bf16[2,577,16,64]{1,3,2,0:T(8,128)(2,1)}, f32[2,16,577]{2,1,0:T(8,128)S(1)}, bf16[2,577,16,64]{1,3,2,0:T(8,128)(2,1)}, bf16[2,577,1...) while((s32[]{:T(128)}, bf16[2,577,16,64]{1,3,2,0:T(8,128)(2,1)}, ...), condition=%wide.region_5.6_spmd, body=%wide.region_2.5_spmd.sunk | while | flops 1406956800 | bytes 81693424 | solution.py:199
  648.9 13.5 fusion.241
  686.2 13.4 fusion.241
  721.6 25.3 %fusion.79 = (u8[577,4096]{1,0:T(8,128)(4,1)}, f32[2,577,4096]{2,1,0:T(8,128)}) fusion(f32[4096]{0:T(1024)S(1)} %copy-done.66, f32[2,577,4096]{2,1,0:T(8,128)} %fusion.98, bf16[2,577,1024]{2,1,0:T(8,128)(2,1)S(1)} %add_convert_fusion.4, bf16[1024,4096]{1,0:T(8,128)(2,1)} %all-gather.21.cloned.1.call-done), kind=kOutput, calls=%fused_computation.115 | convolution fusion | flops 9720631296 | bytes 50946048 | tf_op jit(solution)/shard_map/dot_general | solution.py:210
  746.9 45.7 %multiply_convert_fusion.3 = (bf16[2,577,4096]{2,1,0:T(8,128)(2,1)}, f32[2,577,4096]{2,1,0:T(8,128)}) fusion(f32[2,577,4096]{2,1,0:T(8,128)} %get-tuple-element.164, u8[577,4096]{1,0:T(8,128)(4,1)} %get-tuple-element.163), kind=kLoop, calls=%fused_computation.67 | loop fusion | flops 321421312 | bytes 49631232 | tf_op jit(solution)/shard_map/convert_element_type | solution.py:217
  792.6 30.4 %add_convert_fusion = bf16[2,577,4096]{2,1,0:T(8,128)(2,1)} fusion(f32[2,577,4096]{2,1,0:T(8,128)} %get-tuple-element.151, f32[2,577,4096]{2,1,0:T(8,128)} %fusion.94, f32[2,577,4096]{2,1,0:T(8,128)} %get-tuple-element.164, bf16[4096,1024]{1,0:T(8,128)(2,1)} %all-gather.27.cloned.1.call-done, f32[2]{0:T(128)S(1)} %copy-done.70, bf16[2,577,1024]{2,0,1:T(2,128)(2,1)} %param.29), kind=kOutput, calls=%fused_computation.66 | convolution fusion | flops 9754900480 | bytes 76926984 | tf_op jit(solution)/shard_map/dot_general | solution.py:231
  846.7 18.1 fusion.166
  898.3 158.9 %while.23 = (s32[]{:T(128)}, bf16[2,577,3,16,64]{1,4,3,2,0:T(8,128)(2,1)}, bf16[2,577,16,64]{1,3,2,0:T(8,128)(2,1)S(1)}, bf16[2,577,16,64]{1,3,2,0:T(8,128)(2,1)...) while((s32[]{:T(128)}, ...), condition=%wide.region_12.13_spmd, body=%wide.region_10.12_spmd.sunk | while | flops 3486695424 | bytes 239253520 | solution.py:258
  911.9 15.9 multiply_reduce_fusion.7
  927.8 16.0 multiply_convert_fusion.6
  960.7 13.5 fusion.252
  991.1 15.9 multiply_reduce_fusion.7
  1007.0 15.9 multiply_convert_fusion.6
  1039.9 13.5 fusion.252
  1121.5 13.4 copy.219
  1134.9 18.2 reshape.209
  1208.6 14.1 add_convert_fusion.3
  1229.8 13.6 reduce-scatter.31.cloned.1.call-done
  1245.2 130.5 %reduce-scatter.25.cloned.1.call-done = f32[32,128]{1,0:T(8,128)} async-done(((f32[1024,128]{1,0:T(8,128)}), f32[32,128]{1,0:T(8,128)}) %reduce-scatter.25.cloned.1.call-update) | async-done | bytes 16400
  1377.3 130.2 %reduce-scatter.35.cloned.1.call-done = f32[32,128]{1,0:T(8,128)} async-done(((f32[1024,128]{1,0:T(8,128)}), f32[32,128]{1,0:T(8,128)}) %reduce-scatter.35.cloned.1.call-update) | async-done | bytes 16400
  1509.1 97.3 %reduce-scatter.27.cloned.1.call-done = f32[96,128]{1,0:T(8,128)} async-done(((f32[3072,128]{1,0:T(8,128)}), f32[96,128]{1,0:T(8,128)}) %reduce-scatter.27.cloned.1.call-update) | async-done | bytes 49168
  1608.6 135.7 %reduce-scatter.21.cloned.1.call-done = f32[8,16,128]{2,0,1:T(8,128)} async-done(((f32[8,16,4096]{2,0,1:T(8,128)}), f32[8,16,128]{2,0,1:T(8,128)}) %reduce-scatter.21.cloned.1.call-update) | async-done | bytes 65552 | tf_op jit(solution)/shard_map/reduce_scatter | solution.py:293
  1745.8 133.3 %reduce-scatter.23.cloned.1.call-done = f32[8,16,128]{2,0,1:T(8,128)} async-done(((f32[8,16,4096]{2,0,1:T(8,128)}), f32[8,16,128]{2,0,1:T(8,128)}) %reduce-scatter.23.cloned.1.call-update) | async-done | bytes 65552 | tf_op jit(solution)/shard_map/reduce_scatter | solution.py:294
  (361 shorter events, 429.1 us)
Async XLA Ops:
  7.2 73.9 %all-gather.11.cloned.1.call-start = ((), (), s32[]{:S(2)}) async-start(), calls=%async_computation.8 | async-start | bytes 3342336 | tf_op jit(solution)/shard_map/all_gather | solution.py:139
  7.9 130.3 %all-gather.15.cloned.1.call-start = ((), (), s32[]{:S(2)}) async-start(), calls=%async_computation.10 | async-start | bytes 1114112 | tf_op jit(solution)/shard_map/all_gather | solution.py:140
  8.7 207.3 %all-gather.19.cloned.1.call-start = ((), (), s32[]{:S(2)}) async-start(), calls=%async_computation.12 | async-start | bytes 4456448 | tf_op jit(solution)/shard_map/all_gather | solution.py:141
  9.4 563.4 %all-gather.23.cloned.1.call-start = ((), (), s32[]{:S(2)}) async-start(), calls=%async_computation.14 | async-start | bytes 1081344 | tf_op jit(solution)/shard_map/all_gather | solution.py:134
  10.8 564.4 %all-gather.29.cloned.1.call-start = ((), (), s32[]{:S(2)}) async-start(), calls=%async_computation.17 | async-start | bytes 1081344 | tf_op jit(solution)/shard_map/all_gather | solution.py:135
  12.3 573.5 %all-gather.25.cloned.1.call-start = ((), (), s32[]{:S(2)}) async-start(), calls=%async_computation.15 | async-start | bytes 4456448 | tf_op jit(solution)/shard_map/all_gather | solution.py:142
  12.9 579.7 %all-gather.13.cloned.1.call-start = ((), (), s32[]{:S(2)}) async-start(), calls=%async_computation.9 | async-start | bytes 9437184 | tf_op jit(solution)/shard_map/all_gather | solution.py:148
  85.8 130.3 %copy-start.57 = (bf16[8,16,32]{2,1,0:T(8,128)(2,1)S(1)}, bf16[8,16,32]{2,1,0:T(8,128)(2,1)}, u32[]{:S(2)}) copy-start(bf16[8,16,32]{2,1,0:T(8,128)(2,1)} %param.44) | copy-start | bytes 24580
  85.8 617.2 %all-gather.17.cloned.1.call-start = ((), (), s32[]{:S(2)}) async-start(), calls=%async_computation.11 | async-start | bytes 3145728 | tf_op jit(solution)/shard_map/all_gather | solution.py:149
  140.5 124.7 %copy-start.74 = (bf16[1024]{0:T(1024)(128)(2,1)S(1)}, bf16[1024]{0:T(1024)(128)(2,1)}, u32[]{:S(2)}) copy-start(bf16[1024]{0:T(1024)(128)(2,1)} %param.32) | copy-start | bytes 6148
  140.5 124.7 %copy-start.75 = (bf16[1024]{0:T(1024)(128)(2,1)S(1)}, bf16[1024]{0:T(1024)(128)(2,1)}, u32[]{:S(2)}) copy-start(bf16[1024]{0:T(1024)(128)(2,1)} %param.33) | copy-start | bytes 6148
  140.5 124.8 %copy-start.58 = (bf16[8,16,96]{2,1,0:T(8,128)(2,1)S(1)}, bf16[8,16,96]{2,1,0:T(8,128)(2,1)}, u32[]{:S(2)}) copy-start(bf16[8,16,96]{2,1,0:T(8,128)(2,1)} %param.45) | copy-start | bytes 73732
  140.5 581.0 %all-gather.21.cloned.1.call-start = ((), (), s32[]{:S(2)}) async-start(), calls=%async_computation.13 | async-start | bytes 12582912 | tf_op jit(solution)/shard_map/all_gather | solution.py:150
  216.0 576.7 %all-gather.27.cloned.1.call-start = ((), (), s32[]{:S(2)}) async-start(), calls=%async_computation.16 | async-start | bytes 12582912 | tf_op jit(solution)/shard_map/all_gather | solution.py:151
  265.3 327.3 %copy-start.62 = (f32[1024]{0:T(1024)}, f32[1024]{0:T(1024)S(1)}, u32[]{:S(2)}) copy-start(f32[1024]{0:T(1024)S(1)} %convert_element_type.142) | copy-start | bytes 12292
  265.3 327.3 %copy-start.72 = (f32[1024]{0:T(1024)}, f32[1024]{0:T(1024)S(1)}, u32[]{:S(2)}) copy-start(f32[1024]{0:T(1024)S(1)} %convert_element_type.143) | copy-start | bytes 12292
  350.7 107.5 %copy-start.76 = (bf16[1024]{0:T(1024)(128)(2,1)S(1)}, bf16[1024]{0:T(1024)(128)(2,1)}, u32[]{:S(2)}) copy-start(bf16[1024]{0:T(1024)(128)(2,1)} %param.37) | copy-start | bytes 6148
  350.7 108.1 %copy-start.77 = (bf16[1024]{0:T(1024)(128)(2,1)S(1)}, bf16[1024]{0:T(1024)(128)(2,1)}, u32[]{:S(2)}) copy-start(bf16[1024]{0:T(1024)(128)(2,1)} %param.38) | copy-start | bytes 6148
  350.8 109.9 %copy-start.61 = (bf16[8,16,32]{2,1,0:T(8,128)(2,1)S(1)}, bf16[8,16,32]{2,1,0:T(8,128)(2,1)}, u32[]{:S(2)}) copy-start(bf16[8,16,32]{2,1,0:T(8,128)(2,1)} %param.48) | copy-start | bytes 24580
  458.2 106.9 %copy-start.6 = (bf16[2,577,1024]{2,0,1:T(2,128)(2,1)S(1)}, bf16[2,577,1024]{2,0,1:T(2,128)(2,1)}, u32[]{:S(2)}) copy-start(bf16[2,577,1024]{2,0,1:T(2,128)(2,1)} %param.28) | copy-start | bytes 7090180
  592.2 634.3 %reduce-scatter.33.cloned.1.call-start = ((), (), s32[]{:S(2)}) async-start(), calls=%async_computation.24 | async-start | bytes 540672
  710.2 154.7 %copy-start.44 = (f32[2,577]{1,0:T(2,128)}, f32[2,577]{1,0:T(2,128)S(1)}, u32[]{:S(2)}) copy-start(f32[2,577]{1,0:T(2,128)S(1)} %broadcast_multiply_fusion.4) | copy-start | bytes 13852
  710.9 154.0 %copy-start.48 = (f32[2,577]{1,0:T(2,128)}, f32[2,577]{1,0:T(2,128)S(1)}, u32[]{:S(2)}) copy-start(f32[2,577]{1,0:T(2,128)S(1)} %add_rsqrt_fusion) | copy-start | bytes 13852
  846.7 381.5 %reduce-scatter.29.cloned.1.call-start = ((), (), s32[]{:S(2)}) async-start(), calls=%async_computation.22 | async-start | bytes 540672
  898.2 345.3 %reduce-scatter.31.cloned.1.call-start = ((), (), s32[]{:S(2)}) async-start(), calls=%async_computation.23 | async-start | bytes 540672
  898.3 158.9 %copy-start.34 = (bf16[2,577,16]{1,2,0:T(8,128)(2,1)S(1)}, bf16[2,577,16]{1,2,0:T(8,128)(2,1)}, u32[]{:S(2)}) copy-start(bf16[2,577,16]{1,2,0:T(8,128)(2,1)} %copy-done.33) | copy-start | bytes 110788
  898.3 161.1 %copy-start.43 = (s32[2]{0:T(128)S(1)}, s32[2]{0:T(128)}, u32[]{:S(2)}) copy-start(s32[2]{0:T(128)} %copy-done.41) | copy-start | bytes 28
  1073.0 302.6 %reduce-scatter.25.cloned.1.call-start = ((), (), s32[]{:S(2)}) async-start(), calls=%async_computation.20 | async-start | bytes 540672
  1092.5 414.9 %reduce-scatter.35.cloned.1.call-start = ((), (), s32[]{:S(2)}) async-start(), calls=%async_computation.25 | async-start | bytes 540672
  1113.7 492.7 %reduce-scatter.27.cloned.1.call-start = ((), (), s32[]{:S(2)}) async-start(), calls=%async_computation.21 | async-start | bytes 1622016
  1153.1 591.2 %reduce-scatter.21.cloned.1.call-start = ((), (), s32[]{:S(2)}) async-start(), calls=%async_computation.18 | async-start | bytes 2162688 | tf_op jit(solution)/shard_map/reduce_scatter | solution.py:293
  1161.5 717.7 %reduce-scatter.23.cloned.1.call-start = ((), (), s32[]{:S(2)}) async-start(), calls=%async_computation.19 | async-start | bytes 2162688 | tf_op jit(solution)/shard_map/reduce_scatter | solution.py:294
  (74 other events, 1058.0 us)
Sparse Core Ops, SparseCore 0:
  10.8 70.2 all-gather.10
  83.9 54.3 all-gather.14
  141.0 74.8 all-gather.18
  219.2 49.8 all-gather.22
  271.9 56.4 all-gather.28
  331.0 88.4 all-gather.24
  421.0 17.7 all-gather.12
  440.9 11.9 all-gather.16
  454.4 21.4 all-gather.20
  592.3 17.2 all-gather.26
  846.8 132.3 reduce-scatter.32
  981.4 129.7 reduce-scatter.28
  1113.4 130.0 reduce-scatter.30
  1245.7 129.9 reduce-scatter.24
  1377.7 129.7 reduce-scatter.34
  1513.4 92.9 reduce-scatter.26
  1608.6 135.6 reduce-scatter.20
  1746.4 132.6 reduce-scatter.22
where the time goes:
time: 1900 us; the launch traced here: 1890 us
  waiting for transfers between devices  839 us (44%)
  matrix products  386 us (20%)
  blocking collectives  322 us (17%)
  local copies, waits for them, and re-layouts  193 us (10%)
  other arithmetic  130 us (7%)
    unnamed x24, waiting for transfers between devices  374 us
    reduce_scatter x1, waiting for transfers between devices, on_device(): lax.psum_scatter(fc1_up_term, ('fsdp', 'tensor'), scatter_dimension=2, ti...  136 us
    reduce_scatter x1, waiting for transfers between devices, on_device(): lax.psum_scatter(fc2_down_term, ('fsdp', 'tensor'), scatter_dimension=2,...  133 us
    unnamed x200, local copies, waits for them, and re-layouts  131 us
    all_gather x1, blocking collectives, on_device(): lax.all_gather(qkv_up, ('fsdp', 'tensor'), axis=2, tiled=True)  78.6 us
    all_gather x1, waiting for transfers between devices, on_device(): lax.all_gather(fc1_weight, 'fsdp', axis=0, tiled=True)  75.4 us
    all_gather x1, waiting for transfers between devices, on_device(): lax.all_gather(qkv_weight, 'fsdp', axis=0, tiled=True)  68.2 us
    all_gather x1, blocking collectives, on_device(): lax.all_gather(out_down, ('fsdp', 'tensor'), axis=2, tiled=True)  58.2 us
  transfers between devices with their start and end apart: 18, of which 9 were waited for; matrix products, arithmetic and copies ran while one was open for 34% of the time, Pallas kernels for 0%

commit v1 on v0

--- a/solution.py
+++ b/solution.py
@@ -125,31 +125,38 @@
     own_mask = lax.dynamic_slice_in_dim(filled, own_start, own_images, 0).astype(jnp.float32)[
         :, None, None
     ]
-    stacks = (
-        lax.all_gather(qkv_down, ("fsdp", "tensor"), axis=2, tiled=True),
-        lax.all_gather(qkv_up, ("fsdp", "tensor"), axis=2, tiled=True),
-        lax.all_gather(out_down, ("fsdp", "tensor"), axis=2, tiled=True),
-        lax.all_gather(out_up, ("fsdp", "tensor"), axis=2, tiled=True),
-        lax.all_gather(fc1_down, ("fsdp", "tensor"), axis=2, tiled=True),
-        lax.all_gather(fc1_up, ("fsdp", "tensor"), axis=2, tiled=True),
-        lax.all_gather(fc2_down, ("fsdp", "tensor"), axis=2, tiled=True),
-        lax.all_gather(fc2_up, ("fsdp", "tensor"), axis=2, tiled=True),
-    )
-    qkv_local, out_local, first_local, second_local = (
-        lax.all_gather(qkv_weight, "fsdp", axis=0, tiled=True),
-        lax.all_gather(out_weight, "fsdp", axis=1, tiled=True),
-        lax.all_gather(fc1_weight, "fsdp", axis=0, tiled=True),
-        lax.all_gather(fc2_weight, "fsdp", axis=1, tiled=True),
-    )
+    stack_list = (qkv_down, qkv_up, out_down, out_up, fc1_down, fc1_up, fc2_down, fc2_up)
+    widths = [stacked.shape[2] for stacked in stack_list]
+    packed = lax.all_gather(jnp.concatenate(stack_list, axis=2), ("fsdp", "tensor"), axis=0)
+    members = packed.shape[0]
+    stacks = []
+    offset = 0
+    for width in widths:
+        part = packed[:, :, :, offset : offset + width]
+        stacks.append(part.transpose(1, 2, 0, 3).reshape(ADAPTERS, RANK, members * width))
+        offset += width
+    rows = qkv_weight.shape[0]
+    group = fc1_weight.shape[1]
+    column = qkv_weight.shape[2]
+    weights = jnp.concatenate(
+        [qkv_weight.reshape(rows, 3 * column), out_weight.T, fc1_weight, fc2_weight.T], axis=1
+    )
+    weights = lax.all_gather(weights, "fsdp", axis=0, tiled=True)
+    weights = lax.all_gather(weights, "tensor", axis=0)
+    qkv_local = (
+        weights[:, :, : 3 * column]
+        .reshape(-1, D, 3, column)
+        .transpose(1, 2, 0, 3)
+        .reshape(D, 3, D)
+    )
+    out_local = weights[:, :, 3 * column : 4 * column].transpose(0, 2, 1).reshape(D, D)
+    first_local = (
+        weights[:, :, 4 * column : 4 * column + group].transpose(1, 0, 2).reshape(D, FF)
+    )
+    second_local = weights[:, :, 4 * column + group :].transpose(0, 2, 1).reshape(FF, D)
     split_count = 1
     member = 0
     work_index = lax.dynamic_slice_in_dim(adapter_index, own_start, own_images, 0)
-    qkv_local, out_local, first_local, second_local = (
-        lax.all_gather(qkv_local, "tensor", axis=2, tiled=True),
-        lax.all_gather(out_local, "tensor", axis=0, tiled=True),
-        lax.all_gather(first_local, "tensor", axis=1, tiled=True),
-        lax.all_gather(second_local, "tensor", axis=0, tiled=True),
-    )
     local_heads = HEADS // split_count
     local_width = D // split_count
     hidden_width = FF // split_count
@@ -278,24 +285,31 @@
         hidden_start,
         2,
     )
-    summed = (
-        lax.psum_scatter(
-            gather_back(grad_qkv_down_sel), ("fsdp", "tensor"), scatter_dimension=2, tiled=True
-        ),
-        lax.psum_scatter(qkv_up_term, ("fsdp", "tensor"), scatter_dimension=2, tiled=True),
-        lax.psum_scatter(out_down_term, ("fsdp", "tensor"), scatter_dimension=2, tiled=True),
-        lax.psum_scatter(
-            gather_back(grad_out_up_sel), ("fsdp", "tensor"), scatter_dimension=2, tiled=True
-        ),
-        lax.psum_scatter(
-            gather_back(grad_fc1_down_sel), ("fsdp", "tensor"), scatter_dimension=2, tiled=True
-        ),
-        lax.psum_scatter(fc1_up_term, ("fsdp", "tensor"), scatter_dimension=2, tiled=True),
-        lax.psum_scatter(fc2_down_term, ("fsdp", "tensor"), scatter_dimension=2, tiled=True),
-        lax.psum_scatter(
-            gather_back(grad_fc2_up_sel), ("fsdp", "tensor"), scatter_dimension=2, tiled=True
-        ),
-    )
+    terms = (
+        gather_back(grad_qkv_down_sel),
+        qkv_up_term,
+        out_down_term,
+        gather_back(grad_out_up_sel),
+        gather_back(grad_fc1_down_sel),
+        fc1_up_term,
+        fc2_down_term,
+        gather_back(grad_fc2_up_sel),
+    )
+    packed_terms = jnp.concatenate(
+        [
+            term.reshape(ADAPTERS, RANK, members, width).transpose(2, 0, 1, 3)
+            for term, width in zip(terms, widths)
+        ],
+        axis=3,
+    )
+    scattered = lax.psum_scatter(
+        packed_terms, ("fsdp", "tensor"), scatter_dimension=0, tiled=False
+    )
+    summed = []
+    offset = 0
+    for width in widths:
+        summed.append(scattered[:, :, offset : offset + width])
+        offset += width
     return (
         outputs,
         input_grad,

time: 1900 us -> 1090 us (0.57)
  waiting for transfers between devices: 839 us -> 306 us
  blocking collectives: 322 us -> 0 us
  local copies, waits for them, and re-layouts: 193 us -> 258 us
    unnamed x24 -> x4, waiting for transfers between devices: 374 us -> 0.07 us
    all_gather x6 -> x0, blocking collectives: 322 us -> none  [the longest x1 78.6 us: on_device(): lax.all_gather(qkv_up, ('fsdp', 'tensor'), axis=2, tiled=True)]
    reduce_scatter x2 -> x1, waiting for transfers between devices: 269 us -> 93.4 us  [on_device(): lax.psum_scatter(packed_terms, ('fsdp', 'tensor'), scatter_dimension=0, t...]
    unnamed x200 -> x180, local copies, waits for them, and re-layouts: 131 us -> 18.8 us
    transpose x0 -> x8, local copies, waits for them, and re-layouts: none -> 82 us  [the longest x1 24.9 us: on_device(): weights[:, :, 4 * column:4 * column + group].transpose(1, 0, 2)]
    reshape x0 -> x19, local copies, waits for them, and re-layouts: none -> 56.1 us  [the longest x12 27.8 us: on_device(): term.reshape(ADAPTERS, RANK, members, width).transpose(2, 0, 1, 3)]
    all_gather x9 -> x0, local copies, waits for them, and re-layouts: 33.3 us -> none  [the longest x1 6.65 us: on_device(): lax.all_gather(qkv_up, ('fsdp', 'tensor'), axis=2, tiled=True)]
    slice x0 -> x8, local copies, waits for them, and re-layouts: none -> 31.6 us  [the longest x2 14.5 us: on_device(): weights[:, :, :3 * column].reshape(-1, D, 3, column).transpose(1, 2, 0, 3)]
  transfers between devices with their start and end apart: 18 -> 4, of which waited for: 9 -> 3; matrix products, arithmetic and copies ran while one was open for 34% -> 11% of each run, Pallas kernels for 0% -> 0%
where the time goes in v1:
time: 1090 us; the launch traced here: 1080 us
  matrix products  375 us (34%)
  waiting for transfers between devices  306 us (28%)
  local copies, waits for them, and re-layouts  258 us (24%)
  other arithmetic  128 us (12%)
  between operations  15.1 us (1%)
    all_gather x1, waiting for transfers between devices, on_device(): weights = lax.all_gather(weights, 'fsdp', axis=0, tiled=True)  154 us
    reduce_scatter x1, waiting for transfers between devices, on_device(): lax.psum_scatter(packed_terms, ('fsdp', 'tensor'), scatter_dimension=0, t...  93.4 us
    all_gather x1, waiting for transfers between devices, on_device(): lax.all_gather(jnp.concatenate(stack_list, axis=2), ('fsdp', 'tensor'), a...  58.2 us
    convert_element_type x1, other arithmetic, on_device(): activated = activated.astype(jnp.bfloat16)  45.8 us
    dot_general x8, matrix products, up_map(): jnp.einsum('isr,irw->isw', low_rank, chosen, preferred_element_type=jnp.f...  33.6 us
    dot_general x2, matrix products, attend_back(): jnp.einsum('qhd,khd->hqk', mixed_grad, value_rows, preferred_element_type...  31.7 us
    convert_element_type x2, other arithmetic, attend_back(): score_grad = (prob_rows * (prob_grad - jnp.sum(prob_rows * prob_grad, axi...  31.7 us
    dot_general x1, matrix products, on_device(): jnp.dot(branch_grad_two.reshape(images * SEQ, D), second_local.T, preferr...  28.8 us
  transfers between devices with their start and end apart: 4, of which 3 were waited for; matrix products, arithmetic and copies ran while one was open for 11% of the time, Pallas kernels for 0%

profile of v1, /device:TPU:0, one launch (start us, length us, event | category | flops | bytes accessed | tf_op | source)
XLA Modules:
  0.0 1084.0 jit_solution(3230829216132796515)
XLA Ops:
  12.0 154.2 %all-gather.6.cloned.1.call-done = bf16[1024,6144]{1,0:T(8,128)(2,1)} async-done(((bf16[64,6144]{1,0:T(8,128)(2,1)}), bf16[1024,6144]{1,0:T(8,128)(2,1)}) %all-gather.6.cloned.1.call-update) | async-done | bytes 12582928 | tf_op jit(solution)/shard_map/all_gather | solution.py:144
  171.1 58.2 %all-gather.10.cloned.1.call-done = bf16[256,16,512]{2,1,0:T(8,128)(2,1)} async-done(((bf16[8,16,512]{2,1,0:T(8,128)(2,1)}), bf16[256,16,512]{2,1,0:T(8,128)(2,1)}) %all-gather.10.cloned.1.call-update) | async-done | bytes 4194320 | tf_op jit(solution)/shard_map/all_gather | solution.py:130
  297.6 12.1 %slice_bitcast_fusion = (bf16[2,2048,1024]{1,2,0:T(8,128)(2,1)}, bf16[1024,2,2048]{2,0,1:T(8,128)(2,1)}) fusion(bf16[2,1024,6144]{2,1,0:T(8,128)(2,1)} %bitcast.318), kind=kLoop, calls=%fused_computation.83 | loop fusion | bytes 33554432 | tf_op jit(solution)/shard_map/transpose | solution.py:156
  318.3 16.4 %copy.204 = bf16[1024,3,2,512]{3,2,1,0:T(2,128)(2,1)} copy(bf16[1024,3,2,512]{0,3,1,2:T(8,128)(2,1)} %bitcast.315) | data formatting | bytes 12582912 | tf_op jit(solution)/shard_map/transpose | solution.py:149
  334.7 14.8 %reshape.275 = bf16[1024,3072,1]{1,0,2:T(8,128)(2,1)} reshape(bf16[1024,3,2,512]{3,2,1,0:T(2,128)(2,1)} %copy.204) | data formatting | bytes 12582912 | tf_op jit(solution)/shard_map/reshape;reshape | solution.py:194
  349.6 11.2 %fusion.143 = f32[2,577,3072]{2,1,0:T(8,128)S(1)} fusion(bf16[1024,3072,1]{1,0,2:T(8,128)(2,1)} %reshape.275, f32[1024]{0:T(1024)S(1)} %convert_element_type.143, f32[1024]{0:T(1024)S(1)} %convert_element_type.142, f32[2,577]{1,0:T(2,128)S(1)} %add_rsqrt_fusion.1, f32[2,577]{1,0:T(2,128)S(1)} %broadcast_multiply_fusion.5, ...), kind=kOutput, calls=%fused_computation.230 | convolution fusion | flops 7267430400 | bytes 22852624 | tf_op jit(solution)/shard_map/dot_general | solution.py:195
  381.3 74.8 %while.22 = (s32[]{:T(128)}, bf16[2,577,16,64]{1,3,2,0:T(8,128)(2,1)}, f32[2,16,577]{2,1,0:T(8,128)S(1)}, bf16[2,577,16,64]{1,3,2,0:T(8,128)(2,1)}, bf16[2,577,1...) while((s32[]{:T(128)}, bf16[2,577,16,64]{1,3,2,0:T(8,128)(2,1)}, ...), condition=%wide.region_5.6_spmd, body=%wide.region_2.5_spmd.sunk | while | flops 1406956800 | bytes 81693424 | solution.py:206
  381.7 13.2 %multiply_reduce_fusion.6 = (f32[16,577]{1,0:T(8,128)S(1)}, f32[16,577,577]{1,2,0:T(8,128)}) fusion(bf16[2,577,16,64]{1,3,2,0:T(8,128)(2,1)S(1)} %get-tuple-element.304, s32[]{:T(128)} %get-tuple-element.292, bf16[2,577,16,64]{1,3,2,0:T(8,128)(2,1)} %get-tuple-element.303), kind=kOutput, calls=%fused_computation.2.clone.1 | convolution fusion | flops 692483072 | bytes 23966848 | tf_op jit(solution)/shard_map/while/body/eval_jaxpr/qhd,khd->hqk/dot_general | solution.py:55
  394.9 10.6 exponential_reduce_fusion.2
  405.6 13.4 %fusion.235 = bf16[2,577,16,64]{1,3,2,0:T(8,128)(2,1)} fusion(bf16[2,577,16,64]{1,3,2,0:T(8,128)(2,1)} %get-tuple-element.293, s32[]{:T(128)} %get-tuple-element.292, f32[16,577,577]{1,2,0:T(8,128)} %get-tuple-element.274, f32[16,577]{1,0:T(8,128)S(1)} %fusion.234, bf16[2,577,16,64]{1,3,2,0:T(8,128)(2,1)S(1)} %copy-done.6), kind=kOutput, calls=%fused_computation.8.clone.1 | convolution fusion | flops 698410048 | bytes 26584064 | tf_op jit(solution)/shard_map/while/body/eval_jaxpr/hqk,khd->qhd/dot_general | solution.py:60
  418.9 13.2 %multiply_reduce_fusion.6 = (f32[16,577]{1,0:T(8,128)S(1)}, f32[16,577,577]{1,2,0:T(8,128)}) fusion(bf16[2,577,16,64]{1,3,2,0:T(8,128)(2,1)S(1)} %get-tuple-element.304, s32[]{:T(128)} %get-tuple-element.292, bf16[2,577,16,64]{1,3,2,0:T(8,128)(2,1)} %get-tuple-element.303), kind=kOutput, calls=%fused_computation.2.clone.1 | convolution fusion | flops 692483072 | bytes 23966848 | tf_op jit(solution)/shard_map/while/body/eval_jaxpr/qhd,khd->hqk/dot_general | solution.py:55
  442.8 13.4 %fusion.235 = bf16[2,577,16,64]{1,3,2,0:T(8,128)(2,1)} fusion(bf16[2,577,16,64]{1,3,2,0:T(8,128)(2,1)} %get-tuple-element.293, s32[]{:T(128)} %get-tuple-element.292, f32[16,577,577]{1,2,0:T(8,128)} %get-tuple-element.274, f32[16,577]{1,0:T(8,128)S(1)} %fusion.234, bf16[2,577,16,64]{1,3,2,0:T(8,128)(2,1)S(1)} %copy-done.6), kind=kOutput, calls=%fused_computation.8.clone.1 | convolution fusion | flops 698410048 | bytes 26584064 | tf_op jit(solution)/shard_map/while/body/eval_jaxpr/hqk,khd->qhd/dot_general | solution.py:60
  473.2 24.9 %copy.217 = bf16[1024,2,2048]{2,1,0:T(2,128)(2,1)} copy(bf16[1024,2,2048]{2,0,1:T(8,128)(2,1)S(1)} %bitcast.310) | data formatting | bytes 16777216 | tf_op jit(solution)/shard_map/transpose | solution.py:154
  498.1 14.5 %reshape.278 = bf16[1024,4096,1]{1,0,2:T(8,128)(2,1)} reshape(bf16[1024,2,2048]{2,1,0:T(2,128)(2,1)} %copy.217) | data formatting | bytes 16777216 | tf_op jit(solution)/shard_map/reshape | solution.py:154
  512.6 11.9 %copy.222 = bf16[2,2048,1024]{2,1,0:T(8,128)(2,1)} copy(bf16[2,2048,1024]{1,2,0:T(8,128)(2,1)} %get-tuple-element.166) | data formatting | bytes 16777216 | tf_op jit(solution)/shard_map/transpose | solution.py:156
  536.4 25.4 %fusion.73 = (u8[577,4096]{1,0:T(8,128)(4,1)}, f32[2,577,4096]{2,1,0:T(8,128)}) fusion(f32[4096]{0:T(1024)S(1)} %copy-done.65, f32[2,577,4096]{2,1,0:T(8,128)} %fusion.82, bf16[2,577,1024]{2,1,0:T(8,128)(2,1)S(1)} %add_convert_fusion.4, bf16[1024,4096,1]{1,0,2:T(8,128)(2,1)} %reshape.278), kind=kOutput, calls=%fused_computation.111 | convolution fusion | flops 9720631296 | bytes 50946048 | tf_op jit(solution)/shard_map/dot_general | solution.py:217
  561.8 45.8 %multiply_convert_fusion.3 = (bf16[2,577,4096]{2,1,0:T(8,128)(2,1)}, f32[2,577,4096]{2,1,0:T(8,128)}) fusion(f32[2,577,4096]{2,1,0:T(8,128)} %get-tuple-element.190, u8[577,4096]{1,0:T(8,128)(4,1)} %get-tuple-element.189), kind=kLoop, calls=%fused_computation.67 | loop fusion | flops 321421312 | bytes 49631232 | tf_op jit(solution)/shard_map/convert_element_type | solution.py:224
  607.7 28.8 %add_convert_fusion = bf16[2,577,4096]{2,1,0:T(8,128)(2,1)} fusion(f32[2,577,4096]{2,1,0:T(8,128)} %get-tuple-element.161, f32[2,577,4096]{2,1,0:T(8,128)} %fusion.78, f32[2,577,4096]{2,1,0:T(8,128)} %get-tuple-element.190, bf16[4096,1024,1]{1,0,2:T(8,128)(2,1)} %bitcast.330, f32[2]{0:T(128)} %copy-done.68, bf16[2,577,1024]{2,0,1:T(2,128)(2,1)S(1)} %copy-done.12), kind=kOutput, calls=%fused_computation.66 | convolution fusion | flops 9754900480 | bytes 76926984 | tf_op jit(solution)/shard_map/dot_general | solution.py:238
  653.6 16.6 %fusion.150 = (f32[2,577]{1,0:T(2,128)S(1)}, f32[2,577]{1,0:T(2,128)S(1)}, f32[2,577,1024]{2,1,0:T(8,128)S(1)}) fusion(f32[2,577]{1,0:T(2,128)S(1)} %add_rsqrt_fusion, f32[2,577,1024]{2,1,0:T(8,128)S(1)} %bitcast.303, f32[2,577]{1,0:T(2,128)S(1)} %broadcast_multiply_fusion.4, f32[1024]{0:T(1024)S(1)} %copy-done.63, f32[2,577,1024]{2,1,0:T(8,128)} %fusion.99, ...), kind=kOutput, calls=%fused_computation.233 | convolution fusion | flops 9688723456 | bytes 32045088 | tf_op jit(solution)/shard_map/dot_general | solution.py:246
  689.0 158.1 %while.23 = (s32[]{:T(128)}, bf16[2,577,3,16,64]{1,4,3,2,0:T(8,128)(2,1)}, bf16[2,577,16,64]{1,3,2,0:T(8,128)(2,1)S(1)}, bf16[2,577,16,64]{1,3,2,0:T(8,128)(2,1)...) while((s32[]{:T(128)}, ...), condition=%wide.region_12.13_spmd, body=%wide.region_10.12_spmd.sunk | while | flops 3486695424 | bytes 239253520 | solution.py:265
  689.4 13.2 %fusion.245 = f32[16,577,577]{1,2,0:T(8,128)} fusion(bf16[2,577,16,64]{1,3,2,0:T(8,128)(2,1)} %get-tuple-element.325, s32[]{:T(128)} %get-tuple-element.314, bf16[2,577,16,64]{1,3,2,0:T(8,128)(2,1)S(1)} %get-tuple-element.324), kind=kOutput, calls=%fused_computation.44.clone.1 | convolution fusion | flops 681838592 | bytes 23929920 | tf_op jit(solution)/shard_map/while/body/eval_jaxpr/qhd,khd->hqk/dot_general | solution.py:70
  702.5 15.9 %multiply_reduce_fusion.7 = (f32[16,577]{1,0:T(8,128)S(1)}, f32[16,577,577]{1,2,0:T(8,128)}) fusion(f32[16,577,577]{1,2,0:T(8,128)} %fusion.245, f32[16,577]{1,0:T(8,128)S(1)} %dynamic-slice_bitcast_fusion.2, bf16[2,577,16,64]{1,3,2,0:T(8,128)(2,1)} %get-tuple-element.328, s32[]{:T(128)} %get-tuple-element.314, ...), kind=kOutput, calls=%fused_computation.26.clone.1 | convolution fusion | flops 703136768 | bytes 47924416 | tf_op jit(solution)/shard_map/while/body/eval_jaxpr/qhd,khd->hqk/dot_general | solution.py:74
  718.4 15.9 %multiply_convert_fusion.6 = bf16[16,577,577]{1,2,0:T(8,128)(2,1)S(1)} fusion(f32[16,577,577]{1,2,0:T(8,128)} %get-tuple-element.283, f32[16,577,577]{1,2,0:T(8,128)} %fusion.245, f32[16,577]{1,0:T(8,128)S(1)} %get-tuple-element.284, f32[16,577]{1,0:T(8,128)S(1)} %dynamic-slice_bitcast_fusion.2), kind=kLoop, calls=%fused_computation.25.clone.1 | loop fusion | flops 26634320 | bytes 53342496 | tf_op jit(solution)/shard_map/while/body/eval_jaxpr/convert_element_type | solution.py:85
  751.1 13.4 %fusion.246 = bf16[1,577,1,16,64]{1,4,3,2,0:T(8,128)(2,1)} fusion(f32[16,577,577]{1,2,0:T(8,128)} %fusion.245, f32[16,577]{1,0:T(8,128)S(1)} %dynamic-slice_bitcast_fusion.2, bf16[2,577,16,64]{1,3,2,0:T(8,128)(2,1)} %get-tuple-element.327, s32[]{:T(128)} %get-tuple-element.314), kind=kOutput, calls=%fused_computation.38.clone.1 | convolution fusion | flops 698410048 | bytes 26450496 | tf_op jit(solution)/shard_map/while/body/eval_jaxpr/hqk,qhd->khd/dot_general | solution.py:77
  768.2 13.2 %fusion.245 = f32[16,577,577]{1,2,0:T(8,128)} fusion(bf16[2,577,16,64]{1,3,2,0:T(8,128)(2,1)} %get-tuple-element.325, s32[]{:T(128)} %get-tuple-element.314, bf16[2,577,16,64]{1,3,2,0:T(8,128)(2,1)S(1)} %get-tuple-element.324), kind=kOutput, calls=%fused_computation.44.clone.1 | convolution fusion | flops 681838592 | bytes 23929920 | tf_op jit(solution)/shard_map/while/body/eval_jaxpr/qhd,khd->hqk/dot_general | solution.py:70
  781.3 15.9 %multiply_reduce_fusion.7 = (f32[16,577]{1,0:T(8,128)S(1)}, f32[16,577,577]{1,2,0:T(8,128)}) fusion(f32[16,577,577]{1,2,0:T(8,128)} %fusion.245, f32[16,577]{1,0:T(8,128)S(1)} %dynamic-slice_bitcast_fusion.2, bf16[2,577,16,64]{1,3,2,0:T(8,128)(2,1)} %get-tuple-element.328, s32[]{:T(128)} %get-tuple-element.314, ...), kind=kOutput, calls=%fused_computation.26.clone.1 | convolution fusion | flops 703136768 | bytes 47924416 | tf_op jit(solution)/shard_map/while/body/eval_jaxpr/qhd,khd->hqk/dot_general | solution.py:74
  797.2 15.9 %multiply_convert_fusion.6 = bf16[16,577,577]{1,2,0:T(8,128)(2,1)S(1)} fusion(f32[16,577,577]{1,2,0:T(8,128)} %get-tuple-element.283, f32[16,577,577]{1,2,0:T(8,128)} %fusion.245, f32[16,577]{1,0:T(8,128)S(1)} %get-tuple-element.284, f32[16,577]{1,0:T(8,128)S(1)} %dynamic-slice_bitcast_fusion.2), kind=kLoop, calls=%fused_computation.25.clone.1 | loop fusion | flops 26634320 | bytes 53342496 | tf_op jit(solution)/shard_map/while/body/eval_jaxpr/convert_element_type | solution.py:85
  829.9 13.4 %fusion.246 = bf16[1,577,1,16,64]{1,4,3,2,0:T(8,128)(2,1)} fusion(f32[16,577,577]{1,2,0:T(8,128)} %fusion.245, f32[16,577]{1,0:T(8,128)S(1)} %dynamic-slice_bitcast_fusion.2, bf16[2,577,16,64]{1,3,2,0:T(8,128)(2,1)} %get-tuple-element.327, s32[]{:T(128)} %get-tuple-element.314), kind=kOutput, calls=%fused_computation.38.clone.1 | convolution fusion | flops 698410048 | bytes 26450496 | tf_op jit(solution)/shard_map/while/body/eval_jaxpr/hqk,qhd->khd/dot_general | solution.py:77
  909.5 15.2 %concatenate.23 = f32[32,8,16,512]{3,2,1,0:T(8,128)} concatenate(f32[32,8,16,32]{3,2,1,0:T(8,128)} %bitcast.327, f32[32,8,16,96]{3,2,1,0:T(8,128)} %bitcast.326, f32[32,8,16,32]{3,2,1,0:T(8,128)} %bitcast.325, f32[32,8,16,32]{3,2,1,0:T(8,128)} %bitcast.324, f32[32,8,16,32]{3,2,1,0:T(8,128)} %bitcast.323, f32[32,8,16,128]{3,2,1,0:T(8,128)} %bitcast.322, ...), dimensions={3} | concatenate | bytes 16777216 | tf_op jit(solution)/shard_map/concatenate | solution.py:298
  925.4 13.3 %fusion.160 = f32[2,577,1024]{2,1,0:T(8,128)S(1)} fusion(bf16[2,577,3072]{1,2,0:T(8,128)(2,1)} %bitcast.314, bf16[1024,3072,1]{1,0,2:T(8,128)(2,1)} %reshape.275), kind=kOutput, calls=%fused_computation.242 | convolution fusion | flops 7260340224 | bytes 18108416 | tf_op jit(solution)/shard_map/dot_general | solution.py:271
  960.7 14.1 %add_convert_fusion.3 = bf16[2,577,1024]{2,1,0:T(8,128)(2,1)S(1)} fusion(f32[2,577,1024]{2,1,0:T(8,128)S(1)} %bitcast.305, f32[2,577,1024]{2,1,0:T(8,128)} %fusion.97, f32[1024]{0:T(1024)S(1)} %convert_element_type.165, f32[2]{0:T(128)S(1)} %copy-done.71, bf16[2,577,4096]{2,1,0:T(8,128)(2,1)S(1)} %bitcast.307, bf16[4096,1024,1]{1,0,2:T(8,128)(2,1)} %bitcast.331), kind=kOutput, calls=%fused_computation.108 | convolution fusion | flops 9686362112 | bytes 29663240 | tf_op jit(solution)/shard_map/dot_general | solution.py:225
  978.7 93.4 %reduce-scatter.2.cloned.1.call-done = f32[1,8,16,512]{3,2,1,0:T(8,128)} async-done(((f32[32,8,16,512]{3,2,1,0:T(8,128)}), f32[1,8,16,512]{3,2,1,0:T(8,128)}) %reduce-scatter.2.cloned.1.call-update) | async-done | bytes 262160 | tf_op jit(solution)/shard_map/reduce_scatter | solution.py:305
  (329 shorter events, 316.6 us)
Async XLA Ops:
  7.2 158.9 %all-gather.6.cloned.1.call-start = ((), (), s32[]{:S(2)}) async-start(), calls=%async_computation.1 | async-start | bytes 13369344 | tf_op jit(solution)/shard_map/all_gather | solution.py:144
  10.2 219.1 %all-gather.10.cloned.1.call-start = ((), (), s32[]{:S(2)}) async-start(), calls=%async_computation.4 | async-start | bytes 4325376 | tf_op jit(solution)/shard_map/all_gather | solution.py:130
  11.9 276.8 %all-gather.8.cloned.1.call-start = ((), (), s32[]{:S(2)}) async-start(), calls=%async_computation.3 | async-start | bytes 37748736 | tf_op jit(solution)/shard_map/all_gather | solution.py:145
  166.2 905.9 %reduce-scatter.2.cloned.1.call-start = ((), (), s32[]{:S(2)}) async-start(), calls=%async_computation.2 | async-start | bytes 8650752 | tf_op jit(solution)/shard_map/reduce_scatter | solution.py:305
  166.8 182.8 %copy-start.60 = (f32[1024]{0:T(1024)}, f32[1024]{0:T(1024)S(1)}, u32[]{:S(2)}) copy-start(f32[1024]{0:T(1024)S(1)} %convert_element_type.142) | copy-start | bytes 12292
  166.8 182.8 %copy-start.72 = (f32[1024]{0:T(1024)}, f32[1024]{0:T(1024)S(1)}, u32[]{:S(2)}) copy-start(f32[1024]{0:T(1024)S(1)} %convert_element_type.143) | copy-start | bytes 12292
  169.3 108.4 %copy-start.45 = (s32[2]{0:T(128)}, s32[2]{0:T(128)S(1)}, u32[]{:S(2)}) copy-start(s32[2]{0:T(128)S(1)} %dynamic_slice.33) | copy-start | bytes 28
  169.4 108.9 %copy-start.68 = (f32[2]{0:T(128)}, f32[2]{0:T(128)S(1)}, u32[]{:S(2)}) copy-start(f32[2]{0:T(128)S(1)} %dynamic-slice_convert_fusion) | copy-start | bytes 28
  170.1 179.5 %copy-start.49 = (f32[2,577]{1,0:T(2,128)}, f32[2,577]{1,0:T(2,128)S(1)}, u32[]{:S(2)}) copy-start(f32[2,577]{1,0:T(2,128)S(1)} %broadcast_multiply_fusion.5) | copy-start | bytes 13852
  171.1 178.6 %copy-start.53 = (f32[2,577]{1,0:T(2,128)}, f32[2,577]{1,0:T(2,128)S(1)}, u32[]{:S(2)}) copy-start(f32[2,577]{1,0:T(2,128)S(1)} %add_rsqrt_fusion.1) | copy-start | bytes 13852
  265.5 12.8 %copy-start.11 = (bf16[2,577,1024]{2,0,1:T(2,128)(2,1)S(1)}, bf16[2,577,1024]{2,0,1:T(2,128)(2,1)}, u32[]{:S(2)}) copy-start(bf16[2,577,1024]{2,0,1:T(2,128)(2,1)} %param.29) | copy-start | bytes 7090180
  266.8 12.2 %copy-start.39 = (bf16[2,16,1024]{2,0,1:T(2,128)(2,1)}, bf16[2,16,1024]{2,0,1:T(2,128)(2,1)S(1)}, u32[]{:S(2)}) copy-start(bf16[2,16,1024]{2,0,1:T(2,128)(2,1)S(1)} %convolution_convert_fusion.7) | copy-start | bytes 196612
  273.4 87.5 %copy-start.21 = (bf16[2,16,3072]{2,0,1:T(2,128)(2,1)}, bf16[2,16,3072]{2,0,1:T(2,128)(2,1)S(1)}, u32[]{:S(2)}) copy-start(bf16[2,16,3072]{2,0,1:T(2,128)(2,1)S(1)} %convolution_convert_fusion.2) | copy-start | bytes 589828
  280.5 80.3 %copy-start.41 = (bf16[2,577,16]{1,2,0:T(8,128)(2,1)}, bf16[2,577,16]{1,2,0:T(8,128)(2,1)S(1)}, u32[]{:S(2)}) copy-start(bf16[2,577,16]{1,2,0:T(8,128)(2,1)S(1)} %convolution_convert_fusion.15) | copy-start | bytes 110788
  381.3 79.5 %copy-start.23 = (bf16[2,16,1024]{2,0,1:T(2,128)(2,1)S(1)}, bf16[2,16,1024]{2,0,1:T(2,128)(2,1)}, u32[]{:S(2)}) copy-start(bf16[2,16,1024]{2,0,1:T(2,128)(2,1)} %convolution_convert_fusion.6) | copy-start | bytes 196612
  456.2 12.2 %copy-start.1 = (bf16[2,577,16,64]{1,3,2,0:T(8,128)(2,1)}, bf16[2,577,16,64]{1,3,2,0:T(8,128)(2,1)S(1)}, u32[]{:S(2)}) copy-start(bf16[2,577,16,64]{1,3,2,0:T(8,128)(2,1)S(1)} %get-tuple-element.334) | copy-start | bytes 7090180
  470.3 199.9 %copy-start.47 = (f32[2,577]{1,0:T(2,128)}, f32[2,577]{1,0:T(2,128)S(1)}, u32[]{:S(2)}) copy-start(f32[2,577]{1,0:T(2,128)S(1)} %broadcast_multiply_fusion.4) | copy-start | bytes 13852
  473.1 197.1 %copy-start.51 = (f32[2,577]{1,0:T(2,128)}, f32[2,577]{1,0:T(2,128)S(1)}, u32[]{:S(2)}) copy-start(f32[2,577]{1,0:T(2,128)S(1)} %add_rsqrt_fusion) | copy-start | bytes 13852
  512.6 11.9 %copy-start.62 = (f32[1024]{0:T(1024)S(1)}, f32[1024]{0:T(1024)}, u32[]{:S(2)}) copy-start(f32[1024]{0:T(1024)} %convert_element_type.154) | copy-start | bytes 12292
  512.6 11.9 %copy-start.64 = (f32[1024]{0:T(1024)S(1)}, f32[1024]{0:T(1024)}, u32[]{:S(2)}) copy-start(f32[1024]{0:T(1024)} %convert_element_type.155) | copy-start | bytes 12292
  561.8 45.8 %copy-start.12 = (bf16[2,577,1024]{2,0,1:T(2,128)(2,1)S(1)}, bf16[2,577,1024]{2,0,1:T(2,128)(2,1)}, u32[]{:S(2)}) copy-start(bf16[2,577,1024]{2,0,1:T(2,128)(2,1)} %param.29) | copy-start | bytes 7090180
  636.5 17.0 %slice-start = ((s8[4784128]{0:T(1024)(128)(4,1)}), s8[4194304]{0:T(1024)(128)(4,1)S(1)}, s32[]{:S(2)}) async-start(s8[4784128]{0:T(1024)(128)(4,1)} %bitcast.302), calls=%async_computation.5 | async-start | bytes 8388608
  653.6 16.7 %copy-start.70 = (f32[2]{0:T(128)S(1)}, f32[2]{0:T(128)}, u32[]{:S(2)}) copy-start(f32[2]{0:T(128)} %copy-done.68) | copy-start | bytes 28
  689.0 158.2 %copy-start.42 = (bf16[2,577,16]{1,2,0:T(8,128)(2,1)S(1)}, bf16[2,577,16]{1,2,0:T(8,128)(2,1)}, u32[]{:S(2)}) copy-start(bf16[2,577,16]{1,2,0:T(8,128)(2,1)} %copy-done.41) | copy-start | bytes 110788
  847.1 11.3 %copy-start.5 = (bf16[2,577,4096]{2,1,0:T(8,128)(2,1)S(1)}, bf16[2,577,4096]{2,1,0:T(8,128)(2,1)}, u32[]{:S(2)}) copy-start(bf16[2,577,4096]{2,1,0:T(8,128)(2,1)} %get-tuple-element.160) | copy-start | bytes 28360708
  924.7 16.4 %slice-start.2 = ((s8[4784128]{0:T(1024)(128)(4,1)}), s8[589824]{0:T(1024)(128)(4,1)S(1)}, s32[]{:S(2)}) async-start(s8[4784128]{0:T(1024)(128)(4,1)} %bitcast.304), calls=%async_computation.7 | async-start | bytes 1179648
  925.4 13.3 %copy-start.40 = (bf16[2,16,1024]{2,0,1:T(2,128)(2,1)S(1)}, bf16[2,16,1024]{2,0,1:T(2,128)(2,1)}, u32[]{:S(2)}) copy-start(bf16[2,16,1024]{2,0,1:T(2,128)(2,1)} %copy-done.39) | copy-start | bytes 196612
  925.4 13.3 %copy-start.44 = (bf16[2,577,16]{1,2,0:T(8,128)(2,1)S(1)}, bf16[2,577,16]{1,2,0:T(8,128)(2,1)}, u32[]{:S(2)}) copy-start(bf16[2,577,16]{1,2,0:T(8,128)(2,1)} %convolution_convert_fusion.8) | copy-start | bytes 110788
  925.4 15.8 %slice-start.3 = ((s8[4784128]{0:T(1024)(128)(4,1)}), s8[4194304]{0:T(1024)(128)(4,1)S(1)}, s32[]{:S(2)}) async-start(s8[4784128]{0:T(1024)(128)(4,1)} %bitcast.304), calls=%async_computation.8 | async-start | bytes 8388608
  941.2 19.5 %slice-start.4 = ((s8[9568256]{0:T(1024)(128)(4,1)}), s8[4194304]{0:T(1024)(128)(4,1)S(1)}, s32[]{:S(2)}) async-start(s8[9568256]{0:T(1024)(128)(4,1)} %bitcast.306), calls=%async_computation.9 | async-start | bytes 8388608
  941.3 19.5 %slice-start.5 = ((s8[9568256]{0:T(1024)(128)(4,1)}), s8[4194304]{0:T(1024)(128)(4,1)S(1)}, s32[]{:S(2)}) async-start(s8[9568256]{0:T(1024)(128)(4,1)} %bitcast.306), calls=%async_computation.10 | async-start | bytes 8388608
  949.4 11.3 %slice-start.6 = ((s8[9568256]{0:T(1024)(128)(4,1)}), s8[1179648]{0:T(1024)(128)(4,1)S(1)}, s32[]{:S(2)}) async-start(s8[9568256]{0:T(1024)(128)(4,1)} %bitcast.306), calls=%async_computation.11 | async-start | bytes 2359296
  (66 other events, 352.8 us)
Sparse Core Ops, SparseCore 0:
  11.4 154.7 all-gather.5
  169.0 60.2 all-gather.9
  230.8 38.8 all-gather.7
  924.9 147.2 reduce-scatter.1

commit v2 on v1

v2 whole, which is shorter than its diff:
```python
from functools import partial

import jax
import jax.numpy as jnp
from jax import lax
from jax.experimental import pallas as pl
from jax.experimental.pallas import tpu as pltpu
from jax.sharding import PartitionSpec as P

D = 1024
HEADS = 16
HEAD_DIM = 64
FF = 4096
SEQ = 577
RANK = 16
ADAPTERS = 8
STACK = ADAPTERS * RANK
TILE = 512

epsilon = 1e-05
bf16 = jnp.bfloat16
f32 = jnp.float32
NN = (((1,), (0,)), ((), ()))
NT = (((1,), (1,)), ((), ()))
TN = (((0,), (0,)), ((), ()))
BOTH = ("fsdp", "tensor")


def dot(left, right, dims):
    return lax.dot_general(left, right, dims, preferred_element_type=f32)


def params():
    return pltpu.CompilerParams(vmem_limit_bytes=60 << 20)


def cost(flops, moved, exps=0):
    return pl.CostEstimate(flops=flops, bytes_accessed=moved, transcendentals=exps)


def smem():
    return pl.BlockSpec(memory_space=pltpu.SMEM)


def whole(shape):
    return pl.BlockSpec(shape, lambda *_: (0,) * len(shape), pipeline_mode=pl.Buffered(1))


def image_rows(width=D):
    return pl.BlockSpec((pl.Squeezed(), SEQ, width), lambda i: (i, 0, 0))


def normalize(values):
    center = values - jnp.mean(values, axis=-1, keepdims=True)
    inverse = lax.rsqrt(jnp.mean(center * center, axis=-1, keepdims=True) + epsilon)
    return center * inverse, inverse


def norm_back(upstream, normed, inverse, gain_row):
    scaled = upstream * gain_row
    return inverse * (
        scaled
        - jnp.mean(scaled, axis=-1, keepdims=True)
        - normed * jnp.mean(scaled * normed, axis=-1, keepdims=True)
    )


def chosen_lanes(adapter):
    lanes = lax.broadcasted_iota(jnp.int32, (1, STACK), 1)
    return (lanes // RANK) == adapter


def keep(product, adapter):
    return jnp.where(chosen_lanes(adapter), product, 0.0).astype(bf16)


def add_to(ref, value, first):
    @pl.when(first)
    def _():
        ref[...] = value

    @pl.when(jnp.logical_not(first))
    def _():
        ref[...] += value


def flat(block):
    return block.reshape(D, block.shape[-1])


def qkv_kernel(
    index_ref, tokens_ref, weight_ref, down_ref, up_ref, bias_ref, gain_ref, shift_ref,
    q_ref, k_ref, v_ref, low_ref, a_s, low_s,
):
    group = pl.program_id(0)
    image = pl.program_id(1)

    @pl.when(group == 0)
    def _():
        normed, _ = normalize(tokens_ref[...].astype(f32))
        a = (normed * gain_ref[...] + shift_ref[...]).astype(bf16)
        a_s[image] = a
        low_s[image] = keep(dot(a, down_ref[...], NN), index_ref[image])

    a = a_s[image]
    low = low_s[image]
    low_ref[...] = low
    width = q_ref.shape[-1]
    weight = flat(weight_ref[...])
    start = pl.multiple_of(group * width, width)
    bias = bias_ref[...].astype(f32)
    for part, out_ref in enumerate((q_ref, k_ref, v_ref)):
        value = dot(a, weight[:, part * width : (part + 1) * width], NN)
        value += dot(low, up_ref[pl.ds(part * D + start, width), :], NT)
        if part != 1:
            value += bias[part // 2 : part // 2 + 1]
        out_ref[...] = value.astype(bf16)


def qkv_project(tokens, weights, down, up, index, bias, gain, shift):
    images = tokens.shape[0]
    members, groups, rows, columns = weights.shape
    width = D // groups
    sq = pl.Squeezed()
    out = pl.BlockSpec((sq, SEQ, width), lambda g, i: (i, 0, g))
    vector = whole((1, D))
    return pl.pallas_call(
        qkv_kernel,
        grid=(groups, images),
        in_specs=[
            smem(),
            pl.BlockSpec((sq, SEQ, D), lambda g, i: (i, 0, 0)),
            pl.BlockSpec((members, sq, rows, 3 * width), lambda g, i: (0, g, 0, 0)),
            whole((D, STACK)),
            whole((3 * D, STACK)),
            pl.BlockSpec((2, width), lambda g, i: (0, g)),
            vector,
            vector,
        ],
        out_specs=[out, out, out, pl.BlockSpec((sq, SEQ, STACK), lambda g, i: (i, 0, 0))],
        out_shape=[jax.ShapeDtypeStruct((images, SEQ, D), bf16)] * 3
        + [jax.ShapeDtypeStruct((images, SEQ, STACK), bf16)],
        scratch_shapes=[
            pltpu.VMEM((images, SEQ, D), bf16),
            pltpu.VMEM((images, SEQ, STACK), bf16),
        ],
        compiler_params=params(),
        cost_estimate=cost(6 * images * SEQ * D * D, 20 << 20),
        name="qkv_project",
    )(index, tokens, weights, down, up, bias, gain, shift)


def attend_kernel(q_ref, k_ref, v_ref, o_ref, w_ref):
    q = q_ref[...]
    k = k_ref[...]
    v = v_ref[...]
    low = lax.broadcasted_iota(jnp.int32, q.shape, 1) < HEAD_DIM
    outs = []
    for head in range(2):
        own = low if head == 0 else jnp.logical_not(low)
        queries = jnp.where(own, q * HEAD_DIM**-0.5, jnp.zeros_like(q)).astype(bf16)
        scores = dot(queries, k, NT)
        top = jnp.max(scores, axis=-1, keepdims=True)
        raised = jnp.exp(scores - top)
        total = jnp.sum(raised, axis=-1, keepdims=True)
        prob = (raised * (1.0 / total)).astype(bf16)
        w_ref[head] = prob
        outs.append(dot(prob, v, NN))
    o_ref[...] = jnp.where(low, outs[0], outs[1]).astype(bf16)


def pair_rows():
    return pl.BlockSpec((pl.Squeezed(), SEQ, 2 * HEAD_DIM), lambda i, h: (i, 0, h))


def pair_weights():
    return pl.BlockSpec((2, SEQ, SEQ), lambda i, h: (i * (HEADS // 2) + h, 0, 0))


def attend(q, k, v):
    images = q.shape[0]
    return pl.pallas_call(
        attend_kernel,
        grid=(images, HEADS // 2),
        in_specs=[pair_rows()] * 3,
        out_specs=[pair_rows(), pair_weights()],
        out_shape=[
            jax.ShapeDtypeStruct((images, SEQ, D), bf16),
            jax.ShapeDtypeStruct((images * HEADS, SEQ, SEQ), bf16),
        ],
        compiler_params=params(),
        cost_estimate=cost(16 * images * SEQ * SEQ * D, 40 << 20, images * HEADS * SEQ * SEQ),
        name="attend",
    )(q, k, v)


def attend_back_kernel(q_ref, k_ref, v_ref, do_ref, w_ref, dq_ref, dk_ref, dv_ref):
    q = q_ref[...]
    k = k_ref[...]
    v = v_ref[...]
    do = do_ref[...]
    low = lax.broadcasted_iota(jnp.int32, q.shape, 1) < HEAD_DIM
    grads = []
    for head in range(2):
        own = low if head == 0 else jnp.logical_not(low)
        mixed_grad = jnp.where(own, do, jnp.zeros_like(do))
        prob_grad = dot(mixed_grad, v, NT)
        prob_low = w_ref[head]
        prob = prob_low.astype(f32)
        inner = jnp.sum(prob * prob_grad, axis=-1, keepdims=True)
        score_grad = (prob * (prob_grad - inner)).astype(bf16)
        grads.append((dot(score_grad, k, NN), dot(score_grad, q, TN), dot(prob_low, do, TN)))
    scale = HEAD_DIM**-0.5
    dq_ref[...] = (jnp.where(low, grads[0][0], grads[1][0]) * scale).astype(bf16)
    dk_ref[...] = (jnp.where(low, grads[0][1], grads[1][1]) * scale).astype(bf16)
    dv_ref[...] = jnp.where(low, grads[0][2], grads[1][2]).astype(bf16)


def attend_back(q, k, v, do, prob):
    images = q.shape[0]
    return pl.pallas_call(
        attend_back_kernel,
        grid=(images, HEADS // 2),
        in_specs=[pair_rows()] * 4 + [pair_weights()],
        out_specs=[pair_rows()] * 3,
        out_shape=[jax.ShapeDtypeStruct((images, SEQ, D), bf16)] * 3,
        compiler_params=params(),
        cost_estimate=cost(32 * images * SEQ * SEQ * D, 48 << 20),
        name="attend_back",
    )(q, k, v, do, prob)


def out_kernel(
    index_ref, filled_ref, tokens_ref, o_ref, weight_ref, down_ref, up_ref, bias_ref,
    h_ref, low_ref,
):
    image = pl.program_id(0)
    o = o_ref[...]
    low = keep(dot(o, down_ref[...], NN), index_ref[image])
    low_ref[...] = low
    value = dot(low, up_ref[...], NT) + bias_ref[...]
    width = weight_ref.shape[-1]
    for group in range(weight_ref.shape[1]):
        weight = flat(weight_ref[:, group])
        value += dot(o[:, group * width : (group + 1) * width], weight, NT)
    h_ref[...] = tokens_ref[...].astype(f32) + filled_ref[image].astype(f32) * value


def out_project(tokens, o, weights, down, up, index, filled, bias):
    images = tokens.shape[0]
    members, groups, rows, width = weights.shape
    return pl.pallas_call(
        out_kernel,
        grid=(images,),
        in_specs=[
            smem(),
            smem(),
            image_rows(),
            image_rows(),
            whole((members, groups, rows, width)),
            whole((D, STACK)),
            whole((D, STACK)),
            whole((1, D)),
        ],
        out_specs=[image_rows(), image_rows(STACK)],
        out_shape=[
            jax.ShapeDtypeStruct((images, SEQ, D), f32),
            jax.ShapeDtypeStruct((images, SEQ, STACK), bf16),
        ],
        compiler_params=params(),
        cost_estimate=cost(2 * images * SEQ * D * D, 12 << 20),
        name="out_project",
    )(index, filled, tokens, o, weights, down, up, bias)


def out_back_kernel(
    index_ref, filled_ref, dh_ref, o_ref, low_ref, weight_ref, down_ref, up_ref,
    do_ref, grad_up_ref, grad_down_ref,
):
    image = pl.program_id(0)
    branch = (dh_ref[...] * filled_ref[image].astype(f32)).astype(bf16)
    low_grad = keep(dot(branch, up_ref[...], NN), index_ref[image])
    width = weight_ref.shape[-1]
    for group in range(weight_ref.shape[1]):
        span = slice(group * width, (group + 1) * width)
        value = dot(branch, flat(weight_ref[:, group]), NN)
        value += dot(low_grad, down_ref[span, :], NT)
        do_ref[:, span] = value.astype(bf16)
    add_to(grad_up_ref, dot(low_ref[...], branch, TN).T, image == 0)
    add_to(grad_down_ref, dot(low_grad, o_ref[...], TN).T, image == 0)


def out_back(dh, o, low, weights, down, up, index, filled):
    images = dh.shape[0]
    members, groups, rows, width = weights.shape
    grad = pl.BlockSpec((D, STACK), lambda i: (0, 0))
    return pl.pallas_call(
        out_back_kernel,
        grid=(images,),
        in_specs=[
            smem(),
            smem(),
            image_rows(),
            image_rows(),
            image_rows(STACK),
            whole((members, groups, rows, width)),
            whole((D, STACK)),
            whole((D, STACK)),
        ],
        out_specs=[image_rows(), grad, grad],
        out_shape=[jax.ShapeDtypeStruct((images, SEQ, D), bf16)]
        + [jax.ShapeDtypeStruct((D, STACK), f32)] * 2,
        compiler_params=params(),
        cost_estimate=cost(2 * images * SEQ * D * D, 12 << 20),
        name="out_back",
    )(index, filled, dh, o, low, weights, down, up)


def mlp_kernel(
    index_ref, filled_ref, h_ref, cot_ref, first_ref, second_ref, down1_ref, up1_ref, down2_ref,
    up2_ref, bias1_ref, bias2_ref, gain_ref, shift_ref,
    out_ref, dh_ref, grad_up2_ref, grad_down2_ref, grad_up1_ref, grad_down1_ref,
    a_s, dz_s, low3_s, dlow4_s, z_s, da_s, low4_s, dlow3_s,
):
    tile = pl.program_id(0)
    image = pl.program_id(1)
    last = tile == pl.num_programs(0) - 1
    adapter = index_ref[image]
    mask = filled_ref[image].astype(f32)

    @pl.when(tile == 0)
    def _():
        normed, _ = normalize(h_ref[image])
        a = (normed * gain_ref[...] + shift_ref[...]).astype(bf16)
        a_s[image] = a
        dz = (cot_ref[image].astype(f32) * mask).astype(bf16)
        dz_s[image] = dz
        low3_s[image] = keep(dot(a, down1_ref[...], NN), adapter)
        dlow4_s[image] = keep(dot(dz, up2_ref[...], NN), adapter)

    a = a_s[image]
    dz = dz_s[image]
    low3 = low3_s[image]
    dlow4 = dlow4_s[image]
    first = flat(first_ref[...])
    second = flat(second_ref[...])
    before = dot(a, first, NN) + dot(low3, up1_ref[...], NT) + bias1_ref[...]
    density = jnp.exp(before * before * -0.5) * 0.3989422804014327
    below = 0.5 * lax.erf(before * 0.7071067811865476) + 0.5
    g = (before * below).astype(bf16)
    slope = below + before * density
    dg = dot(dz, second, NN) + dot(dlow4, down2_ref[...], NT)
    df = (dg * slope).astype(bf16)
    z_part = dot(g, second, NT)
    da_part = dot(df, first, NT)
    low4_part = dot(g, down2_ref[...], NN)
    dlow3_part = dot(df, up1_ref[...], NN)

    @pl.when(tile == 0)
    def _():
        z_s[image] = z_part
        da_s[image] = da_part
        low4_s[image] = low4_part
        dlow3_s[image] = dlow3_part

    @pl.when(tile > 0)
    def _():
        z_s[image] += z_part
        da_s[image] += da_part
        low4_s[image] += low4_part
        dlow3_s[image] += dlow3_part

    add_to(grad_down2_ref, dot(dlow4, g, TN).T, image == 0)
    add_to(grad_up1_ref, dot(low3, df, TN).T, image == 0)

    @pl.when(last)
    def _():
        low4 = keep(low4_s[image], adapter)
        h = h_ref[image]
        z = z_s[image] + dot(low4, up2_ref[...], NT) + bias2_ref[...]
        out_ref[...] = (h + mask * z).astype(bf16)
        add_to(grad_up2_ref, dot(low4, dz, TN).T, image == 0)
        dlow3 = keep(dlow3_s[image], adapter)
        da = da_s[image] + dot(dlow3, down1_ref[...], NT)
        add_to(grad_down1_ref, dot(dlow3, a, TN).T, image == 0)
        normed, inverse = normalize(h)
        dh_ref[...] = cot_ref[image].astype(f32) + norm_back(
            da, normed, inverse, gain_ref[...]
        )


def mlp(h, cot, first, second, down1, up1, down2, up2, index, filled, bias1, bias2, gain, shift):
    images = h.shape[0]
    members, groups, rows, columns = first.shape
    tiles = FF // TILE
    per_group = columns // TILE
    sq = pl.Squeezed()
    weight = pl.BlockSpec(
        (members, sq, rows, TILE), lambda j, i: (0, j // per_group, 0, j % per_group)
    )
    tall = pl.BlockSpec((TILE, STACK), lambda j, i: (j, 0))
    short = pl.BlockSpec((D, STACK), lambda j, i: (0, 0))
    late = pl.BlockSpec((sq, SEQ, D), lambda j, i: (jnp.where(j == tiles - 1, i, 0), 0, 0))
    return pl.pallas_call(
        mlp_kernel,
        grid=(tiles, images),
        in_specs=[
            smem(),
            smem(),
            whole((images, SEQ, D)),
            whole((images, SEQ, D)),
            weight,
            weight,
            whole((D, STACK)),
            tall,
            tall,
            whole((D, STACK)),
            pl.BlockSpec((1, TILE), lambda j, i: (0, j)),
            whole((1, D)),
            whole((1, D)),
            whole((1, D)),
        ],
        out_specs=[late, late, short, tall, tall, short],
        out_shape=[
            jax.ShapeDtypeStruct((images, SEQ, D), bf16),
            jax.ShapeDtypeStruct((images, SEQ, D), f32),
            jax.ShapeDtypeStruct((D, STACK), f32),
            jax.ShapeDtypeStruct((FF, STACK), f32),
            jax.ShapeDtypeStruct((FF, STACK), f32),
            jax.ShapeDtypeStruct((D, STACK), f32),
        ],
        scratch_shapes=[
            pltpu.VMEM((images, SEQ, D), bf16),
            pltpu.VMEM((images, SEQ, D), bf16),
            pltpu.VMEM((images, SEQ, STACK), bf16),
            pltpu.VMEM((images, SEQ, STACK), bf16),
            pltpu.VMEM((images, SEQ, D), f32),
            pltpu.VMEM((images, SEQ, D), f32),
            pltpu.VMEM((images, SEQ, STACK), f32),
            pltpu.VMEM((images, SEQ, STACK), f32),
        ],
        compiler_params=params(),
        cost_estimate=cost(8 * images * SEQ * D * FF, 40 << 20, 2 * images * SEQ * FF),
        name="mlp",
    )(index, filled, h, cot, first, second, down1, up1, down2, up2, bias1, bias2, gain, shift)


def qkv_back_kernel(
    index_ref, tokens_ref, dh_ref, dq_ref, dk_ref, dv_ref, low_ref, weight_ref, down_ref, up_ref,
    gain_ref, shift_ref, grad_ref, grad_up_ref, grad_down_ref,
):
    image = pl.program_id(0)
    normed, inverse = normalize(tokens_ref[...].astype(f32))
    gain = gain_ref[...]
    a = (normed * gain + shift_ref[...]).astype(bf16)
    parts = (dq_ref[...], dk_ref[...], dv_ref[...])
    low_grad = dot(parts[0], up_ref[0:D, :], NN)
    for part in (1, 2):
        low_grad += dot(parts[part], up_ref[part * D : (part + 1) * D, :], NN)
    low_grad = keep(low_grad, index_ref[image])
    da = dot(low_grad, down_ref[...], NT)
    width = weight_ref.shape[-1] // 3
    for group in range(weight_ref.shape[1]):
        weight = flat(weight_ref[:, group])
        for part in range(3):
            da += dot(
                parts[part][:, group * width : (group + 1) * width],
                weight[:, part * width : (part + 1) * width],
                NT,
            )
    low = low_ref[...]
    for part in range(3):
        add_to(
            grad_up_ref.at[part * D : (part + 1) * D, :],
            dot(low, parts[part], TN).T,
            image == 0,
        )
    add_to(grad_down_ref, dot(low_grad, a, TN).T, image == 0)
    grad_ref[...] = dh_ref[...] + norm_back(da, normed, inverse, gain)


def qkv_back(tokens, dh, dq, dk, dv, low, weights, down, up, index, gain, shift):
    images = tokens.shape[0]
    members, groups, rows, columns = weights.shape
    return pl.pallas_call(
        qkv_back_kernel,
        grid=(images,),
        in_specs=[
            smem(),
            image_rows(),
            image_rows(),
            image_rows(),
            image_rows(),
            image_rows(),
            image_rows(STACK),
            whole((members, groups, rows, columns)),
            whole((D, STACK)),
            whole((3 * D, STACK)),
            whole((1, D)),
            whole((1, D)),
        ],
        out_specs=[
            image_rows(),
            pl.BlockSpec((3 * D, STACK), lambda i: (0, 0)),
            pl.BlockSpec((D, STACK), lambda i: (0, 0)),
        ],
        out_shape=[
            jax.ShapeDtypeStruct((images, SEQ, D), f32),
            jax.ShapeDtypeStruct((3 * D, STACK), f32),
            jax.ShapeDtypeStruct((D, STACK), f32),
        ],
        compiler_params=params(),
        cost_estimate=cost(6 * images * SEQ * D * D, 28 << 20),
        name="qkv_back",
    )(index, tokens, dh, dq, dk, dv, low, weights, down, up, gain, shift)


def on_device(
    tokens,
    cotangent,
    adapter_index,
    filled,
    ln1_gain,
    ln1_shift,
    qkv_weight,
    qv_bias,
    out_weight,
    out_bias,
    ln2_gain,
    ln2_shift,
    fc1_weight,
    fc1_bias,
    fc2_weight,
    fc2_bias,
    qkv_down,
    qkv_up,
    out_down,
    out_up,
    fc1_down,
    fc1_up,
    fc2_down,
    fc2_up,
):
    images = tokens.shape[0]
    own_start = lax.axis_index("tensor") * images
    index = lax.dynamic_slice_in_dim(adapter_index, own_start, images, 0)
    mask = lax.dynamic_slice_in_dim(filled, own_start, images, 0)
    stack_list = (qkv_down, qkv_up, out_down, out_up, fc1_down, fc1_up, fc2_down, fc2_up)
    widths = [stacked.shape[2] for stacked in stack_list]
    spans = []
    offset = 0
    for width in widths:
        spans.append(slice(offset, offset + width))
        offset += width
    packed = jnp.concatenate([stacked.reshape(STACK, -1) for stacked in stack_list], axis=1).T
    rows = qkv_weight.shape[0]
    column = qkv_weight.shape[2]
    hidden = fc1_weight.shape[1]
    packed = lax.all_gather(packed, BOTH, axis=0)
    gather = lambda shard: lax.all_gather(shard, BOTH, axis=0).reshape(
        D // rows, D // column, rows, -1
    )
    qkv_all = gather(qkv_weight.reshape(rows, 3 * column))
    rest = gather(jnp.concatenate([out_weight.T, fc1_weight, fc2_weight.T], axis=1))
    out_all = rest[..., :column]
    first_all = rest[..., column : column + hidden]
    second_all = rest[..., column + hidden :]
    full = [packed[:, span, :].reshape(-1, STACK) for span in spans]
    row = lambda vector: vector.astype(f32)[None, :]
    q, k, v, low_one = qkv_project(
        tokens, qkv_all, full[0], full[1], index, qv_bias, row(ln1_gain), row(ln1_shift)
    )
    o, prob = attend(q, k, v)
    h, low_out = out_project(tokens, o, out_all, full[2], full[3], index, mask, row(out_bias))
    outputs, dh, grad_up2, grad_down2, grad_up1, grad_down1 = mlp(
        h, cotangent, first_all, second_all, full[4], full[5], full[6], full[7], index, mask,
        row(fc1_bias), row(fc2_bias), row(ln2_gain), row(ln2_shift),
    )
    do, grad_out_up, grad_out_down = out_back(
        dh, o, low_out, out_all, full[2], full[3], index, mask
    )
    dq, dk, dv = attend_back(q, k, v, do, prob)
    input_grad, grad_qkv_up, grad_qkv_down = qkv_back(
        tokens, dh, dq, dk, dv, low_one, qkv_all, full[0], full[1], index,
        row(ln1_gain), row(ln1_shift),
    )
    terms = (
        grad_qkv_down, grad_qkv_up, grad_out_down, grad_out_up,
        grad_down1, grad_up1, grad_down2, grad_up2,
    )
    members = packed.shape[0]
    summed = lax.psum_scatter(
        jnp.concatenate([term.reshape(members, -1, STACK) for term in terms], axis=1),
        BOTH,
        scatter_dimension=0,
        tiled=False,
    ).T
    grads = [summed[:, span].reshape(ADAPTERS, RANK, -1) for span in spans]
    return (outputs, input_grad, *grads)


def solution(mesh):
    images = P(BOTH, None, None)
    stacked = P(None, None, BOTH)
    in_specs = (
        images, images, P("fsdp"), P("fsdp"), P(), P(), P("fsdp", None, "tensor"), P(),
        P("tensor", "fsdp"), P(), P(), P(), P("fsdp", "tensor"), P(), P("tensor", "fsdp"), P(),
    ) + (stacked,) * 8
    out_specs = (images, images) + (stacked,) * 8
    return jax.shard_map(
        on_device, mesh=mesh, in_specs=in_specs, out_specs=out_specs, check_vma=False
    )
```

time: 1090 us -> 668 us (0.61)
  matrix products: 375 us -> 0 us
  Pallas kernels: 0 us -> 244 us
  local copies, waits for them, and re-layouts: 258 us -> 70.1 us
  other arithmetic: 128 us -> 10.8 us
  waiting for transfers between devices: 306 us -> 320 us
    dot_general x62 -> x0, matrix products: 375 us -> none  [the longest x8 33.6 us: up_map(): jnp.einsum('isr,irw->isw', low_rank, chosen, preferred_element_type=jnp.f...]
    pallas_call x0 -> x7, Pallas kernels: none -> 244 us  [the longest x1 94.3 us: mlp(): pl.pallas_call(mlp_kernel, grid=(tiles, images), in_specs=[smem(), smem()...]
    convert_element_type x13 -> x0, other arithmetic: 87.4 us -> none  [the longest x1 45.8 us: on_device(): activated = activated.astype(jnp.bfloat16)]
    transpose x8 -> x0, local copies, waits for them, and re-layouts: 82 us -> none  [the longest x1 24.9 us: on_device(): weights[:, :, 4 * column:4 * column + group].transpose(1, 0, 2)]
    reshape x19 -> x0, local copies, waits for them, and re-layouts: 56.1 us -> none  [the longest x12 27.8 us: on_device(): term.reshape(ADAPTERS, RANK, members, width).transpose(2, 0, 1, 3)]
    reduce_scatter x1, waiting for transfers between devices: 93.4 us -> 135 us  [on_device(): lax.psum_scatter(jnp.concatenate([term.reshape(members, -1, STACK) for te...]
    all_gather x3, waiting for transfers between devices: 212 us -> 185 us  [the longest x2 136 us: on_device(): lax.all_gather(shard, BOTH, axis=0)]
    another operation x4 -> x1, local copies, waits for them, and re-layouts: 24.4 us -> 0.94 us  [on_device(): lax.all_gather(shard, BOTH, axis=0)]
  transfers between devices with their start and end apart: 4 -> 4, of which waited for: 3 -> 4; matrix products, arithmetic and copies ran while one was open for 11% -> 7% of each run, Pallas kernels for 0% -> 7%
where the time goes in v2:
time: 668 us; the launch traced here: 659 us
  waiting for transfers between devices  320 us (48%)
  Pallas kernels  244 us (37%)
  local copies, waits for them, and re-layouts  70.1 us (10%)
  between operations  14.3 us (2%)
  other arithmetic  10.8 us (2%)
    all_gather x2, waiting for transfers between devices, on_device(): lax.all_gather(shard, BOTH, axis=0)  136 us
    reduce_scatter x1, waiting for transfers between devices, on_device(): lax.psum_scatter(jnp.concatenate([term.reshape(members, -1, STACK) for te...  135 us
    pallas_call x1, Pallas kernels, mlp(): pl.pallas_call(mlp_kernel, grid=(tiles, images), in_specs=[smem(), smem()...  94.3 us
    pallas_call x1, Pallas kernels, attend_back(): pl.pallas_call(attend_back_kernel, grid=(images, HEADS // 2), in_specs=[p...  49.3 us
    all_gather x1, waiting for transfers between devices, on_device(): packed = lax.all_gather(packed, BOTH, axis=0)  49.1 us
    pallas_call x1, Pallas kernels, attend(): pl.pallas_call(attend_kernel, grid=(images, HEADS // 2), in_specs=[pair_r...  32.9 us
    pallas_call x1, Pallas kernels, qkv_back(): pl.pallas_call(qkv_back_kernel, grid=(images,), in_specs=[smem(), image_r...  30.7 us
    unnamed x32, local copies, waits for them, and re-layouts  28 us
  transfers between devices with their start and end apart: 4, of which 4 were waited for; matrix products, arithmetic and copies ran while one was open for 7% of the time, Pallas kernels for 7%

profile of v2, /device:TPU:0, one launch (start us, length us, event | category | flops | bytes accessed | tf_op | source)
XLA Modules:
  0.0 659.3 jit_solution(15634837889633465412)
XLA Ops:
  7.2 1.8 concatenate.9
  11.3 1.9 pad_maximum_fusion
  13.2 1.4 dynamic_slice.6.index_ref
  15.9 1.3 broadcast_in_dim.51
  21.0 1.3 broadcast_in_dim.57
  22.3 1.3 broadcast_in_dim.55
  23.5 1.3 broadcast_in_dim.54
  24.9 2.2 copy.68.tokens_ref
  27.0 2.1 copy.69.cot_ref
  29.1 49.1 %all-gather.8.cloned.1.call-done = bf16[16384,128]{0,1:T(8,128)(2,1)} async-done(((bf16[512,128]{0,1:T(8,128)(2,1)}), bf16[16384,128]{0,1:T(8,128)(2,1)}) %all-gather.8.cloned.1.call-update) | async-done | bytes 4194320 | tf_op jit(solution)/shard_map/all_gather | solution.py:559
  78.2 6.4 copy.66
  84.6 2.2 slice.77
  86.8 2.4 fusion.1
  89.2 1.5 fusion.2
  90.7 58.1 %all-gather.6.cloned.1.call-done = bf16[32,64,1536]{2,1,0:T(8,128)(2,1)} async-done(((bf16[1,64,1536]{2,1,0:T(8,128)(2,1)}), bf16[32,64,1536]{2,1,0:T(8,128)(2,1)}) %all-gather.6.cloned.1.call-update) | async-done | bytes 6291472 | tf_op jit(solution)/shard_map/all_gather | solution.py:560
  148.8 16.1 %qkv_project.1 = (bf16[2,577,1024]{2,1,0:T(8,128)(2,1)}, bf16[2,577,1024]{2,1,0:T(8,128)(2,1)}, bf16[2,577,1024]{2,1,0:T(8,128)(2,1)}, bf16[2,577,128]{2,1,0:T(8,128)(2,1)}) custom-call(s32[2]{0:T(128)} %dynamic_slice.6.index_ref, bf16[2,577,1024]{2,1,0:T(8,128)(2,1)} %copy.68.tokens_ref, bf16[16,2,64,1536]{3,2,1,0:T(8,128)(2,1)} %bitcast.104, ...), custom_call_target="tpu_custom_call" | custom-call | flops 7260340224 | bytes 20971520 | tf_op jit(solution)/shard_map/qkv_project/pallas_call | solution.py:127
  164.9 32.9 %attend.1 = (bf16[2,577,1024]{2,1,0:T(8,128)(2,1)}, bf16[32,577,577]{2,1,0:T(8,128)(2,1)}) custom-call(bf16[2,577,1024]{2,1,0:T(8,128)(2,1)} %get-tuple-element.33.q_ref, bf16[2,577,1024]{2,1,0:T(8,128)(2,1)} %get-tuple-element.34.k_ref, bf16[2,577,1024]{2,1,0:T(8,128)(2,1)} %get-tuple-element.35.v_ref), custom_call_target="tpu_custom_call" | custom-call | flops 10909417472 | bytes 41943040 | tf_op jit(solution)/shard_map/attend/pallas_call | solution.py:182
  197.8 77.7 %all-gather.10.cloned.1.call-done = bf16[2048,4608]{1,0:T(8,128)(2,1)} async-done(((bf16[64,4608]{1,0:T(8,128)(2,1)}), bf16[2048,4608]{1,0:T(8,128)(2,1)}) %all-gather.10.cloned.1.call-update) | async-done | bytes 18874384 | tf_op jit(solution)/shard_map/all_gather | solution.py:560
  275.5 3.1 slice.78.weight_ref
  278.6 12.0 %fusion = (bf16[16,2,64,2048]{3,2,1,0:T(8,128)(2,1)}, bf16[16,2,64,2048]{3,2,1,0:T(8,128)(2,1)}) fusion(bf16[16,2,64,4608]{3,2,1,0:T(8,128)(2,1)} %bitcast.49), kind=kLoop, calls=%fused_computation.9 | loop fusion | bytes 33554432 | tf_op jit(solution)/shard_map/slice | solution.py:567
  290.6 9.2 %out_project.1 = (f32[2,577,1024]{2,1,0:T(8,128)}, bf16[2,577,128]{2,1,0:T(8,128)(2,1)}) custom-call(s32[2]{0:T(128)} %dynamic_slice.6.index_ref, s32[2]{0:T(128)} %dynamic_slice.7.filled_ref, bf16[2,577,1024]{2,1,0:T(8,128)(2,1)} %copy.68.tokens_ref, bf16[2,577,1024]{2,1,0:T(8,128)(2,1)} %get-tuple-element.36.o_ref, ...), custom_call_target="tpu_custom_call" | custom-call | flops 2420113408 | bytes 12582912 | tf_op jit(solution)/shard_map/out_project/pallas_call | solution.py:252
  299.7 94.3 %mlp.1 = (bf16[2,577,1024]{2,1,0:T(8,128)(2,1)}, f32[2,577,1024]{2,1,0:T(8,128)}, f32[1024,128]{1,0:T(8,128)}, f32[4096,128]{1,0:T(8,128)}, f32[4096,128]{1,0:T(8,128)}, /*index=5*/f32[1024,128]{1,0:T(8,128)}) custom-call(s32[2]{0:T(128)} %dynamic_slice.6.index_ref, s32[2]{0:T(128)} %dynamic_slice.7.filled_ref, f32[2,577,1024]{2,1,0:T(8,128)} %get-tuple-element.37.h_ref, ...), custom_call_target="tpu_custom_call" | custom-call | flops 38721814528 | bytes 41943040 | tf_op jit(solution)/shard_map/mlp/pallas_call | solution.py:404
  394.1 11.5 %out_back.1 = (bf16[2,577,1024]{2,1,0:T(8,128)(2,1)}, f32[1024,128]{1,0:T(8,128)}, f32[1024,128]{1,0:T(8,128)}) custom-call(s32[2]{0:T(128)} %dynamic_slice.6.index_ref, s32[2]{0:T(128)} %dynamic_slice.7.filled_ref, f32[2,577,1024]{2,1,0:T(8,128)} %get-tuple-element.39.dh_ref, bf16[2,577,1024]{2,1,0:T(8,128)(2,1)} %get-tuple-element.36.o_ref, ...), custom_call_target="tpu_custom_call" | custom-call | flops 2420113408 | bytes 12582912 | tf_op jit(solution)/shard_map/out_back/pallas_call | solution.py:297
  405.6 49.3 %attend_back.1 = (bf16[2,577,1024]{2,1,0:T(8,128)(2,1)}, bf16[2,577,1024]{2,1,0:T(8,128)(2,1)}, bf16[2,577,1024]{2,1,0:T(8,128)(2,1)}) custom-call(bf16[2,577,1024]{2,1,0:T(8,128)(2,1)} %get-tuple-element.33.q_ref, bf16[2,577,1024]{2,1,0:T(8,128)(2,1)} %get-tuple-element.34.k_ref, bf16[2,577,1024]{2,1,0:T(8,128)(2,1)} %get-tuple-element.35.v_ref, ...), custom_call_target="tpu_custom_call" | custom-call | flops 21818834944 | bytes 50331648 | tf_op jit(solution)/shard_map/attend_back/pallas_call | solution.py:221
  454.9 30.7 %qkv_back.1 = (f32[2,577,1024]{2,1,0:T(8,128)}, f32[3072,128]{1,0:T(8,128)}, f32[1024,128]{1,0:T(8,128)}) custom-call(s32[2]{0:T(128)} %dynamic_slice.6.index_ref, bf16[2,577,1024]{2,1,0:T(8,128)(2,1)} %copy.68.tokens_ref, f32[2,577,1024]{2,1,0:T(8,128)} %get-tuple-element.39.dh_ref, bf16[2,577,1024]{2,1,0:T(8,128)(2,1)} %get-tuple-element.43.dq_ref, ...), custom_call_target="tpu_custom_call" | custom-call | flops 7260340224 | bytes 29360128 | tf_op jit(solution)/shard_map/qkv_back/pallas_call | solution.py:485
  485.7 2.0 constant_dynamic-update-slice_fusion.7
  487.7 2.9 constant_dynamic-update-slice_fusion.6
  493.2 1.5 constant_dynamic-update-slice_fusion.2
  494.6 1.5 constant_dynamic-update-slice_fusion.1
  497.0 8.3 %copy.80 = f32[2,577,1024]{2,0,1:T(2,128)} copy(f32[2,577,1024]{2,1,0:T(8,128)} %get-tuple-element.77) | data formatting | bytes 9453568
  505.4 3.8 copy.79
  509.2 134.8 %reduce-scatter.2.cloned.1.call-done = f32[1,512,128]{2,1,0:T(8,128)} async-done(((f32[32,512,128]{2,1,0:T(8,128)}), f32[1,512,128]{2,1,0:T(8,128)}) %reduce-scatter.2.cloned.1.call-update) | async-done | bytes 262160 | tf_op jit(solution)/shard_map/reduce_scatter | solution.py:592
  (49 shorter events, 19.1 us)
Async XLA Ops:
  7.2 17.7 %copy-start.2 = (bf16[2,577,1024]{2,0,1:T(2,128)(2,1)S(1)}, bf16[2,577,1024]{2,0,1:T(2,128)(2,1)}, u32[]{:S(2)}) copy-start(bf16[2,577,1024]{2,0,1:T(2,128)(2,1)} %param.24) | copy-start | bytes 7090180
  7.2 71.0 %all-gather.8.cloned.1.call-start = ((), (), s32[]{:S(2)}) async-start(), calls=%async_computation.3 | async-start | bytes 4325376 | tf_op jit(solution)/shard_map/all_gather | solution.py:559
  9.1 139.7 %all-gather.6.cloned.1.call-start = ((), (), s32[]{:S(2)}) async-start(), calls=%async_computation.1 | async-start | bytes 6488064 | tf_op jit(solution)/shard_map/all_gather | solution.py:560
  11.2 264.3 %all-gather.10.cloned.1.call-start = ((), (), s32[]{:S(2)}) async-start(), calls=%async_computation.4 | async-start | bytes 19464192 | tf_op jit(solution)/shard_map/all_gather | solution.py:560
  13.2 630.9 %reduce-scatter.2.cloned.1.call-start = ((), (), s32[]{:S(2)}) async-start(), calls=%async_computation.2 | async-start | bytes 8650752 | tf_op jit(solution)/shard_map/reduce_scatter | solution.py:592
  13.2 13.8 %copy-start.3 = (bf16[2,577,1024]{2,0,1:T(2,128)(2,1)S(1)}, bf16[2,577,1024]{2,0,1:T(2,128)(2,1)}, u32[]{:S(2)}) copy-start(bf16[2,577,1024]{2,0,1:T(2,128)(2,1)} %param.25) | copy-start | bytes 7090180
  84.6 4.6 copy-start
  454.9 35.7 %copy-start.9 = (f32[1024,128]{1,0:T(8,128)S(1)}, f32[1024,128]{1,0:T(8,128)}, u32[]{:S(2)}) copy-start(f32[1024,128]{1,0:T(8,128)} %get-tuple-element.50) | copy-start | bytes 1572868
  485.7 5.8 copy-start.8
  485.7 6.6 %copy-start.7 = (f32[1024,128]{1,0:T(8,128)S(1)}, f32[1024,128]{1,0:T(8,128)}, u32[]{:S(2)}) copy-start(f32[1024,128]{1,0:T(8,128)} %get-tuple-element.52) | copy-start | bytes 1572868
  485.7 7.5 %copy-start.5 = (f32[4096,128]{1,0:T(8,128)S(1)}, f32[4096,128]{1,0:T(8,128)}, u32[]{:S(2)}) copy-start(f32[4096,128]{1,0:T(8,128)} %get-tuple-element.53) | copy-start | bytes 6291460
  487.7 6.9 %copy-start.4 = (f32[4096,128]{1,0:T(8,128)S(1)}, f32[4096,128]{1,0:T(8,128)}, u32[]{:S(2)}) copy-start(f32[4096,128]{1,0:T(8,128)} %get-tuple-element.54) | copy-start | bytes 6291460
  492.3 3.8 copy-start.6
  497.0 8.4 %copy-start.1 = (bf16[2,577,1024]{2,1,0:T(8,128)(2,1)S(1)}, bf16[2,577,1024]{2,1,0:T(8,128)(2,1)}, u32[]{:S(2)}) copy-start(bf16[2,577,1024]{2,1,0:T(8,128)(2,1)} %get-tuple-element.76) | copy-start | bytes 7090180
Sparse Core Ops, SparseCore 0:
  11.5 66.6 all-gather.7
  81.1 67.6 all-gather.5
  152.3 123.1 all-gather.9
  497.1 146.8 reduce-scatter.1

commit v3 on v2

v3 whole, which is shorter than its diff:
```python
import math
from functools import partial

import jax
import jax.numpy as jnp
from jax import lax
from jax.experimental import pallas as pl
from jax.experimental.pallas import tpu as pltpu
from jax.sharding import PartitionSpec as P

D = 1024
HEADS = 16
HEAD_DIM = 64
FF = 4096
SEQ = 577
RANK = 16
ADAPTERS = 8
STACK = ADAPTERS * RANK
TILE = 512

epsilon = 1e-05
bf16 = jnp.bfloat16
f32 = jnp.float32
NN = (((1,), (0,)), ((), ()))
NT = (((1,), (1,)), ((), ()))
TN = (((0,), (0,)), ((), ()))
BOTH = ("fsdp", "tensor")


def dot(left, right, dims):
    return lax.dot_general(left, right, dims, preferred_element_type=f32)


def params():
    return pltpu.CompilerParams(vmem_limit_bytes=60 << 20)


def cost(flops, moved, exps=0):
    return pl.CostEstimate(flops=flops, bytes_accessed=moved, transcendentals=exps)


def smem():
    return pl.BlockSpec(memory_space=pltpu.SMEM)


def whole(shape):
    return pl.BlockSpec(shape, lambda *_: (0,) * len(shape), pipeline_mode=pl.Buffered(1))


def image_rows(width=D):
    return pl.BlockSpec((pl.Squeezed(), SEQ, width), lambda i: (i, 0, 0))


def normalize(values):
    center = values - jnp.mean(values, axis=-1, keepdims=True)
    inverse = lax.rsqrt(jnp.mean(center * center, axis=-1, keepdims=True) + epsilon)
    return center * inverse, inverse


def norm_back(upstream, normed, inverse, gain_row):
    scaled = upstream * gain_row
    return inverse * (
        scaled
        - jnp.mean(scaled, axis=-1, keepdims=True)
        - normed * jnp.mean(scaled * normed, axis=-1, keepdims=True)
    )


def chosen_lanes(adapter):
    lanes = lax.broadcasted_iota(jnp.int32, (1, STACK), 1)
    return (lanes // RANK) == adapter


def keep(product, adapter):
    return jnp.where(chosen_lanes(adapter), product, 0.0).astype(bf16)


def add_to(ref, value, first):
    @pl.when(first)
    def _():
        ref[...] = value

    @pl.when(jnp.logical_not(first))
    def _():
        ref[...] += value


def flat(block):
    return block.reshape(D, block.shape[-1])


def any_space():
    return pl.BlockSpec(memory_space=pl.ANY)


class Stream:
    def __init__(self, sources, lane, width, slots, sems):
        self.sources, self.lane, self.width = sources, lane, width
        self.slots, self.sems = slots, sems

    def copy(self, source, inner, slot):
        lanes = pl.ds(self.lane, self.width)
        return pltpu.make_async_copy(
            source.at[inner, :, :, lanes], self.slots.at[slot], self.sems.at[slot]
        )

    def start(self, group, slot):
        offset = 0
        for source in self.sources:
            count = source.shape[0]

            @pl.when(jnp.logical_and(group >= offset, group < offset + count))
            def _(source=source, offset=offset):
                self.copy(source, group - offset, slot).start()

            offset += count

    def start_all(self):
        group = 0
        for source in self.sources:
            for inner in range(source.shape[0]):
                self.copy(source, inner, group).start()
                group += 1

    def wait(self, slot):
        self.copy(self.sources[0], 0, slot).wait()


def qkv_kernel(count, *refs):
    table_ref, index_ref, tokens_ref = refs[:3]
    sources = refs[3 : 3 + count]
    down_ref, up_ref, bias_ref, gain_ref, shift_ref = refs[3 + count : 8 + count]
    q_ref, k_ref, v_ref, low_ref, a_s, low_s, slots, sems = refs[8 + count :]
    group = pl.program_id(0)
    image = pl.program_id(1)
    width = q_ref.shape[-1]
    stream = Stream(sources, 0, 3 * width, slots, sems)
    slot = group % 2

    @pl.when(jnp.logical_and(group == 0, image == 0))
    def _():
        stream.start(group, 0)

    @pl.when(group == 0)
    def _():
        normed, _ = normalize(tokens_ref[...].astype(f32))
        a = (normed * gain_ref[...] + shift_ref[...]).astype(bf16)
        a_s[image] = a
        low_s[image] = keep(dot(a, down_ref[...], NN), index_ref[image])

    @pl.when(image == 0)
    def _():
        stream.wait(slot)

        @pl.when(group + 1 < pl.num_programs(0))
        def _():
            stream.start(group + 1, 1 - slot)

    a = a_s[image]
    low = low_s[image]
    low_ref[...] = low
    weight = flat(slots[slot])
    start = pl.multiple_of(table_ref[group] * width, width)
    bias = bias_ref[...].astype(f32)
    for part, out_ref in enumerate((q_ref, k_ref, v_ref)):
        value = dot(a, weight[:, part * width : (part + 1) * width], NN)
        value += dot(low, up_ref[pl.ds(part * D + start, width), :], NT)
        if part != 1:
            value += bias[part // 2 : part // 2 + 1]
        out_ref[...] = value.astype(bf16)


def group_count(sources):
    return sum(source.shape[0] for source in sources)


def qkv_project(tokens, sources, table, down, up, index, bias, gain, shift):
    images = tokens.shape[0]
    members, rows = sources[0].shape[1:3]
    groups = group_count(sources)
    width = D // groups
    sq = pl.Squeezed()
    out = pl.BlockSpec((sq, SEQ, width), lambda g, i, t: (i, 0, t[g]))
    vector = whole((1, D))
    grid_spec = pltpu.PrefetchScalarGridSpec(
        num_scalar_prefetch=1,
        grid=(groups, images),
        in_specs=[smem(), pl.BlockSpec((sq, SEQ, D), lambda g, i, t: (i, 0, 0))]
        + [any_space()] * len(sources)
        + [
            whole((D, STACK)),
            whole((3 * D, STACK)),
            pl.BlockSpec((2, width), lambda g, i, t: (0, t[g])),
            vector,
            vector,
        ],
        out_specs=[out, out, out, pl.BlockSpec((sq, SEQ, STACK), lambda g, i, t: (i, 0, 0))],
        scratch_shapes=[
            pltpu.VMEM((images, SEQ, D), bf16),
            pltpu.VMEM((images, SEQ, STACK), bf16),
            pltpu.VMEM((2, members, rows, 3 * width), bf16),
            pltpu.SemaphoreType.DMA((2,)),
        ],
    )
    return pl.pallas_call(
        partial(qkv_kernel, len(sources)),
        grid_spec=grid_spec,
        out_shape=[jax.ShapeDtypeStruct((images, SEQ, D), bf16)] * 3
        + [jax.ShapeDtypeStruct((images, SEQ, STACK), bf16)],
        compiler_params=params(),
        cost_estimate=cost(6 * images * SEQ * D * D, 20 << 20),
        name="qkv_project",
    )(table, index, tokens, *sources, down, up, bias, gain, shift)


def attend_kernel(q_ref, k_ref, v_ref, o_ref, w_ref):
    q = q_ref[...]
    k = k_ref[...]
    v = v_ref[...]
    low = lax.broadcasted_iota(jnp.int32, q.shape, 1) < HEAD_DIM
    outs = []
    for head in range(2):
        own = low if head == 0 else jnp.logical_not(low)
        queries = jnp.where(own, q * HEAD_DIM**-0.5, jnp.zeros_like(q)).astype(bf16)
        scores = dot(queries, k, NT)
        top = jnp.max(scores, axis=-1, keepdims=True)
        raised = jnp.exp(scores - top)
        total = jnp.sum(raised, axis=-1, keepdims=True)
        prob = (raised * (1.0 / total)).astype(bf16)
        w_ref[head] = prob
        outs.append(dot(prob, v, NN))
    o_ref[...] = jnp.where(low, outs[0], outs[1]).astype(bf16)


def pair_rows(image):
    return pl.BlockSpec((pl.Squeezed(), SEQ, 2 * HEAD_DIM), lambda h: (image, 0, h))


def pair_weights(image):
    return pl.BlockSpec((2, SEQ, SEQ), lambda h: (image * (HEADS // 2) + h, 0, 0))


def into(kernel, inputs):
    def body(*refs):
        kernel(*refs[:inputs], *refs[len(refs) - (len(refs) - inputs) // 2 :])

    return body


def per_image(kernel, name, image, inputs, in_specs, outs, out_specs, filled, flops, moved, exps):
    count = len(inputs)
    if filled is None:
        return pl.pallas_call(
            kernel, grid=(HEADS // 2,), in_specs=in_specs, out_specs=out_specs, out_shape=outs,
            compiler_params=params(), cost_estimate=cost(flops, moved, exps), name=name,
        )(*inputs)
    return pl.pallas_call(
        into(kernel, count), grid=(HEADS // 2,), in_specs=in_specs + [any_space()] * len(outs),
        out_specs=out_specs, out_shape=outs,
        input_output_aliases={count + n: n for n in range(len(outs))},
        compiler_params=params(), cost_estimate=cost(flops, moved, exps), name=name,
    )(*inputs, *filled)


def attend(q, k, v, image, filled):
    images = q.shape[0]
    outs = [
        jax.ShapeDtypeStruct((images, SEQ, D), bf16),
        jax.ShapeDtypeStruct((images * HEADS, SEQ, SEQ), bf16),
    ]
    return per_image(
        attend_kernel, "attend", image, (q, k, v), [pair_rows(image)] * 3, outs,
        [pair_rows(image), pair_weights(image)], filled,
        16 * SEQ * SEQ * D, 20 << 20, HEADS * SEQ * SEQ,
    )


def attend_back_kernel(q_ref, k_ref, v_ref, do_ref, w_ref, dq_ref, dk_ref, dv_ref):
    q = q_ref[...]
    k = k_ref[...]
    v = v_ref[...]
    do = do_ref[...]
    low = lax.broadcasted_iota(jnp.int32, q.shape, 1) < HEAD_DIM
    grads = []
    for head in range(2):
        own = low if head == 0 else jnp.logical_not(low)
        mixed_grad = jnp.where(own, do, jnp.zeros_like(do))
        prob_grad = dot(mixed_grad, v, NT)
        prob_low = w_ref[head]
        prob = prob_low.astype(f32)
        inner = jnp.sum(prob * prob_grad, axis=-1, keepdims=True)
        score_grad = (prob * (prob_grad - inner)).astype(bf16)
        grads.append((dot(score_grad, k, NN), dot(score_grad, q, TN), dot(prob_low, do, TN)))
    scale = HEAD_DIM**-0.5
    dq_ref[...] = (jnp.where(low, grads[0][0], grads[1][0]) * scale).astype(bf16)
    dk_ref[...] = (jnp.where(low, grads[0][1], grads[1][1]) * scale).astype(bf16)
    dv_ref[...] = jnp.where(low, grads[0][2], grads[1][2]).astype(bf16)


def attend_back(q, k, v, do, prob, image, filled):
    outs = [jax.ShapeDtypeStruct(q.shape, bf16)] * 3
    return per_image(
        attend_back_kernel, "attend_back", image, (q, k, v, do, prob),
        [pair_rows(image)] * 4 + [pair_weights(image)], outs, [pair_rows(image)] * 3, filled,
        32 * SEQ * SEQ * D, 24 << 20, 0,
    )


def out_kernel(count, lane, *refs):
    table_ref, index_ref, filled_ref, tokens_ref, o_ref = refs[:5]
    sources = refs[5 : 5 + count]
    down_ref, up_ref, bias_ref, h_ref, low_ref, slots, sems = refs[5 + count :]
    image = pl.program_id(0)
    groups = slots.shape[0]
    width = slots.shape[-1]
    stream = Stream(sources, lane, width, slots, sems)

    @pl.when(image == 0)
    def _():
        stream.start_all()

    low = keep(dot(o_ref[...], down_ref[...], NN), index_ref[image])
    low_ref[...] = low
    value = dot(low, up_ref[...], NT) + bias_ref[...]
    for group in range(groups):
        @pl.when(image == 0)
        def _(group=group):
            stream.wait(group)

        start = pl.multiple_of(table_ref[group] * width, width)
        value += dot(o_ref[:, pl.ds(start, width)], flat(slots[group]), NT)
    h_ref[...] = tokens_ref[...].astype(f32) + filled_ref[image].astype(f32) * value


def out_slots(sources):
    members, rows = sources[0].shape[1:3]
    groups = group_count(sources)
    return [
        pltpu.VMEM((groups, members, rows, D // groups), bf16),
        pltpu.SemaphoreType.DMA((groups,)),
    ]


def out_project(tokens, o, sources, lane, table, down, up, index, filled, bias):
    images = tokens.shape[0]
    return pl.pallas_call(
        partial(out_kernel, len(sources), lane),
        grid=(images,),
        in_specs=[smem(), smem(), smem(), image_rows(), image_rows()]
        + [any_space()] * len(sources)
        + [whole((D, STACK)), whole((D, STACK)), whole((1, D))],
        out_specs=[image_rows(), image_rows(STACK)],
        out_shape=[
            jax.ShapeDtypeStruct((images, SEQ, D), f32),
            jax.ShapeDtypeStruct((images, SEQ, STACK), bf16),
        ],
        scratch_shapes=out_slots(sources),
        compiler_params=params(),
        cost_estimate=cost(2 * images * SEQ * D * D, 12 << 20),
        name="out_project",
    )(table, index, filled, tokens, o, *sources, down, up, bias)


def out_back_kernel(count, lane, *refs):
    table_ref, index_ref, filled_ref, dh_ref, o_ref, low_ref = refs[:6]
    sources = refs[6 : 6 + count]
    down_ref, up_ref, do_ref, grad_up_ref, grad_down_ref = refs[6 + count : 11 + count]
    grad_up_s, grad_down_s, slots, sems = refs[11 + count :]
    image = pl.program_id(0)
    last = image == pl.num_programs(0) - 1
    width = slots.shape[-1]
    stream = Stream(sources, lane, width, slots, sems)

    @pl.when(image == 0)
    def _():
        stream.start_all()

    branch = (dh_ref[...] * filled_ref[image].astype(f32)).astype(bf16)
    low_grad = keep(dot(branch, up_ref[...], NN), index_ref[image])
    add_to(grad_up_s, dot(low_ref[...], branch, TN), image == 0)
    add_to(grad_down_s, dot(low_grad, o_ref[...], TN), image == 0)
    for group in range(slots.shape[0]):
        @pl.when(image == 0)
        def _(group=group):
            stream.wait(group)

        start = pl.multiple_of(table_ref[group] * width, width)
        value = dot(branch, flat(slots[group]), NN)
        value += dot(low_grad, down_ref[pl.ds(start, width), :], NT)
        do_ref[:, pl.ds(start, width)] = value.astype(bf16)

    @pl.when(last)
    def _():
        grad_up_ref[...] = grad_up_s[...].T.astype(bf16)
        grad_down_ref[...] = grad_down_s[...].T.astype(bf16)


def out_back(dh, o, low, sources, lane, table, down, up, index, filled):
    images = dh.shape[0]
    grad = pl.BlockSpec((D, STACK), lambda i: (0, 0))
    return pl.pallas_call(
        partial(out_back_kernel, len(sources), lane),
        grid=(images,),
        in_specs=[smem(), smem(), smem(), image_rows(), image_rows(), image_rows(STACK)]
        + [any_space()] * len(sources)
        + [whole((D, STACK)), whole((D, STACK))],
        out_specs=[image_rows(), grad, grad],
        out_shape=[jax.ShapeDtypeStruct((images, SEQ, D), bf16)]
        + [jax.ShapeDtypeStruct((D, STACK), bf16)] * 2,
        scratch_shapes=[pltpu.VMEM((STACK, D), f32)] * 2 + out_slots(sources),
        compiler_params=params(),
        cost_estimate=cost(2 * images * SEQ * D * D, 12 << 20),
        name="out_back",
    )(table, index, filled, dh, o, low, *sources, down, up)


def mlp_kernel(
    index_ref, filled_ref, h_ref, cot_ref, first_ref, second_ref, down1_ref, up1_ref, down2_ref,
    up2_ref, bias1_ref, bias2_ref, gain_ref, shift_ref,
    out_ref, dh_ref, grad_up2_ref, grad_down2_ref, grad_up1_ref, grad_down1_ref,
    a_s, dz_s, low3_s, dlow4_s, z_s, da_s, low4_s, dlow3_s,
    grad_up2_s, grad_down2_s, grad_up1_s, grad_down1_s,
):
    tile = pl.program_id(0)
    image = pl.program_id(1)
    last = tile == pl.num_programs(0) - 1
    final = image == pl.num_programs(1) - 1
    adapter = index_ref[image]
    mask = filled_ref[image].astype(f32)

    @pl.when(tile == 0)
    def _():
        normed, _ = normalize(h_ref[image])
        a = (normed * gain_ref[...] + shift_ref[...]).astype(bf16)
        a_s[image] = a
        dz = (cot_ref[image].astype(f32) * mask).astype(bf16)
        dz_s[image] = dz
        low3_s[image] = keep(dot(a, down1_ref[...], NN), adapter)
        dlow4_s[image] = keep(dot(dz, up2_ref[...], NN), adapter)

    a = a_s[image]
    dz = dz_s[image]
    low3 = low3_s[image]
    dlow4 = dlow4_s[image]
    first = flat(first_ref[...])
    second = flat(second_ref[...])
    before = dot(a, first, NN) + dot(low3, up1_ref[...], NT) + bias1_ref[...]
    density = jnp.exp(before * before * -0.5) * 0.3989422804014327
    below = 0.5 * lax.erf(before * 0.7071067811865476) + 0.5
    g = (before * below).astype(bf16)
    slope = below + before * density
    dg = dot(dz, second, NN) + dot(dlow4, down2_ref[...], NT)
    df = (dg * slope).astype(bf16)
    z_part = dot(g, second, NT)
    da_part = dot(df, first, NT)
    low4_part = dot(g, down2_ref[...], NN)
    dlow3_part = dot(df, up1_ref[...], NN)

    @pl.when(tile == 0)
    def _():
        z_s[image] = z_part
        da_s[image] = da_part
        low4_s[image] = low4_part
        dlow3_s[image] = dlow3_part

    @pl.when(tile > 0)
    def _():
        z_s[image] += z_part
        da_s[image] += da_part
        low4_s[image] += low4_part
        dlow3_s[image] += dlow3_part

    add_to(grad_down2_s, dot(dlow4, g, TN), image == 0)
    add_to(grad_up1_s, dot(low3, df, TN), image == 0)

    @pl.when(final)
    def _():
        grad_down2_ref[...] = grad_down2_s[...].T.astype(bf16)
        grad_up1_ref[...] = grad_up1_s[...].T.astype(bf16)

    @pl.when(last)
    def _():
        low4 = keep(low4_s[image], adapter)
        h = h_ref[image]
        z = z_s[image] + dot(low4, up2_ref[...], NT) + bias2_ref[...]
        out_ref[...] = (h + mask * z).astype(bf16)
        add_to(grad_up2_s, dot(low4, dz, TN), image == 0)
        dlow3 = keep(dlow3_s[image], adapter)
        da = da_s[image] + dot(dlow3, down1_ref[...], NT)
        add_to(grad_down1_s, dot(dlow3, a, TN), image == 0)
        normed, inverse = normalize(h)
        dh_ref[...] = cot_ref[image].astype(f32) + norm_back(
            da, normed, inverse, gain_ref[...]
        )

    @pl.when(jnp.logical_and(last, final))
    def _():
        grad_up2_ref[...] = grad_up2_s[...].T.astype(bf16)
        grad_down1_ref[...] = grad_down1_s[...].T.astype(bf16)


def mlp(h, cot, weights, down1, up1, down2, up2, index, filled, bias1, bias2, gain, shift):
    images = h.shape[0]
    members, groups, rows, _ = weights.shape
    hidden = FF // groups
    width = min(TILE, hidden)
    per_group = hidden // width
    tiles = FF // width
    sq = pl.Squeezed()

    def weight(base):
        return pl.BlockSpec(
            (members, sq, rows, width),
            lambda j, i: (0, j // per_group, 0, base * per_group + j % per_group),
        )

    tall = pl.BlockSpec((width, STACK), lambda j, i: (j, 0))
    short = pl.BlockSpec((D, STACK), lambda j, i: (0, 0))
    late = pl.BlockSpec((sq, SEQ, D), lambda j, i: (jnp.where(j == tiles - 1, i, 0), 0, 0))
    return pl.pallas_call(
        mlp_kernel,
        grid=(tiles, images),
        in_specs=[
            smem(),
            smem(),
            whole((images, SEQ, D)),
            whole((images, SEQ, D)),
            weight(0),
            weight(1),
            whole((D, STACK)),
            tall,
            tall,
            whole((D, STACK)),
            pl.BlockSpec((1, width), lambda j, i: (0, j)),
            whole((1, D)),
            whole((1, D)),
            whole((1, D)),
        ],
        out_specs=[late, late, short, tall, tall, short],
        out_shape=[
            jax.ShapeDtypeStruct((images, SEQ, D), bf16),
            jax.ShapeDtypeStruct((images, SEQ, D), f32),
            jax.ShapeDtypeStruct((D, STACK), bf16),
            jax.ShapeDtypeStruct((FF, STACK), bf16),
            jax.ShapeDtypeStruct((FF, STACK), bf16),
            jax.ShapeDtypeStruct((D, STACK), bf16),
        ],
        scratch_shapes=[
            pltpu.VMEM((images, SEQ, D), bf16),
            pltpu.VMEM((images, SEQ, D), bf16),
            pltpu.VMEM((images, SEQ, STACK), bf16),
            pltpu.VMEM((images, SEQ, STACK), bf16),
            pltpu.VMEM((images, SEQ, D), f32),
            pltpu.VMEM((images, SEQ, D), f32),
            pltpu.VMEM((images, SEQ, STACK), f32),
            pltpu.VMEM((images, SEQ, STACK), f32),
            pltpu.VMEM((STACK, D), f32),
            pltpu.VMEM((STACK, width), f32),
            pltpu.VMEM((STACK, width), f32),
            pltpu.VMEM((STACK, D), f32),
        ],
        compiler_params=params(),
        cost_estimate=cost(8 * images * SEQ * D * FF, 40 << 20, 2 * images * SEQ * FF),
        name="mlp",
    )(index, filled, h, cot, weights, weights, down1, up1, down2, up2, bias1, bias2, gain, shift)


def qkv_grads_kernel(
    index_ref, tokens_ref, dq_ref, dk_ref, dv_ref, low_ref, up_ref, gain_ref, shift_ref,
    low_grad_ref, grad_up_ref, grad_down_ref, grad_up_s, grad_down_s,
):
    image = pl.program_id(0)
    parts = (dq_ref, dk_ref, dv_ref)
    low = low_ref[...]
    low_grad = dot(parts[0][...], up_ref[0:D, :], NN)
    for part in (1, 2):
        low_grad += dot(parts[part][...], up_ref[part * D : (part + 1) * D, :], NN)
    low_grad = keep(low_grad, index_ref[image])
    low_grad_ref[...] = low_grad
    for part in range(3):
        add_to(grad_up_s.at[part], dot(low, parts[part][...], TN), image == 0)
    normed, _ = normalize(tokens_ref[...].astype(f32))
    a = (normed * gain_ref[...] + shift_ref[...]).astype(bf16)
    add_to(grad_down_s, dot(low_grad, a, TN), image == 0)

    @pl.when(image == pl.num_programs(0) - 1)
    def _():
        for part in range(3):
            grad_up_ref[part * D : (part + 1) * D, :] = grad_up_s[part].T.astype(bf16)
        grad_down_ref[...] = grad_down_s[...].T.astype(bf16)


def qkv_grads(tokens, dq, dk, dv, low, up, index, gain, shift):
    images = tokens.shape[0]
    return pl.pallas_call(
        qkv_grads_kernel,
        grid=(images,),
        in_specs=[smem()]
        + [image_rows()] * 4
        + [image_rows(STACK), whole((3 * D, STACK)), whole((1, D)), whole((1, D))],
        out_specs=[
            image_rows(STACK),
            pl.BlockSpec((3 * D, STACK), lambda i: (0, 0)),
            pl.BlockSpec((D, STACK), lambda i: (0, 0)),
        ],
        out_shape=[
            jax.ShapeDtypeStruct((images, SEQ, STACK), bf16),
            jax.ShapeDtypeStruct((3 * D, STACK), bf16),
            jax.ShapeDtypeStruct((D, STACK), bf16),
        ],
        scratch_shapes=[pltpu.VMEM((3, STACK, D), f32), pltpu.VMEM((STACK, D), f32)],
        compiler_params=params(),
        cost_estimate=cost(2 * images * SEQ * D * D, 12 << 20),
        name="qkv_grads",
    )(index, tokens, dq, dk, dv, low, up, gain, shift)


def qkv_back_kernel(count, *refs):
    table_ref, tokens_ref, dh_ref, dq_ref, dk_ref, dv_ref, low_grad_ref = refs[:7]
    sources = refs[7 : 7 + count]
    down_ref, gain_ref = refs[7 + count : 9 + count]
    grad_ref, slots, sems = refs[-3:]
    width = slots.shape[-1] // 3
    stream = Stream(sources, 0, 3 * width, slots, sems)
    stream.start_all()
    parts = (dq_ref, dk_ref, dv_ref)
    da = dot(low_grad_ref[...], down_ref[...], NT)
    normed, inverse = normalize(tokens_ref[...].astype(f32))
    for group in range(slots.shape[0]):
        stream.wait(group)
        start = pl.multiple_of(table_ref[group] * width, width)
        weight = flat(slots[group])
        for part in range(3):
            da += dot(
                parts[part][:, pl.ds(start, width)],
                weight[:, part * width : (part + 1) * width],
                NT,
            )
    grad_ref[...] = dh_ref[...] + norm_back(da, normed, inverse, gain_ref[...])


def qkv_back(tokens, dh, dq, dk, dv, low_grad, sources, table, down, gain, image, filled):
    images = tokens.shape[0]
    members, rows = sources[0].shape[1:3]
    groups = group_count(sources)
    at_image = lambda width=D: pl.BlockSpec((pl.Squeezed(), SEQ, width), lambda i: (image, 0, 0))
    extra = [] if filled is None else [filled]
    inputs = (table, tokens, dh, dq, dk, dv, low_grad, *sources, down, gain, *extra)
    return pl.pallas_call(
        partial(qkv_back_kernel, len(sources)),
        grid=(1,),
        in_specs=[smem()]
        + [at_image()] * 5
        + [at_image(STACK)]
        + [any_space()] * len(sources)
        + [whole((D, STACK)), whole((1, D))]
        + [any_space()] * len(extra),
        out_specs=at_image(),
        out_shape=jax.ShapeDtypeStruct((images, SEQ, D), f32),
        scratch_shapes=[
            pltpu.VMEM((groups, members, rows, 3 * D // groups), bf16),
            pltpu.SemaphoreType.DMA((groups,)),
        ],
        input_output_aliases={len(inputs) - 1: 0} if extra else {},
        compiler_params=params(),
        cost_estimate=cost(6 * SEQ * D * D, 18 << 20),
        name="qkv_back",
    )(*inputs)


STEPS = (16, 2, 2)


def along_x(array):
    return lax.ppermute(array, "fsdp", [(f, f ^ 1) for f in range(16)])


def along_y(array):
    return lax.ppermute(array, "fsdp", [(f, f ^ 2) for f in range(16)])


def along_z(array, shift):
    pairs = [(f, (f // 4 + shift) % 4 * 4 + f % 4) for f in range(16)]
    return lax.ppermute(array, "fsdp", pairs)


def other_core(array):
    return lax.ppermute(array, "tensor", [(0, 1), (1, 0)])


def positions():
    f = lax.axis_index("fsdp")
    t = lax.axis_index("tensor")
    z, y, x = f // 4, f // 2 % 2, f % 2
    places = [z, (z + 3) % 4, (z + 2) % 4, (z + 1) % 4, y, 1 - y, x, 1 - x, t, 1 - t]
    return jnp.stack(places).astype(jnp.int32)


def move(name, places, parts, outs, moves, room=None):
    room = room or (4 << 20) + sum(2 * math.prod(shape) for shape in outs)

    def kernel(places_ref, *refs):
        sems = refs[-1]
        copies = []
        for number, (part, out, source, target) in enumerate(moves):
            copies.append(
                pltpu.make_async_copy(
                    source(refs[part], places_ref),
                    target(refs[len(parts) + out], places_ref),
                    sems.at[number],
                )
            )
            copies[-1].start()
        for copy in copies:
            copy.wait()

    return pl.pallas_call(
        kernel,
        in_specs=[smem()] + [any_space()] * len(parts),
        out_specs=[pl.BlockSpec(memory_space=pltpu.VMEM)] * len(outs),
        out_shape=[jax.ShapeDtypeStruct(shape, bf16) for shape in outs],
        scratch_shapes=[pltpu.SemaphoreType.DMA((len(moves),))],
        compiler_params=pltpu.CompilerParams(vmem_limit_bytes=room),
        name=name,
    )(places, *parts)


def everything(ref, places):
    return ref


def after(value, *others):
    return lax.optimization_barrier((value, *others))[0]


class Piece:
    def __init__(self, shard, places, tag):
        self.shard, self.places, self.tag = shard, places, tag
        self.rows, self.half = shard.shape[0], shard.shape[1] // 2

    def send_z(self):
        self.parts = [self.shard] + [along_z(self.shard, shift) for shift in (1, 2, 3)]

    def wait_for(self, other):
        self.parts[0] = after(self.parts[0], other)

    def join_z(self):
        half = self.half
        self.a, self.b = move(
            "gather_z" + self.tag, self.places, self.parts, [(4, self.rows, half)] * 2,
            [
                (
                    shift, side,
                    lambda ref, p, side=side: ref.at[:, pl.ds(side * half, half)],
                    lambda ref, p, shift=shift: ref.at[p[shift]],
                )
                for shift in range(4)
                for side in range(2)
            ],
        )

    def send_half(self):
        self.parts = [self.a, along_y(self.a), self.b, along_x(self.b)]

    def join_half(self):
        self.a, self.b = move(
            "gather_yx" + self.tag, self.places, self.parts, [(4, 2, self.rows, self.half)] * 2,
            [
                (0, 0, everything, lambda ref, p: ref.at[:, p[4]]),
                (1, 0, everything, lambda ref, p: ref.at[:, p[5]]),
                (2, 1, everything, lambda ref, p: ref.at[:, p[6]]),
                (3, 1, everything, lambda ref, p: ref.at[:, p[7]]),
            ],
        )

    def send_rest(self):
        self.parts = [self.a, along_x(self.a), self.b, along_y(self.b)]

    def join_rest(self):
        (joined,) = move(
            "gather_xy" + self.tag, self.places, self.parts,
            [(2, 4, 2, 2, self.rows, self.half)],
            [
                (0, 0, everything, lambda ref, p: ref.at[0, :, :, p[6]]),
                (1, 0, everything, lambda ref, p: ref.at[0, :, :, p[7]]),
                (2, 0, everything, lambda ref, p: ref.at[1, :, p[4]]),
                (3, 0, everything, lambda ref, p: ref.at[1, :, p[5]]),
            ],
        )
        self.own = joined.reshape(2, 16, self.rows, self.half)
        self.sources = (self.own, other_core(self.own))


class SmallPiece(Piece):
    def join_z(self):
        (self.a,) = move(
            "gather_z" + self.tag, self.places, self.parts, [(4, self.rows, 2 * self.half)],
            [
                (shift, 0, everything, lambda ref, p, shift=shift: ref.at[p[shift]])
                for shift in range(4)
            ],
        )

    def send_layer(self):
        diagonal = lax.ppermute(self.a, "fsdp", [(f, f ^ 3) for f in range(16)])
        self.parts = [self.a, along_x(self.a), along_y(self.a), diagonal]

    def join_layer(self):
        half = self.half
        (joined,) = move(
            "gather_layer" + self.tag, self.places, self.parts,
            [(2, 4, 2, 2, self.rows, half)],
            [
                (
                    part, 0,
                    lambda ref, p, side=side: ref.at[:, :, pl.ds(side * half, half)],
                    lambda ref, p, side=side, y=y, x=x: ref.at[side, :, p[y], p[x]],
                )
                for part, (y, x) in enumerate(((4, 6), (4, 7), (5, 6), (5, 7)))
                for side in range(2)
            ],
        )
        self.own = joined.reshape(2, 16, self.rows, half)
        self.sources = (self.own, other_core(self.own))


def transposed(stacked):
    return stacked.reshape(STACK, -1).T


def halves(rows_by_lanes, pieces):
    rows = rows_by_lanes.shape[0]
    split = rows_by_lanes.reshape(rows, pieces, 2, -1)
    return [split[:, :, side].reshape(rows, -1) for side in range(2)]


class StepGather:
    def __init__(self, qkv_weight, out_weight, fc1_weight, fc2_weight, shards):
        rows, _, column = qkv_weight.shape
        qd, qu, od, ou, f1d, f1u, f2d, f2u = shards
        places = positions()
        t = lax.axis_index("tensor")
        qkv_a, qkv_b = halves(qkv_weight.reshape(rows, 3 * column), 3)
        out_a, out_b = halves(out_weight.T, 1)
        low1 = jnp.concatenate([qd, qu], axis=0)
        low2 = jnp.concatenate([od, ou], axis=0)
        low3 = jnp.concatenate([f1d, f2u], axis=0)
        self.piece1 = Piece(
            jnp.concatenate([qkv_a, low1[:64], qkv_b, low1[64:]], axis=1), places, "1"
        )
        self.piece2 = SmallPiece(jnp.concatenate([out_a, low2, out_b, low3], axis=1), places, "2")
        hidden = jnp.concatenate(
            [fc1_weight, fc2_weight.T, f1u[:64], f1u[64:], f2d[:64], f2d[64:]], axis=1
        )
        self.hidden = hidden
        self.places, self.column = places, column
        self.width = fc1_weight.shape[1]
        self.groups = jnp.stack([2 * t, 2 * t + 1, 2 - 2 * t, 3 - 2 * t]).astype(jnp.int32)
        self.lane = 0

    def first(self):
        one, two = self.piece1, self.piece2
        one.send_z()
        one.join_z()
        two.shard = after(two.shard, one.a)
        hidden = after(self.hidden, one.a)
        self.hidden = lax.all_gather(hidden, BOTH, axis=0).reshape(16, 2, *hidden.shape)
        one.send_half()
        one.join_half()
        one.send_rest()
        two.send_z()
        one.join_rest()
        lanes = pl.ds(3 * self.column // 2, STACK)
        qd, qu = move(
            "stacks1", self.places, one.sources, [(16, 2, 32, STACK), (16, 2, 96, STACK)],
            [
                m
                for source, core in ((0, 8), (1, 9))
                for m in (
                    (source, 0, lambda ref, p: ref.at[0, :, pl.ds(0, 32), lanes],
                     lambda ref, p, core=core: ref.at[:, p[core]]),
                    (source, 1, lambda ref, p: ref.at[0, :, pl.ds(32, 32), lanes],
                     lambda ref, p, core=core: ref.at[:, p[core], pl.ds(0, 32)]),
                    (source, 1, lambda ref, p: ref.at[1, :, :, lanes],
                     lambda ref, p, core=core: ref.at[:, p[core], pl.ds(32, 64)]),
                )
            ],
        )
        return one.sources, qd.reshape(-1, STACK), qu.reshape(-1, STACK)

    def after_qkv(self, q):
        two = self.piece2
        two.wait_for(q)
        two.join_z()
        two.send_layer()
        return after(q, two.a)

    def second(self, o):
        self.piece2.wait_for(o)
        self.piece2.join_layer()
        lanes = pl.ds(self.column // 2, STACK)
        stacks = move(
            "stacks2", self.places, self.piece2.sources, [(16, 2, 32, STACK)] * 4,
            [
                (source, out,
                 lambda ref, p, out=out: ref.at[out // 2, :, pl.ds(out % 2 * 32, 32), lanes],
                 lambda ref, p, core=core: ref.at[:, p[core]])
                for source, core in ((0, 8), (1, 9))
                for out in range(4)
            ],
        )
        od, ou, f1d, f2u = [stack.reshape(-1, STACK) for stack in stacks]
        self.stacks = (f1d, f2u)
        return self.piece2.sources, od, ou

    def third(self):
        base = 2 * self.width
        f1u, f2d = move(
            "stacks3", self.places, [self.hidden], [(16, 2, 128, STACK)] * 2,
            [
                (0, out,
                 lambda ref, p, out=out, side=side: ref.at[
                     :, :, :, pl.ds(base + (2 * out + side) * STACK, STACK)],
                 lambda ref, p, side=side: ref.at[:, :, pl.ds(side * 64, 64)])
                for out in range(2)
                for side in range(2)
            ],
            room=60 << 20,
        )
        f1d, f2u = self.stacks
        return self.hidden, (f1d, f1u.reshape(-1, STACK), f2d.reshape(-1, STACK), f2u)


class WholeGather:
    def __init__(self, qkv_weight, out_weight, fc1_weight, fc2_weight, shards):
        rows, _, column = qkv_weight.shape
        piece = jnp.concatenate(
            [fc1_weight, fc2_weight.T, qkv_weight.reshape(rows, 3 * column), out_weight.T],
            axis=1,
        )
        groups = lax.axis_size("tensor")
        self.joined = lax.all_gather(piece, BOTH, axis=0).reshape(-1, groups, *piece.shape)
        stacked = lax.all_gather(jnp.concatenate(shards, axis=0), BOTH, axis=0)
        self.full = []
        offset = 0
        for shard in shards:
            part = stacked[:, offset : offset + shard.shape[0]]
            self.full.append(part.reshape(-1, STACK))
            offset += shard.shape[0]
        start = 2 * fc1_weight.shape[1]
        by_group = self.joined[..., start:].transpose(1, 0, 2, 3)
        self.qkv, self.out = by_group[..., : 3 * column], by_group[..., 3 * column :]
        self.groups = jnp.arange(groups, dtype=jnp.int32)
        self.lane = 0

    def first(self):
        return (self.qkv,), self.full[0], self.full[1]

    def after_qkv(self, q):
        return q

    def second(self, o):
        return (self.out,), self.full[2], self.full[3]

    def third(self):
        return self.joined, self.full[4:]


def small_call(name, kernel, places, parts, outs):
    vmem = pl.BlockSpec(memory_space=pltpu.VMEM)
    return pl.pallas_call(
        kernel,
        in_specs=[smem()] + [vmem] * len(parts),
        out_specs=[vmem] * len(outs),
        out_shape=[jax.ShapeDtypeStruct(shape, dtype) for shape, dtype in outs],
        compiler_params=pltpu.CompilerParams(vmem_limit_bytes=24 << 20),
        name=name,
    )(places, *parts)


def add(*values):
    total = values[0].astype(f32)
    for value in values[1:]:
        total += value.astype(f32)
    return total


class StepScatter:
    def __init__(self, terms, tag):
        self.places, self.tag = positions(), tag
        self.widths = [term.shape[0] // 32 for term in terms]
        self.total = sum(self.widths)
        moves = []
        offset = 0
        for number, width in enumerate(self.widths):
            for out, core in enumerate((8, 9)):
                moves.append(
                    (number, out,
                     lambda ref, p, core=core: ref.at[:, :, :, p[core]],
                     lambda ref, p, offset=offset, width=width: ref.at[
                         :, :, :, pl.ds(offset, width)])
                )
            offset += width
        split = [
            term.reshape(4, 2, 2, 2, width, STACK) for term, width in zip(terms, self.widths)
        ]
        kept, sent = move(
            "scatter_core" + tag, self.places, split, [(4, 2, 2, self.total, STACK)] * 2, moves
        )
        self.parts = [kept, other_core(sent)]
        self.mark = kept

    def wait_for(self, other):
        self.parts[0] = after(self.parts[0], other)

    def layer(self):
        def kernel(p, kept, came, *outs):
            for out, y, x in zip(outs, (4, 4, 5, 5), (6, 7, 6, 7)):
                out[...] = add(kept[:, p[y], p[x]], came[:, p[y], p[x]]).astype(bf16)

        shape = ((4, self.total, STACK), bf16)
        own, to_x, to_y, to_both = small_call(
            "scatter_layer" + self.tag, kernel, self.places, self.parts, [shape] * 4
        )
        diagonal = lax.ppermute(to_both, "fsdp", [(f, f ^ 3) for f in range(16)])
        self.parts = [own, along_x(to_x), along_y(to_y), diagonal]
        self.mark = own

    def layers(self):
        def kernel(p, one, two, three, four, *outs):
            for shift, out in enumerate(outs):
                z = (p[0] + shift) % 4
                out[...] = add(one[z], two[z], three[z], four[z]).astype(out.dtype)

        own, *sends = small_call(
            "scatter_layers" + self.tag, kernel, self.places, self.parts,
            [((self.total, STACK), f32)] + [((self.total, STACK), bf16)] * 3,
        )
        self.parts = [own] + [along_z(send, shift + 1) for shift, send in enumerate(sends)]
        self.mark = own

    def finish(self):
        def kernel(p, own, first, second, third, *outs):
            value = add(own[...], first[...], second[...], third[...])
            offset = 0
            for width, out in zip(self.widths, outs):
                out[...] = value[offset : offset + width].T
                offset += width

        return small_call(
            "scatter_sum" + self.tag, kernel, self.places, self.parts,
            [((STACK, width), f32) for width in self.widths],
        )


class WholeScatter:
    def __init__(self, terms, tag):
        members = lax.axis_size(BOTH)
        packed = jnp.concatenate(
            [term.reshape(members, -1, STACK).astype(f32) for term in terms], axis=1
        )
        self.widths = [term.shape[0] // members for term in terms]
        self.summed = lax.psum_scatter(packed, BOTH, scatter_dimension=0, tiled=False)
        self.mark = terms[0]

    def wait_for(self, other):
        pass

    def layer(self):
        pass

    def layers(self):
        pass

    def finish(self):
        grads = []
        offset = 0
        for width in self.widths:
            grads.append(self.summed[offset : offset + width].T)
            offset += width
        return grads


def on_device(
    tokens,
    cotangent,
    adapter_index,
    filled,
    ln1_gain,
    ln1_shift,
    qkv_weight,
    qv_bias,
    out_weight,
    out_bias,
    ln2_gain,
    ln2_shift,
    fc1_weight,
    fc1_bias,
    fc2_weight,
    fc2_bias,
    qkv_down,
    qkv_up,
    out_down,
    out_up,
    fc1_down,
    fc1_up,
    fc2_down,
    fc2_up,
):
    images = tokens.shape[0]
    own_start = lax.axis_index("tensor") * images
    index = lax.dynamic_slice_in_dim(adapter_index, own_start, images, 0)
    mask = lax.dynamic_slice_in_dim(filled, own_start, images, 0)
    stack_list = (qkv_down, qkv_up, out_down, out_up, fc1_down, fc1_up, fc2_down, fc2_up)
    steps = (lax.axis_size("fsdp"), lax.axis_size("tensor"), images) == STEPS
    shards = [transposed(stacked) for stacked in stack_list]
    gather = (StepGather if steps else WholeGather)(
        qkv_weight, out_weight, fc1_weight, fc2_weight, shards
    )
    scatter = StepScatter if steps else WholeScatter
    groups = gather.groups
    row = lambda vector: vector.astype(f32)[None, :]
    qkv_sources, qkv_down_full, qkv_up_full = gather.first()
    q, k, v, low_one = qkv_project(
        tokens, qkv_sources, groups, qkv_down_full, qkv_up_full, index, qv_bias, row(ln1_gain),
        row(ln1_shift),
    )
    q = gather.after_qkv(q)
    mixed = None
    for image in range(images):
        mixed = attend(q, k, v, image, mixed)
    o, prob = mixed
    out_sources, out_down_full, out_up_full = gather.second(o)
    h, low_out = out_project(
        tokens, o, out_sources, gather.lane, groups, out_down_full, out_up_full, index, mask,
        row(out_bias),
    )
    mlp_weights, stacks = gather.third()
    outputs, dh, grad_up2, grad_down2, grad_up1, grad_down1 = mlp(
        h, cotangent, mlp_weights, *stacks, index, mask,
        row(fc1_bias), row(fc2_bias), row(ln2_gain), row(ln2_shift),
    )
    do, grad_out_up, grad_out_down = out_back(
        dh, o, low_out, out_sources, gather.lane, groups, out_down_full, out_up_full, index, mask
    )
    early = scatter(
        [grad_out_down, grad_out_up, grad_down1, grad_up1, grad_down2, grad_up2], "1"
    )
    do = after(do, early.mark)
    grads = None
    for image in range(images):
        grads = attend_back(q, k, v, do, prob, image, grads)
        if image == 0:
            early.wait_for(grads[0])
            early.layer()
            grads = (after(grads[0], early.mark), *grads[1:])
    dq, dk, dv = grads
    early.wait_for(dq)
    early.layers()
    dq = after(dq, early.mark)
    low_grad, grad_qkv_up, grad_qkv_down = qkv_grads(
        tokens, dq, dk, dv, low_one, qkv_up_full, index, row(ln1_gain), row(ln1_shift)
    )
    late = scatter([grad_qkv_down, grad_qkv_up], "2")
    low_grad = after(low_grad, late.mark)
    input_grad = None
    for image in range(images):
        input_grad = qkv_back(
            tokens, dh, dq, dk, dv, low_grad, qkv_sources, groups, qkv_down_full,
            row(ln1_gain), image, input_grad,
        )
        if image == 0:
            late.wait_for(input_grad)
            late.layer()
            input_grad = after(input_grad, late.mark)
    late.layers()
    grads = [grad.reshape(ADAPTERS, RANK, -1) for grad in (*late.finish(), *early.finish())]
    return (outputs, input_grad, *grads)


def solution(mesh):
    images = P(BOTH, None, None)
    stacked = P(None, None, BOTH)
    in_specs = (
        images, images, P("fsdp"), P("fsdp"), P(), P(), P("fsdp", None, "tensor"), P(),
        P("tensor", "fsdp"), P(), P(), P(), P("fsdp", "tensor"), P(), P("tensor", "fsdp"), P(),
    ) + (stacked,) * 8
    out_specs = (images, images) + (stacked,) * 8
    return jax.shard_map(
        on_device, mesh=mesh, in_specs=in_specs, out_specs=out_specs, check_vma=False
    )
```

time: 668 us -> 442 us (0.66)
  waiting for transfers between devices: 320 us -> 58.7 us
  starting transfers between devices: 0.16 us -> 45.5 us
  Pallas kernels: 244 us -> 282 us
  local copies, waits for them, and re-layouts: 70.1 us -> 32.3 us
    all_gather x3 -> x1, waiting for transfers between devices: 185 us -> 9.98 us  [first(): lax.all_gather(hidden, BOTH, axis=0).reshape(16, 2, *hidden.shape)]
    reduce_scatter x1 -> x0, waiting for transfers between devices: 135 us -> none  [on_device(): lax.psum_scatter(jnp.concatenate([term.reshape(members, -1, STACK) for te...]
    ppermute x0 -> x29, waiting for transfers between devices: none -> 48.7 us  [the longest x5 25.7 us: along_x(): return lax.ppermute(array, 'fsdp', [(f, f ^ 1) for f in range(16)])]
    ppermute x0 -> x29, starting transfers between devices: none -> 45.5 us  [the longest x12 29.2 us: along_z(): return lax.ppermute(array, 'fsdp', pairs)]
    pallas_call x6 -> x26, Pallas kernels: 150 us -> 189 us  [the longest x2 43.2 us: per_image(): pl.pallas_call(kernel, grid=(HEADS // 2,), in_specs=in_specs, out_specs=o...]
    slice x16 -> x3, local copies, waits for them, and re-layouts: 29.5 us -> 0.37 us  [the longest x2 0.37 us: halves(): return [split[:, :, side].reshape(rows, -1) for side in range(2)]]
    unnamed x32 -> x93, local copies, waits for them, and re-layouts: 28 us -> 28 us
  transfers between devices with their start and end apart: 4 -> 30, of which waited for: 4 -> 7; matrix products, arithmetic and copies ran while one was open for 7% -> 6% of each run, Pallas kernels for 7% -> 34%
where the time goes in v3:
time: 442 us; the launch traced here: 438 us
  Pallas kernels  282 us (64%)
  waiting for transfers between devices  58.7 us (13%)
  starting transfers between devices  45.5 us (10%)
  local copies, waits for them, and re-layouts  32.3 us (7%)
  between operations  15.2 us (3%)
  other arithmetic  4.84 us (1%)
    pallas_call x1, Pallas kernels, mlp(): pl.pallas_call(mlp_kernel, grid=(tiles, images), in_specs=[smem(), smem()...  92.6 us
    pallas_call x2, Pallas kernels, per_image(): pl.pallas_call(kernel, grid=(HEADS // 2,), in_specs=in_specs, out_specs=o...  43.2 us
    pallas_call x2, Pallas kernels, per_image(): pl.pallas_call(into(kernel, count), grid=(HEADS // 2,), in_specs=in_specs...  43.1 us
    ppermute x12, starting transfers between devices, along_z(): return lax.ppermute(array, 'fsdp', pairs)  29.2 us
    unnamed x93, local copies, waits for them, and re-layouts  28 us
    ppermute x5, waiting for transfers between devices, along_x(): return lax.ppermute(array, 'fsdp', [(f, f ^ 1) for f in range(16)])  25.7 us
    pallas_call x2, Pallas kernels, qkv_back(): pl.pallas_call(partial(qkv_back_kernel, len(sources)), grid=(1,), in_spec...  22.9 us
    pallas_call x1, Pallas kernels, qkv_project(): pl.pallas_call(partial(qkv_kernel, len(sources)), grid_spec=grid_spec, ou...  18.1 us
  transfers between devices with their start and end apart: 30, of which 7 were waited for; matrix products, arithmetic and copies ran while one was open for 6% of the time, Pallas kernels for 34%

profile of v3, /device:TPU:0, one launch (start us, length us, event | category | flops | bytes accessed | tf_op | source)
XLA Modules:
  0.0 438.3 jit_solution(10734252342284792579)
XLA Ops:
  9.9 3.1 collective-permute-start
  13.0 2.6 collective-permute-start.1
  17.5 4.1 collective-permute-done.refs_1_
  21.6 9.0 %collective-permute-done.1.refs_2_ = bf16[64,1792]{1,0:T(8,128)(2,1)S(1)} collective-permute-done((bf16[64,1792]{1,0:T(8,128)(2,1)S(1)}, bf16[64,1792]{1,0:T(8,128)(2,1)S(1)}, u32[]{:S(2)}, u32[]{:S(2)}) %collective-permute-start.1) | collective-permute-done | bytes 229408 | tf_op jit(solution)/shard_map/ppermute | solution.py:684
  34.5 9.3 %collective-permute-done.3.refs_1_ = bf16[4,64,896]{2,1,0:T(8,128)(2,1)S(1)} collective-permute-done((bf16[4,64,896]{2,1,0:T(8,128)(2,1)S(1)}, bf16[4,64,896]{2,1,0:T(8,128)(2,1)S(1)}, u32[]{:S(2)}, u32[]{:S(2)}) %collective-permute-start.3) | collective-permute-done | bytes 458784 | tf_op jit(solution)/shard_map/ppermute | solution.py:679
  48.1 24.4 %collective-permute-done.5.refs_1_ = bf16[4,2,64,896]{3,2,1,0:T(8,128)(2,1)S(1)} collective-permute-done((bf16[4,2,64,896]{3,2,1,0:T(8,128)(2,1)S(1)}, bf16[4,2,64,896]{3,2,1,0:T(8,128)(2,1)S(1)}, u32[]{:S(2)}, u32[]{:S(2)}) %collective-permute-start.5) | collective-permute-done | bytes 917536 | tf_op jit(solution)/shard_map/ppermute | solution.py:675
  73.0 2.8 gather_xy1.1
  76.0 2.2 copy.69.refs_2_.refs_3_.tokens_ref.refs_1_
  81.1 4.7 %collective-permute-start.10 = (bf16[64,768]{1,0:T(8,128)(2,1)S(1)}, bf16[64,768]{1,0:T(8,128)(2,1)S(1)}, u32[]{:S(2)}, u32[]{:S(2)}) collective-permute-start(bf16[64,768]{1,0:T(8,128)(2,1)S(1)} %maximum_maximum_fusion.refs_0_), channel_id=1, source_target_pairs={{0,24},{2,26},{4,28},{6,30},{8,0},{10,2},{12,4},{14,6},{16,8},{18,... | collective-permute-start | bytes 294920 | tf_op jit(solution)/shard_map/ppermute | solution.py:684
  85.8 6.8 %collective-permute-start.8 = (bf16[64,768]{1,0:T(8,128)(2,1)S(1)}, bf16[64,768]{1,0:T(8,128)(2,1)S(1)}, u32[]{:S(2)}, u32[]{:S(2)}) collective-permute-start(bf16[64,768]{1,0:T(8,128)(2,1)S(1)} %maximum_maximum_fusion.refs_0_), channel_id=1, source_target_pairs={{0,8},{2,10},{4,12},{6,14},{8,16},{10,18},{12,20},{14,22},{16,24},... | collective-permute-start | bytes 294920 | tf_op jit(solution)/shard_map/ppermute | solution.py:684
  94.0 1.9 stacks1.1
  97.6 18.1 %qkv_project.1 = (bf16[2,577,1024]{2,1,0:T(8,128)(2,1)}, bf16[2,577,1024]{2,1,0:T(8,128)(2,1)}, bf16[2,577,1024]{2,1,0:T(8,128)(2,1)}, bf16[2,577,128]{2,1,0:T(8,128)(2,1)}) custom-call(s32[4]{0:T(128)} %pad_add_fusion.refs_0_, s32[2]{0:T(128)} %dynamic_slice.6.refs_1_.index_ref, bf16[2,577,1024]{2,1,0:T(8,128)(2,1)} %copy.69.refs_2_.refs_3_.tokens_ref.refs_1_, ...), custom_call_target="tpu_custom_call" | custom-call | flops 7260340224 | bytes 20971520 | tf_op jit(solution)/shard_map/qkv_project/pallas_call | solution.py:205
  117.0 3.4 collective-permute-start.13
  120.4 17.3 %attend.2 = (bf16[2,577,1024]{2,1,0:T(8,128)(2,1)}, bf16[32,577,577]{2,1,0:T(8,128)(2,1)}) custom-call(bf16[2,577,1024]{2,1,0:T(8,128)(2,1)} %get-tuple-element.100.q_ref.refs_0_, bf16[2,577,1024]{2,1,0:T(8,128)(2,1)} %get-tuple-element.101.k_ref.refs_1_, bf16[2,577,1024]{2,1,0:T(8,128)(2,1)} %get-tuple-element.102.v_ref.refs_2_), custom_call_target="tpu_custom_call" | custom-call | flops 5454708736 | bytes 20971520 | tf_op jit(solution)/shard_map/attend/pallas_call | solution.py:253
  137.7 17.4 %attend.3 = (bf16[2,577,1024]{2,1,0:T(8,128)(2,1)}, bf16[32,577,577]{2,1,0:T(8,128)(2,1)}) custom-call(bf16[2,577,1024]{2,1,0:T(8,128)(2,1)} %get-tuple-element.100.q_ref.refs_0_, bf16[2,577,1024]{2,1,0:T(8,128)(2,1)} %get-tuple-element.101.k_ref.refs_1_, ...), custom_call_target="tpu_custom_call", output_to_operand_aliasing={{0}: (3, {}), {1}: (4, {})} | custom-call | flops 5454708736 | bytes 20971520 | tf_op jit(solution)/shard_map/attend/pallas_call | solution.py:257
  157.5 2.1 copy.72.cot_ref
  165.7 11.8 %out_project.1 = (f32[2,577,1024]{2,1,0:T(8,128)}, bf16[2,577,128]{2,1,0:T(8,128)(2,1)}) custom-call(s32[4]{0:T(128)} %pad_add_fusion.refs_0_, s32[2]{0:T(128)} %dynamic_slice.6.refs_1_.index_ref, s32[2]{0:T(128)} %dynamic_slice.7.refs_2_.filled_ref, bf16[2,577,1024]{2,1,0:T(8,128)(2,1)} %copy.69.refs_2_.refs_3_.tokens_ref.refs_1_, ...), custom_call_target="tpu_custom_call" | custom-call | flops 2420113408 | bytes 12582912 | tf_op jit(solution)/shard_map/out_project/pallas_call | solution.py:346
  177.5 10.0 %all-gather.3.cloned.1.call-done = bf16[2048,4608]{1,0:T(8,128)(2,1)} async-done(((bf16[64,4608]{1,0:T(8,128)(2,1)}), bf16[2048,4608]{1,0:T(8,128)(2,1)}) %all-gather.3.cloned.1.call-update) | async-done | bytes 18874384 | tf_op jit(solution)/shard_map/all_gather | solution.py:867
  187.5 3.7 stacks3.1
  191.2 92.6 %mlp.1 = (bf16[2,577,1024]{2,1,0:T(8,128)(2,1)}, f32[2,577,1024]{2,1,0:T(8,128)}, bf16[1024,128]{1,0:T(8,128)(2,1)}, bf16[4096,128]{1,0:T(8,128)(2,1)}, bf16[409...) custom-call(s32[2]{0:T(128)} %dynamic_slice.6.refs_1_.index_ref, s32[2]{0:T(128)} %dynamic_slice.7.refs_2_.filled_ref, ...), custom_call_target="tpu_custom_call" | custom-call | flops 38721814528 | bytes 41943040 | tf_op jit(solution)/shard_map/mlp/pallas_call | solution.py:520
  283.8 14.6 %out_back.1 = (bf16[2,577,1024]{2,1,0:T(8,128)(2,1)}, bf16[1024,128]{1,0:T(8,128)(2,1)}, bf16[1024,128]{1,0:T(8,128)(2,1)}) custom-call(s32[4]{0:T(128)} %pad_add_fusion.refs_0_, s32[2]{0:T(128)} %dynamic_slice.6.refs_1_.index_ref, s32[2]{0:T(128)} %dynamic_slice.7.refs_2_.filled_ref, f32[2,577,1024]{2,1,0:T(8,128)} %get-tuple-element.116.refs_3_.refs_2_, ...), custom_call_target="tpu_custom_call" | custom-call | flops 2420113408 | bytes 12582912 | tf_op jit(solution)/shard_map/out_back/pallas_call | solution.py:401
  301.3 2.1 scatter_core1.1
  303.8 25.9 %attend_back.2 = (bf16[2,577,1024]{2,1,0:T(8,128)(2,1)}, bf16[2,577,1024]{2,1,0:T(8,128)(2,1)}, bf16[2,577,1024]{2,1,0:T(8,128)(2,1)}) custom-call(bf16[2,577,1024]{2,1,0:T(8,128)(2,1)} %get-tuple-element.100.q_ref.refs_0_, bf16[2,577,1024]{2,1,0:T(8,128)(2,1)} %get-tuple-element.101.k_ref.refs_1_, bf16[2,577,1024]{2,1,0:T(8,128)(2,1)} %get-tuple-element.102.v_ref.refs_2_, ...), custom_call_target="tpu_custom_call" | custom-call | flops 10909417472 | bytes 25165824 | tf_op jit(solution)/shard_map/attend_back/pallas_call | solution.py:253
  334.9 25.7 %attend_back.3 = (bf16[2,577,1024]{2,1,0:T(8,128)(2,1)}, bf16[2,577,1024]{2,1,0:T(8,128)(2,1)}, bf16[2,577,1024]{2,1,0:T(8,128)(2,1)}) custom-call(bf16[2,577,1024]{2,1,0:T(8,128)(2,1)} %get-tuple-element.100.q_ref.refs_0_, bf16[2,577,1024]{2,1,0:T(8,128)(2,1)} %get-tuple-element.101.k_ref.refs_1_, ...), custom_call_target="tpu_custom_call", output_to_operand_aliasing={{0}: (5, {}), {1}: (6, {}), {2}: (7, {})} | custom-call | flops 10909417472 | bytes 25165824 | tf_op jit(solution)/shard_map/attend_back/pallas_call | solution.py:257
  361.4 13.4 %qkv_grads.1 = (bf16[2,577,128]{2,1,0:T(8,128)(2,1)}, bf16[3072,128]{1,0:T(8,128)(2,1)}, bf16[1024,128]{1,0:T(8,128)(2,1)}) custom-call(s32[2]{0:T(128)} %dynamic_slice.6.refs_1_.index_ref, bf16[2,577,1024]{2,1,0:T(8,128)(2,1)} %copy.69.refs_2_.refs_3_.tokens_ref.refs_1_, bf16[2,577,1024]{2,1,0:T(8,128)(2,1)} %get-tuple-element.141.dq_ref.refs_3_, ...), custom_call_target="tpu_custom_call" | custom-call | flops 2420113408 | bytes 12582912 | tf_op jit(solution)/shard_map/qkv_grads/pallas_call | solution.py:595
  378.1 11.4 %qkv_back.2.refs_11_ = f32[2,577,1024]{2,1,0:T(8,128)} custom-call(s32[4]{0:T(128)} %pad_add_fusion.refs_0_, bf16[2,577,1024]{2,1,0:T(8,128)(2,1)} %copy.69.refs_2_.refs_3_.tokens_ref.refs_1_, f32[2,577,1024]{2,1,0:T(8,128)} %get-tuple-element.116.refs_3_.refs_2_, bf16[2,577,1024]{2,1,0:T(8,128)(2,1)} %get-tuple-element.141.dq_ref.refs_3_, ...), custom_call_target="tpu_custom_call" | custom-call | flops 3630170112 | bytes 18874368 | tf_op jit(solution)/shard_map/qkv_back/pallas_call | solution.py:649
  395.6 2.4 collective-permute-start.28
  398.0 5.5 %copy.76 = bf16[2,577,1024]{2,0,1:T(2,128)(2,1)} copy(bf16[2,577,1024]{2,1,0:T(8,128)(2,1)} %get-tuple-element.182) | data formatting | bytes 4726784
  405.8 2.4 collective-permute-start.24
  408.2 2.0 collective-permute-start.25
  410.2 11.5 %qkv_back.3 = f32[2,577,1024]{2,1,0:T(8,128)} custom-call(s32[4]{0:T(128)} %pad_add_fusion.refs_0_, bf16[2,577,1024]{2,1,0:T(8,128)(2,1)} %copy.69.refs_2_.refs_3_.tokens_ref.refs_1_, f32[2,577,1024]{2,1,0:T(8,128)} %get-tuple-element.116.refs_3_.refs_2_, bf16[2,577,1024]{2,1,0:T(8,128)(2,1)} %get-tuple-element.141.dq_ref.refs_3_, ...), custom_call_target="tpu_custom_call", output_to_operand_aliasing={{}: (11, {})} | custom-call | flops 3630170112 | bytes 18874368 | tf_op jit(solution)/shard_map/qkv_back/pallas_call | solution.py:649
  421.7 8.2 %copy.77 = f32[2,577,1024]{2,0,1:T(2,128)} copy(f32[2,577,1024]{2,1,0:T(8,128)} %qkv_back.3) | data formatting | bytes 9453568
  (177 shorter events, 50.8 us)
Async XLA Ops:
  7.2 180.3 %all-gather.3.cloned.1.call-start = ((), (), s32[]{:S(2)}) async-start(), calls=%async_computation | async-start | bytes 19464192 | tf_op jit(solution)/shard_map/all_gather | solution.py:867
  9.9 11.7 %collective-permute-start = (bf16[64,1792]{1,0:T(8,128)(2,1)S(1)}, bf16[64,1792]{1,0:T(8,128)(2,1)S(1)}, u32[]{:S(2)}, u32[]{:S(2)}) collective-permute-start(bf16[64,1792]{1,0:T(8,128)(2,1)S(1)} %fusion.2.refs_0_), channel_id=1, source_target_pairs={{0,8},{2,10},{4,12},{6,14},{8,16},{10,18},{12,20},{14,22},{16,24},... | collective-permute-start | bytes 688136 | tf_op jit(solution)/shard_map/ppermute | solution.py:684
  13.0 17.6 %collective-permute-start.1 = (bf16[64,1792]{1,0:T(8,128)(2,1)S(1)}, bf16[64,1792]{1,0:T(8,128)(2,1)S(1)}, u32[]{:S(2)}, u32[]{:S(2)}) collective-permute-start(bf16[64,1792]{1,0:T(8,128)(2,1)S(1)} %fusion.2.refs_0_), channel_id=1, source_target_pairs={{0,16},{2,18},{4,20},{6,22},{8,24},{10,26},{12,28},{14,30},{16,0},... | collective-permute-start | bytes 688136 | tf_op jit(solution)/shard_map/ppermute | solution.py:684
  15.6 15.0 %collective-permute-start.2 = (bf16[64,1792]{1,0:T(8,128)(2,1)S(1)}, bf16[64,1792]{1,0:T(8,128)(2,1)S(1)}, u32[]{:S(2)}, u32[]{:S(2)}) collective-permute-start(bf16[64,1792]{1,0:T(8,128)(2,1)S(1)} %fusion.2.refs_0_), channel_id=1, source_target_pairs={{0,24},{2,26},{4,28},{6,30},{8,0},{10,2},{12,4},{14,6},{16,8},{18,... | collective-permute-start | bytes 688136 | tf_op jit(solution)/shard_map/ppermute | solution.py:684
  17.5 144.6 %copy-start.14 = (s32[10]{0:T(128)}, s32[10]{0:T(128)S(1)}, u32[]{:S(2)}) copy-start(s32[10]{0:T(128)S(1)} %stack.85.places_ref.p) | copy-start | bytes 124
  31.4 12.4 %collective-permute-start.3 = (bf16[4,64,896]{2,1,0:T(8,128)(2,1)S(1)}, bf16[4,64,896]{2,1,0:T(8,128)(2,1)S(1)}, u32[]{:S(2)}, u32[]{:S(2)}) collective-permute-start(bf16[4,64,896]{2,1,0:T(8,128)(2,1)S(1)} %get-tuple-element.91.refs_0_), channel_id=1, source_target_pairs={{0,4},{2,6},{4,0},{6,2},{8,12},{10,14},{12,8},{14,10},{16,20},{18,... | collective-permute-start | bytes 1376264 | tf_op jit(solution)/shard_map/ppermute | solution.py:679
  33.0 12.1 %collective-permute-start.4 = (bf16[4,64,896]{2,1,0:T(8,128)(2,1)S(1)}, bf16[4,64,896]{2,1,0:T(8,128)(2,1)S(1)}, u32[]{:S(2)}, u32[]{:S(2)}) collective-permute-start(bf16[4,64,896]{2,1,0:T(8,128)(2,1)S(1)} %get-tuple-element.92.refs_2_), channel_id=1, source_target_pairs={{0,2},{2,0},{4,6},{6,4},{8,10},{10,8},{12,14},{14,12},{16,18},{18,... | collective-permute-start | bytes 1376264 | tf_op jit(solution)/shard_map/ppermute | solution.py:675
  46.0 26.5 %collective-permute-start.5 = (bf16[4,2,64,896]{3,2,1,0:T(8,128)(2,1)S(1)}, bf16[4,2,64,896]{3,2,1,0:T(8,128)(2,1)S(1)}, u32[]{:S(2)}, u32[]{:S(2)}) collective-permute-start(bf16[4,2,64,896]{3,2,1,0:T(8,128)(2,1)S(1)} %get-tuple-element.93.refs_0_), channel_id=1, source_target_pairs={{0,2},{2,0},{4,6},{6,4},{8,10},{10,8},{12,14},{14,12},{16,18},{18,... | collective-permute-start | bytes 2752520 | tf_op jit(solution)/shard_map/ppermute | solution.py:675
  47.6 28.4 %copy-start.18 = (bf16[2,577,1024]{2,0,1:T(2,128)(2,1)S(1)}, bf16[2,577,1024]{2,0,1:T(2,128)(2,1)}, u32[]{:S(2)}) copy-start(bf16[2,577,1024]{2,0,1:T(2,128)(2,1)} %param.24) | copy-start | bytes 7090180
  47.6 25.5 %collective-permute-start.6 = (bf16[4,2,64,896]{3,2,1,0:T(8,128)(2,1)S(1)}, bf16[4,2,64,896]{3,2,1,0:T(8,128)(2,1)S(1)}, u32[]{:S(2)}, u32[]{:S(2)}) collective-permute-start(bf16[4,2,64,896]{3,2,1,0:T(8,128)(2,1)S(1)} %get-tuple-element.94.refs_2_), channel_id=1, source_target_pairs={{0,4},{2,6},{4,0},{6,2},{8,12},{10,14},{12,8},{14,10},{16,20},{18,... | collective-permute-start | bytes 2752520 | tf_op jit(solution)/shard_map/ppermute | solution.py:679
  75.9 18.1 %collective-permute-start.7 = (bf16[2,16,64,896]{3,2,1,0:T(8,128)(2,1)}, bf16[2,16,64,896]{3,2,1,0:T(8,128)(2,1)}, u32[]{:S(2)}, u32[]{:S(2)}) collective-permute-start(bf16[2,16,64,896]{3,2,1,0:T(8,128)(2,1)} %bitcast.18.refs_0_.refs_3_.refs_7_), channel_id=1, source_target_pairs={{0,1},{1,0},{2,3},{3,2},{4,5},{5,4},{6,7},{7,6},{8,9},{9,8},{10,11... | collective-permute-start | bytes 11010056 | tf_op jit(solution)/shard_map/ppermute | solution.py:688
  81.1 34.6 %collective-permute-start.10 = (bf16[64,768]{1,0:T(8,128)(2,1)S(1)}, bf16[64,768]{1,0:T(8,128)(2,1)S(1)}, u32[]{:S(2)}, u32[]{:S(2)}) collective-permute-start(bf16[64,768]{1,0:T(8,128)(2,1)S(1)} %maximum_maximum_fusion.refs_0_), channel_id=1, source_target_pairs={{0,24},{2,26},{4,28},{6,30},{8,0},{10,2},{12,4},{14,6},{16,8},{18,... | collective-permute-start | bytes 294920 | tf_op jit(solution)/shard_map/ppermute | solution.py:684
  85.8 29.9 %collective-permute-start.8 = (bf16[64,768]{1,0:T(8,128)(2,1)S(1)}, bf16[64,768]{1,0:T(8,128)(2,1)S(1)}, u32[]{:S(2)}, u32[]{:S(2)}) collective-permute-start(bf16[64,768]{1,0:T(8,128)(2,1)S(1)} %maximum_maximum_fusion.refs_0_), channel_id=1, source_target_pairs={{0,8},{2,10},{4,12},{6,14},{8,16},{10,18},{12,20},{14,22},{16,24},... | collective-permute-start | bytes 294920 | tf_op jit(solution)/shard_map/ppermute | solution.py:684
  92.5 23.2 %collective-permute-start.9 = (bf16[64,768]{1,0:T(8,128)(2,1)S(1)}, bf16[64,768]{1,0:T(8,128)(2,1)S(1)}, u32[]{:S(2)}, u32[]{:S(2)}) collective-permute-start(bf16[64,768]{1,0:T(8,128)(2,1)S(1)} %maximum_maximum_fusion.refs_0_), channel_id=1, source_target_pairs={{0,16},{2,18},{4,20},{6,22},{8,24},{10,26},{12,28},{14,30},{16,0},... | collective-permute-start | bytes 294920 | tf_op jit(solution)/shard_map/ppermute | solution.py:684
  116.8 38.3 %collective-permute-start.11 = (bf16[4,64,768]{2,1,0:T(8,128)(2,1)S(1)}, bf16[4,64,768]{2,1,0:T(8,128)(2,1)S(1)}, u32[]{:S(2)}, u32[]{:S(2)}) collective-permute-start(bf16[4,64,768]{2,1,0:T(8,128)(2,1)S(1)} %gather_z2.1.refs_0_), channel_id=1, source_target_pairs={{0,2},{2,0},{4,6},{6,4},{8,10},{10,8},{12,14},{14,12},{16,18},{18,... | collective-permute-start | bytes 1179656 | tf_op jit(solution)/shard_map/ppermute | solution.py:675
  116.9 38.2 %collective-permute-start.12 = (bf16[4,64,768]{2,1,0:T(8,128)(2,1)S(1)}, bf16[4,64,768]{2,1,0:T(8,128)(2,1)S(1)}, u32[]{:S(2)}, u32[]{:S(2)}) collective-permute-start(bf16[4,64,768]{2,1,0:T(8,128)(2,1)S(1)} %gather_z2.1.refs_0_), channel_id=1, source_target_pairs={{0,4},{2,6},{4,0},{6,2},{8,12},{10,14},{12,8},{14,10},{16,20},{18,... | collective-permute-start | bytes 1179656 | tf_op jit(solution)/shard_map/ppermute | solution.py:679
  117.0 38.2 %collective-permute-start.13 = (bf16[4,64,768]{2,1,0:T(8,128)(2,1)S(1)}, bf16[4,64,768]{2,1,0:T(8,128)(2,1)S(1)}, u32[]{:S(2)}, u32[]{:S(2)}) collective-permute-start(bf16[4,64,768]{2,1,0:T(8,128)(2,1)S(1)} %gather_z2.1.refs_0_), channel_id=1, source_target_pairs={{0,6},{2,4},{4,2},{6,0},{8,14},{10,12},{12,10},{14,8},{16,22},{18,... | collective-permute-start | bytes 1179656 | tf_op jit(solution)/shard_map/ppermute | solution.py:805
  156.1 6.0 %collective-permute-start.14 = (bf16[2,16,64,384]{3,2,1,0:T(8,128)(2,1)S(1)}, bf16[2,16,64,384]{3,2,1,0:T(8,128)(2,1)S(1)}, u32[]{:S(2)}, u32[]{:S(2)}) collective-permute-start(bf16[2,16,64,384]{3,2,1,0:T(8,128)(2,1)S(1)} %bitcast.81), channel_id=1, source_target_pairs={{0,1},{1,0},{2,3},{3,2},{4,5},{5,4},{6,7},{7,6},{8,9},{9,8},{10,11... | collective-permute-start | bytes 4718600 | tf_op jit(solution)/shard_map/ppermute | solution.py:688
  303.5 26.2 %collective-permute-start.15 = (bf16[4,2,2,384,128]{4,3,2,1,0:T(8,128)(2,1)}, bf16[4,2,2,384,128]{4,3,2,1,0:T(8,128)(2,1)S(1)}, u32[]{:S(2)}, u32[]{:S(2)}) collective-permute-start(bf16[4,2,2,384,128]{4,3,2,1,0:T(8,128)(2,1)} %get-tuple-element.130), channel_id=1, source_target_pairs={{0,1},{1,0},{2,3},{3,2},{4,5},{5,4},{6,7},{7,6},{8,9},{9,8},{10,11... | collective-permute-start | bytes 4718600 | tf_op jit(solution)/shard_map/ppermute | solution.py:688
  331.4 29.2 %collective-permute-start.16 = (bf16[4,384,128]{2,1,0:T(8,128)(2,1)}, bf16[4,384,128]{2,1,0:T(8,128)(2,1)S(1)}, u32[]{:S(2)}, u32[]{:S(2)}) collective-permute-start(bf16[4,384,128]{2,1,0:T(8,128)(2,1)} %get-tuple-element.137), channel_id=1, source_target_pairs={{0,2},{2,0},{4,6},{6,4},{8,10},{10,8},{12,14},{14,12},{16,18},{18,... | collective-permute-start | bytes 1179656 | tf_op jit(solution)/shard_map/ppermute | solution.py:675
  332.8 27.8 %collective-permute-start.17 = (bf16[4,384,128]{2,1,0:T(8,128)(2,1)}, bf16[4,384,128]{2,1,0:T(8,128)(2,1)S(1)}, u32[]{:S(2)}, u32[]{:S(2)}) collective-permute-start(bf16[4,384,128]{2,1,0:T(8,128)(2,1)} %get-tuple-element.138), channel_id=1, source_target_pairs={{0,4},{2,6},{4,0},{6,2},{8,12},{10,14},{12,8},{14,10},{16,20},{18,... | collective-permute-start | bytes 1179656 | tf_op jit(solution)/shard_map/ppermute | solution.py:679
  333.4 27.2 %collective-permute-start.18 = (bf16[4,384,128]{2,1,0:T(8,128)(2,1)S(1)}, bf16[4,384,128]{2,1,0:T(8,128)(2,1)S(1)}, u32[]{:S(2)}, u32[]{:S(2)}) collective-permute-start(bf16[4,384,128]{2,1,0:T(8,128)(2,1)S(1)} %get-tuple-element.139), channel_id=1, source_target_pairs={{0,6},{2,4},{4,2},{6,0},{8,14},{10,12},{12,10},{14,8},{16,22},{18,... | collective-permute-start | bytes 1179656 | tf_op jit(solution)/shard_map/ppermute | solution.py:1025
  377.6 11.9 %collective-permute-start.19 = (bf16[4,2,2,128,128]{4,3,2,1,0:T(8,128)(2,1)S(1)}, bf16[4,2,2,128,128]{4,3,2,1,0:T(8,128)(2,1)S(1)}, u32[]{:S(2)}, u32[]{:S(2)}) collective-permute-start(bf16[4,2,2,128,128]{4,3,2,1,0:T(8,128)(2,1)S(1)} %get-tuple-element.151), channel_id=1, source_target_pairs={{0,1},{1,0},{2,3},{3,2},{4,5},{5,4},{6,7},{7,6},{8,9},{9,8},{10,11... | collective-permute-start | bytes 1572872 | tf_op jit(solution)/shard_map/ppermute | solution.py:688
  377.6 17.9 %collective-permute-start.26 = (bf16[384,128]{1,0:T(8,128)(2,1)S(1)}, bf16[384,128]{1,0:T(8,128)(2,1)S(1)}, u32[]{:S(2)}, u32[]{:S(2)}) collective-permute-start(bf16[384,128]{1,0:T(8,128)(2,1)S(1)} %get-tuple-element.163), channel_id=1, source_target_pairs={{0,8},{2,10},{4,12},{6,14},{8,16},{10,18},{12,20},{14,22},{16,24},... | collective-permute-start | bytes 294920 | tf_op jit(solution)/shard_map/ppermute | solution.py:684
  390.2 14.7 %collective-permute-start.20 = (bf16[4,128,128]{2,1,0:T(8,128)(2,1)S(1)}, bf16[4,128,128]{2,1,0:T(8,128)(2,1)S(1)}, u32[]{:S(2)}, u32[]{:S(2)}) collective-permute-start(bf16[4,128,128]{2,1,0:T(8,128)(2,1)S(1)} %get-tuple-element.154), channel_id=1, source_target_pairs={{0,2},{2,0},{4,6},{6,4},{8,10},{10,8},{12,14},{14,12},{16,18},{18,... | collective-permute-start | bytes 393224 | tf_op jit(solution)/shard_map/ppermute | solution.py:675
  391.7 13.3 %collective-permute-start.21 = (bf16[4,128,128]{2,1,0:T(8,128)(2,1)S(1)}, bf16[4,128,128]{2,1,0:T(8,128)(2,1)S(1)}, u32[]{:S(2)}, u32[]{:S(2)}) collective-permute-start(bf16[4,128,128]{2,1,0:T(8,128)(2,1)S(1)} %get-tuple-element.155), channel_id=1, source_target_pairs={{0,4},{2,6},{4,0},{6,2},{8,12},{10,14},{12,8},{14,10},{16,20},{18,... | collective-permute-start | bytes 393224 | tf_op jit(solution)/shard_map/ppermute | solution.py:679
  392.3 12.6 %collective-permute-start.22 = (bf16[4,128,128]{2,1,0:T(8,128)(2,1)S(1)}, bf16[4,128,128]{2,1,0:T(8,128)(2,1)S(1)}, u32[]{:S(2)}, u32[]{:S(2)}) collective-permute-start(bf16[4,128,128]{2,1,0:T(8,128)(2,1)S(1)} %get-tuple-element.156), channel_id=1, source_target_pairs={{0,6},{2,4},{4,2},{6,0},{8,14},{10,12},{12,10},{14,8},{16,22},{18,... | collective-permute-start | bytes 393224 | tf_op jit(solution)/shard_map/ppermute | solution.py:1025
  393.7 9.8 %collective-permute-start.27 = (bf16[384,128]{1,0:T(8,128)(2,1)S(1)}, bf16[384,128]{1,0:T(8,128)(2,1)S(1)}, u32[]{:S(2)}, u32[]{:S(2)}) collective-permute-start(bf16[384,128]{1,0:T(8,128)(2,1)S(1)} %get-tuple-element.164), channel_id=1, source_target_pairs={{0,16},{2,18},{4,20},{6,22},{8,24},{10,26},{12,28},{14,30},{16,0},... | collective-permute-start | bytes 294920 | tf_op jit(solution)/shard_map/ppermute | solution.py:684
  395.6 8.0 %collective-permute-start.28 = (bf16[384,128]{1,0:T(8,128)(2,1)S(1)}, bf16[384,128]{1,0:T(8,128)(2,1)S(1)}, u32[]{:S(2)}, u32[]{:S(2)}) collective-permute-start(bf16[384,128]{1,0:T(8,128)(2,1)S(1)} %get-tuple-element.165), channel_id=1, source_target_pairs={{0,24},{2,26},{4,28},{6,30},{8,0},{10,2},{12,4},{14,6},{16,8},{18,... | collective-permute-start | bytes 294920 | tf_op jit(solution)/shard_map/ppermute | solution.py:684
  405.6 24.3 %collective-permute-start.23 = (bf16[128,128]{1,0:T(8,128)(2,1)S(1)}, bf16[128,128]{1,0:T(8,128)(2,1)S(1)}, u32[]{:S(2)}, u32[]{:S(2)}) collective-permute-start(bf16[128,128]{1,0:T(8,128)(2,1)S(1)} %get-tuple-element.158), channel_id=1, source_target_pairs={{0,8},{2,10},{4,12},{6,14},{8,16},{10,18},{12,20},{14,22},{16,24},... | collective-permute-start | bytes 98312 | tf_op jit(solution)/shard_map/ppermute | solution.py:684
  405.8 24.1 %collective-permute-start.24 = (bf16[128,128]{1,0:T(8,128)(2,1)S(1)}, bf16[128,128]{1,0:T(8,128)(2,1)S(1)}, u32[]{:S(2)}, u32[]{:S(2)}) collective-permute-start(bf16[128,128]{1,0:T(8,128)(2,1)S(1)} %get-tuple-element.159), channel_id=1, source_target_pairs={{0,16},{2,18},{4,20},{6,22},{8,24},{10,26},{12,28},{14,30},{16,0},... | collective-permute-start | bytes 98312 | tf_op jit(solution)/shard_map/ppermute | solution.py:684
  408.2 21.6 %collective-permute-start.25 = (bf16[128,128]{1,0:T(8,128)(2,1)S(1)}, bf16[128,128]{1,0:T(8,128)(2,1)S(1)}, u32[]{:S(2)}, u32[]{:S(2)}) collective-permute-start(bf16[128,128]{1,0:T(8,128)(2,1)S(1)} %get-tuple-element.160), channel_id=1, source_target_pairs={{0,24},{2,26},{4,28},{6,30},{8,0},{10,2},{12,4},{14,6},{16,8},{18,... | collective-permute-start | bytes 98312 | tf_op jit(solution)/shard_map/ppermute | solution.py:684
  (38 other events, 179.9 us)
Sparse Core Ops, SparseCore 0:
  31.6 155.8 all-gather.2
